TPU v7x, 128 devices: a whole 4x4x4 slice. The times are simulated.
128 devices in a mesh: lat: 8 (over x, y_lo), lon: 16 (over z, y_hi, core).
Axes of the slice: x: 4, y: 4 (y_hi: 2, y_lo: 2; y = y_hi * 2 + y_lo), z: 4, core: 2. Of those that a mesh axis runs over, the one named last changes fastest.
Arguments:
- fine_tokens: bfloat16 [128, 2048, 512], P('lat', 'lon'), may hold values from -6 to 6
- latents: bfloat16 [64, 1024, 512], P('lat', 'lon'), may hold values from -6 to 6
- upsample_weight: bfloat16 [8192, 512], replicated, may hold values from -0.125 to 0.125
- uniting_in: bfloat16 [1024, 1024], replicated, may hold values from -0.1875 to 0.1875
- uniting_out: bfloat16 [1024, 512], replicated, may hold values from -0.1875 to 0.1875
- cotangent: bfloat16 [128, 2048, 512], P('lat', 'lon'), may hold values from -6 to 6
Outputs:
- united: bfloat16 [128, 2048, 512], P('lat', 'lon')
- latent_grad: float32 [64, 1024, 512], P('lat', 'lon')
- uniting_in_grad: float32 [1024, 1024], P('lon', 'lat')
- uniting_out_grad: float32 [1024, 512], P('lon', 'lat')
All inputs are finite; a program needn't handle non-finite values.
Results may differ from a plain program's by a relative error of at most 0.014.
Values may be sent and summed in bfloat16 or wider, within the bound.
No kernel may reach another device: no remote copies, remote signals or barrier semaphores. Data moves between devices by JAX's collectives and lax.ppermute only.
A program may use at most 128 MiB of HBM per device.

v0:
```python
import jax
import jax.numpy as jnp
from jax import lax
from jax.sharding import PartitionSpec as P

ROW_STEP = (1, 0, 0, -1)
ROW_PARITY = (1, 0, 1, 0)


def with_halo(array, sides, width, wrap):
    for axis, dim in sides:
        devices, length = (lax.axis_size(axis), array.shape[dim])
        up = [(i, (i + 1) % devices) for i in range(devices if wrap else devices - 1)]
        down = [(j, i) for i, j in up]
        last = lax.slice_in_dim(array, length - width, length, axis=dim)
        first = lax.slice_in_dim(array, 0, width, axis=dim)
        before = lax.ppermute(last, axis, up)
        after = lax.ppermute(first, axis, down)
        array = jnp.concatenate([before, array, after], axis=dim)
    return array


def extend_latents(latents):
    row_extended = with_halo(latents, (("lat", 0),), 1, False)
    extended = with_halo(row_extended, (("lon", 1),), 1, True)
    return extended


def extend_cotangent(up_cot):
    row_extended = with_halo(up_cot, (("lat", 0),), 1, False)
    extended = with_halo(row_extended, (("lon", 1),), 1, True)
    return extended


def assemble_grid(parity_blocks):
    upper = jnp.stack([parity_blocks[0][0], parity_blocks[0][1]], axis=2)
    lower = jnp.stack([parity_blocks[1][0], parity_blocks[1][1]], axis=2)
    stacked = jnp.stack([upper, lower], axis=1)
    dims = stacked.shape
    return stacked.reshape(dims[0] * 2, dims[2] * 2, dims[4])


def shards(fine_tokens, latents, upsample_weight, uniting_in, uniting_out, cotangent):
    lat_rows, lat_cols, latent_width = latents.shape
    model_width = fine_tokens.shape[2]
    latent_ext = extend_latents(latents)
    kernels = upsample_weight.reshape(16, model_width, latent_width)
    parity_blocks = []
    for parity_row in range(2):
        block_row = []
        for parity_col in range(2):
            summed = jnp.zeros((lat_rows, lat_cols, model_width), jnp.float32)
            for kernel_row in range(4):
                for kernel_col in range(4):
                    if (
                        ROW_PARITY[kernel_row] == parity_row
                        and ROW_PARITY[kernel_col] == parity_col
                    ):
                        row_start = 1 + ROW_STEP[kernel_row]
                        col_start = 1 + ROW_STEP[kernel_col]
                        source = latent_ext[
                            row_start : row_start + lat_rows, col_start : col_start + lat_cols
                        ]
                        summed = summed + lax.dot_general(
                            source,
                            kernels[kernel_row * 4 + kernel_col],
                            (((2,), (1,)), ((), ())),
                            preferred_element_type=jnp.float32,
                        )
            block_row.append(summed.astype(jnp.bfloat16))
        parity_blocks.append(block_row)
    upsampled = assemble_grid(parity_blocks)
    token_count = fine_tokens.shape[0] * fine_tokens.shape[1]
    tokens = fine_tokens.reshape(token_count, model_width)
    joined = jnp.concatenate([tokens, upsampled.reshape(token_count, model_width)], axis=1)
    hidden_pre = jnp.dot(joined, uniting_in, preferred_element_type=jnp.float32)
    activation = jax.nn.silu(hidden_pre).astype(jnp.bfloat16)
    united = (
        tokens.astype(jnp.float32)
        + jnp.dot(activation, uniting_out, preferred_element_type=jnp.float32)
    ).astype(jnp.bfloat16)
    upstream = cotangent.reshape(token_count, model_width)
    act_grad = lax.dot_general(
        upstream, uniting_out, (((1,), (1,)), ((), ())), preferred_element_type=jnp.float32
    )
    sigmoid_gate = jax.nn.sigmoid(hidden_pre)
    pre_grad = (act_grad * sigmoid_gate * (1.0 + hidden_pre * (1.0 - sigmoid_gate))).astype(
        jnp.bfloat16
    )
    out_local = lax.dot_general(
        activation, upstream, (((0,), (0,)), ((), ())), preferred_element_type=jnp.float32
    )
    in_local = lax.dot_general(
        joined, pre_grad, (((0,), (0,)), ((), ())), preferred_element_type=jnp.float32
    )
    in_part, out_part = (
        lax.psum_scatter(
            in_local.astype(jnp.bfloat16), "lon", scatter_dimension=0, tiled=True
        ).astype(jnp.float32),
        lax.psum_scatter(
            out_local.astype(jnp.bfloat16), "lon", scatter_dimension=0, tiled=True
        ).astype(jnp.float32),
    )
    uniting_in_grad, uniting_out_grad = (
        lax.psum_scatter(in_part, "lat", scatter_dimension=1, tiled=True),
        lax.psum_scatter(out_part, "lat", scatter_dimension=1, tiled=True),
    )
    up_cot = lax.dot_general(
        pre_grad,
        uniting_in[model_width:],
        (((1,), (1,)), ((), ())),
        preferred_element_type=jnp.float32,
    )
    up_cot = up_cot.astype(jnp.bfloat16).reshape(fine_tokens.shape)
    cot_ext = extend_cotangent(up_cot)
    split_grid = cot_ext.reshape(lat_rows + 1, 2, lat_cols + 1, 2, model_width).transpose(
        1, 3, 0, 2, 4
    )
    latent_grad = jnp.zeros((lat_rows, lat_cols, latent_width), jnp.float32)
    for kernel_row in range(4):
        for kernel_col in range(4):
            row_start = 1 + ROW_PARITY[kernel_row] - 2 * ROW_STEP[kernel_row]
            col_start = 1 + ROW_PARITY[kernel_col] - 2 * ROW_STEP[kernel_col]
            window = split_grid[
                row_start % 2,
                col_start % 2,
                row_start // 2 : row_start // 2 + lat_rows,
                col_start // 2 : col_start // 2 + lat_cols,
            ]
            latent_grad = latent_grad + lax.dot_general(
                window,
                kernels[kernel_row * 4 + kernel_col],
                (((2,), (0,)), ((), ())),
                preferred_element_type=jnp.float32,
            )
    return (united.reshape(fine_tokens.shape), latent_grad, uniting_in_grad, uniting_out_grad)


def solution(mesh):
    return jax.shard_map(
        shards,
        mesh=mesh,
        in_specs=(
            P("lat", "lon", None),
            P("lat", "lon", None),
            P(),
            P(),
            P(),
            P("lat", "lon", None),
        ),
        out_specs=(P("lat", "lon", None), P("lat", "lon", None), P("lon", "lat"), P("lon", "lat")),
        check_vma=False,
    )
```

profile of v0, /device:TPU:1, one launch (start us, length us, event | category | flops | bytes accessed | tf_op | source)
XLA Modules:
  0.0 289.7 jit_solution(16119393409054338638)
XLA Ops:
  9.6 4.7 %collective-permute-start = (bf16[1,64,512]{2,1,0:T(8,128)(2,1)S(1)}, bf16[1,64,512]{2,1,0:T(8,128)(2,1)S(1)}, u32[]{:S(2)}, u32[]{:S(2)}) collective-permute-start(bf16[1,64,512]{2,1,0:T(8,128)(2,1)S(1)} %get-tuple-element.14), channel_id=1, source_target_pairs={{0,16},{16,32},{32,48},{48,64},{64,80},{80,96},{96,112},{1,17},{17... | collective-permute-start | bytes 196616 | tf_op jit(solution)/shard_map/ppermute | solution.py:17
  17.8 1.9 fusion.32
  21.5 4.3 %collective-permute-start.2 = (bf16[10,1,512]{2,1,0:T(2,128)(2,1)S(1)}, bf16[10,1,512]{2,1,0:T(2,128)(2,1)S(1)}, u32[]{:S(2)}, u32[]{:S(2)}) collective-permute-start(bf16[10,1,512]{2,1,0:T(2,128)(2,1)S(1)} %get-tuple-element.8), channel_id=1, source_target_pairs={{0,1},{1,2},{2,3},{3,4},{4,5},{5,6},{6,7},{7,8},{8,9},{9,10},{10,1... | collective-permute-start | bytes 30728 | tf_op jit(solution)/shard_map/ppermute | solution.py:17
  32.8 3.5 %copy.12 = bf16[8,2,64,2,512]{4,3,2,1,0:T(2,128)(2,1)} copy(bf16[8,2,64,2,512]{4,2,0,3,1:T(8,128)(2,1)S(1)} %pad_maximum_fusion.4) | data formatting | bytes 4194304 | tf_op jit(solution)/shard_map/stack | solution.py:38
  36.3 4.2 %reshape_reshape.3 = bf16[2048,512]{1,0:T(8,128)(2,1)} reshape(bf16[8,2,64,2,512]{4,3,2,1,0:T(2,128)(2,1)} %copy.12) | data formatting | bytes 4194304 | tf_op jit(solution)/shard_map/reshape;reshape | solution.py:75
  40.5 7.8 %multiply_convert_fusion.1 = (bf16[2048,1024]{1,0:T(8,128)(2,1)S(1)}, f32[2048,1024]{1,0:T(8,128)S(1)}) fusion(bf16[1024,1024]{1,0:T(8,128)(2,1)} %param.9, bf16[2048,512]{1,0:T(8,128)(2,1)} %reshape_reshape.3, bf16[2048,512]{1,0:T(8,128)(2,1)} %bitcast.194), kind=kOutput, calls=%fused_computation.1 | convolution fusion | flops 4313841664 | bytes 18874368 | tf_op jit(solution)/shard_map/dot_general | solution.py:76
  48.4 5.1 %multiply_convert_fusion = bf16[2048,1024]{1,0:T(8,128)(2,1)S(1)} fusion(f32[2048,1024]{1,0:T(8,128)S(1)} %get-tuple-element.20, bf16[2048,512]{1,0:T(8,128)(2,1)S(1)} %bitcast.170, bf16[1024,512]{1,0:T(8,128)(2,1)S(1)} %copy-done.6), kind=kOutput, calls=%fused_computation | convolution fusion | flops 2166358016 | bytes 15728640 | tf_op jit(solution)/shard_map/dot_general | solution.py:83
  53.4 2.4 convolution_convert_fusion
  57.3 3.2 %collective-permute-start.4 = (bf16[1,128,512]{2,1,0:T(8,128)(2,1)S(1)}, bf16[1,128,512]{2,1,0:T(8,128)(2,1)S(1)}, u32[]{:S(2)}, u32[]{:S(2)}) collective-permute-start(bf16[1,128,512]{2,1,0:T(8,128)(2,1)S(1)} %get-tuple-element.6), channel_id=1, source_target_pairs={{0,16},{16,32},{32,48},{48,64},{64,80},{80,96},{96,112},{1,17},{17... | collective-permute-start | bytes 393224 | tf_op jit(solution)/shard_map/ppermute | solution.py:17
  61.8 3.4 %convolution_convert_fusion.1 = bf16[1024,512]{1,0:T(8,128)(2,1)} fusion(bf16[2048,1024]{1,0:T(8,128)(2,1)S(1)} %get-tuple-element.19, bf16[2048,512]{1,0:T(8,128)(2,1)S(1)} %bitcast.171), kind=kOutput, calls=%fused_computation.12 | convolution fusion | flops 2148007936 | bytes 7340032 | tf_op jit(solution)/shard_map/dot_general | solution.py:90
  65.4 9.4 %fusion.2 = bf16[1024,1024]{1,0:T(8,128)(2,1)} fusion(bf16[2048,1024]{1,0:T(8,128)(2,1)} %copy-done.8, bf16[2048,512]{1,0:T(8,128)(2,1)} %reshape_reshape.3, bf16[2048,512]{1,0:T(8,128)(2,1)} %bitcast.195), kind=kOutput, calls=%fused_computation.11 | convolution fusion | flops 4304404480 | bytes 10485760 | tf_op jit(solution)/shard_map/dot_general | solution.py:93
  75.9 3.9 %collective-permute-start.6 = (bf16[18,1,512]{2,1,0:T(2,128)(2,1)S(1)}, bf16[18,1,512]{2,1,0:T(2,128)(2,1)S(1)}, u32[]{:S(2)}, u32[]{:S(2)}) collective-permute-start(bf16[18,1,512]{2,1,0:T(2,128)(2,1)S(1)} %get-tuple-element.4), channel_id=1, source_target_pairs={{0,1},{1,2},{2,3},{3,4},{4,5},{5,6},{6,7},{7,8},{8,9},{9,10},{10,1... | collective-permute-start | bytes 55304 | tf_op jit(solution)/shard_map/ppermute | solution.py:17
  79.8 7.0 %add_convert_fusion = bf16[2048,512]{1,0:T(8,128)(2,1)} fusion(bf16[2048,512]{1,0:T(8,128)(2,1)} %bitcast.196, bf16[2048,1024]{1,0:T(8,128)(2,1)} %copy-done.7, bf16[1024,512]{1,0:T(8,128)(2,1)} %param.10), kind=kOutput, calls=%fused_computation.4 | convolution fusion | flops 2150629376 | bytes 9437184 | tf_op jit(solution)/shard_map/dot_general | solution.py:80
  87.1 3.8 %pad_maximum_fusion.3 = bf16[18,130,512]{2,1,0:T(8,128)(2,1)} fusion(bf16[18,1,512]{2,1,0:T(2,128)(2,1)S(1)} %collective-permute-done.7, bf16[1,128,512]{2,1,0:T(8,128)(2,1)S(1)} %collective-permute-done.5, bf16[16,128,512]{2,1,0:T(8,128)(2,1)} %bitcast.191, bf16[1,128,512]{2,1,0:T(8,128)(2,1)S(1)} %collective-permute-done.4, ...), kind=kLoop, calls=%fused_computation.9 | loop fusion | flops 11980800 | bytes 4792320 | tf_op jit(solution)/shard_map/concatenate | solution.py:19
  90.9 6.0 %reshape.62 = bf16[9,2,65,2,512]{4,3,2,1,0:T(2,128)(2,1)} reshape(bf16[18,130,512]{2,1,0:T(8,128)(2,1)} %pad_maximum_fusion.3) | data formatting | bytes 4792320 | tf_op jit(solution)/shard_map/reshape | solution.py:116
  96.9 2.3 copy.17
  99.2 1.9 fusion.27
  109.8 24.9 %reduce-scatter.11.cloned.1.call-done = bf16[64,512]{1,0:T(8,128)(2,1)} async-done(((bf16[1024,512]{1,0:T(8,128)(2,1)}), bf16[64,512]{1,0:T(8,128)(2,1)}) %reduce-scatter.11.cloned.1.call-update) | async-done | bytes 65552 | tf_op jit(solution)/shard_map/reduce_scatter | solution.py:100
  136.4 2.6 convolution_add_fusion.4
  139.0 69.7 %reduce-scatter.7.cloned.1.call-done = bf16[64,1024]{1,0:T(8,128)(2,1)} async-done(((bf16[1024,1024]{1,0:T(8,128)(2,1)}), bf16[64,1024]{1,0:T(8,128)(2,1)}) %reduce-scatter.7.cloned.1.call-update) | async-done | bytes 131088 | tf_op jit(solution)/shard_map/reduce_scatter | solution.py:97
  210.4 2.0 convolution_add_fusion.3
  212.4 2.6 convolution_add_fusion.2
  215.0 29.1 %reduce-scatter.13.cloned.1.call-done = f32[64,64]{1,0:T(8,128)} async-done(((f32[512,64]{1,0:T(8,128)}), f32[64,64]{1,0:T(8,128)}) %reduce-scatter.13.cloned.1.call-update) | async-done | bytes 16400
  245.6 37.6 %reduce-scatter.9.cloned.1.call-done = f32[64,128]{1,0:T(8,128)} async-done(((f32[64,1024]{1,0:T(8,128)}), f32[64,128]{1,0:T(8,128)}) %reduce-scatter.9.cloned.1.call-update) | async-done | bytes 32784 | tf_op jit(solution)/shard_map/reduce_scatter | solution.py:105
  (82 shorter events, 32.2 us)
Async XLA Ops:
  7.2 41.1 %copy-start = (bf16[16,128,512]{2,1,0:T(8,128)(2,1)S(1)}, bf16[16,128,512]{2,1,0:T(8,128)(2,1)}, u32[]{:S(2)}) copy-start(bf16[16,128,512]{2,1,0:T(8,128)(2,1)} %param.11) | copy-start | bytes 6291460
  7.2 10.6 %copy-start.3 = (bf16[8,64,512]{2,1,0:T(8,128)(2,1)S(1)}, bf16[8,64,512]{2,1,0:T(8,128)(2,1)}, u32[]{:S(2)}) copy-start(bf16[8,64,512]{2,1,0:T(8,128)(2,1)} %param.7) | copy-start | bytes 1572868
  7.2 127.5 %reduce-scatter.11.cloned.1.call-start = ((), (), s32[]{:S(2)}) async-start(), calls=%async_computation.6 | async-start | bytes 1114112 | tf_op jit(solution)/shard_map/reduce_scatter | solution.py:100
  8.3 13.1 %collective-permute-start.1 = (bf16[1,64,512]{2,1,0:T(8,128)(2,1)S(1)}, bf16[1,64,512]{2,1,0:T(8,128)(2,1)S(1)}, u32[]{:S(2)}, u32[]{:S(2)}) collective-permute-start(bf16[1,64,512]{2,1,0:T(8,128)(2,1)S(1)} %get-tuple-element.13), channel_id=1, source_target_pairs={{16,0},{32,16},{48,32},{64,48},{80,64},{96,80},{112,96},{17,1},{33... | collective-permute-start | bytes 196616 | tf_op jit(solution)/shard_map/ppermute | solution.py:18
  9.6 11.6 %collective-permute-start = (bf16[1,64,512]{2,1,0:T(8,128)(2,1)S(1)}, bf16[1,64,512]{2,1,0:T(8,128)(2,1)S(1)}, u32[]{:S(2)}, u32[]{:S(2)}) collective-permute-start(bf16[1,64,512]{2,1,0:T(8,128)(2,1)S(1)} %get-tuple-element.14), channel_id=1, source_target_pairs={{0,16},{16,32},{32,48},{48,64},{64,80},{80,96},{96,112},{1,17},{17... | collective-permute-start | bytes 196616 | tf_op jit(solution)/shard_map/ppermute | solution.py:17
  15.9 9.8 %copy-start.2 = (bf16[8192,512]{1,0:T(8,128)(2,1)S(1)}, bf16[8192,512]{1,0:T(8,128)(2,1)}, u32[]{:S(2)}) copy-start(bf16[8192,512]{1,0:T(8,128)(2,1)} %param.8) | copy-start | bytes 25165828
  21.5 5.2 %collective-permute-start.2 = (bf16[10,1,512]{2,1,0:T(2,128)(2,1)S(1)}, bf16[10,1,512]{2,1,0:T(2,128)(2,1)S(1)}, u32[]{:S(2)}, u32[]{:S(2)}) collective-permute-start(bf16[10,1,512]{2,1,0:T(2,128)(2,1)S(1)} %get-tuple-element.8), channel_id=1, source_target_pairs={{0,1},{1,2},{2,3},{3,4},{4,5},{5,6},{6,7},{7,8},{8,9},{9,10},{10,1... | collective-permute-start | bytes 30728 | tf_op jit(solution)/shard_map/ppermute | solution.py:17
  25.8 4.7 %collective-permute-start.3 = (bf16[10,1,512]{2,1,0:T(2,128)(2,1)S(1)}, bf16[10,1,512]{2,1,0:T(2,128)(2,1)S(1)}, u32[]{:S(2)}, u32[]{:S(2)}) collective-permute-start(bf16[10,1,512]{2,1,0:T(2,128)(2,1)S(1)} %get-tuple-element.9), channel_id=1, source_target_pairs={{1,0},{2,1},{3,2},{4,3},{5,4},{6,5},{7,6},{8,7},{9,8},{10,9},{11,1... | collective-permute-start | bytes 30728 | tf_op jit(solution)/shard_map/ppermute | solution.py:18
  40.5 7.9 %copy-start.6 = (bf16[1024,512]{1,0:T(8,128)(2,1)S(1)}, bf16[1024,512]{1,0:T(8,128)(2,1)}, u32[]{:S(2)}) copy-start(bf16[1024,512]{1,0:T(8,128)(2,1)} %param.10) | copy-start | bytes 3145732
  48.3 13.5 %copy-start.7 = (bf16[2048,1024]{1,0:T(8,128)(2,1)}, bf16[2048,1024]{1,0:T(8,128)(2,1)S(1)}, u32[]{:S(2)}) copy-start(bf16[2048,1024]{1,0:T(8,128)(2,1)S(1)} %get-tuple-element.19) | copy-start | bytes 12582916
  48.3 5.1 %copy-start.5 = (bf16[1024,1024]{1,0:T(8,128)(2,1)S(1)}, bf16[1024,1024]{1,0:T(8,128)(2,1)}, u32[]{:S(2)}) copy-start(bf16[1024,1024]{1,0:T(8,128)(2,1)} %param.9) | copy-start | bytes 6291460
  53.4 2.5 copy-start.8
  55.9 1.4 copy-start.4
  57.3 17.6 %collective-permute-start.4 = (bf16[1,128,512]{2,1,0:T(8,128)(2,1)S(1)}, bf16[1,128,512]{2,1,0:T(8,128)(2,1)S(1)}, u32[]{:S(2)}, u32[]{:S(2)}) collective-permute-start(bf16[1,128,512]{2,1,0:T(8,128)(2,1)S(1)} %get-tuple-element.6), channel_id=1, source_target_pairs={{0,16},{16,32},{32,48},{48,64},{64,80},{80,96},{96,112},{1,17},{17... | collective-permute-start | bytes 393224 | tf_op jit(solution)/shard_map/ppermute | solution.py:17
  60.5 14.4 %collective-permute-start.5 = (bf16[1,128,512]{2,1,0:T(8,128)(2,1)S(1)}, bf16[1,128,512]{2,1,0:T(8,128)(2,1)S(1)}, u32[]{:S(2)}, u32[]{:S(2)}) collective-permute-start(bf16[1,128,512]{2,1,0:T(8,128)(2,1)S(1)} %get-tuple-element.7), channel_id=1, source_target_pairs={{16,0},{32,16},{48,32},{64,48},{80,64},{96,80},{112,96},{17,1},{33... | collective-permute-start | bytes 393224 | tf_op jit(solution)/shard_map/ppermute | solution.py:18
  65.2 143.6 %reduce-scatter.7.cloned.1.call-start = ((), (), s32[]{:S(2)}) async-start(), calls=%async_computation.4 | async-start | bytes 2228224 | tf_op jit(solution)/shard_map/reduce_scatter | solution.py:97
  75.9 11.2 %collective-permute-start.6 = (bf16[18,1,512]{2,1,0:T(2,128)(2,1)S(1)}, bf16[18,1,512]{2,1,0:T(2,128)(2,1)S(1)}, u32[]{:S(2)}, u32[]{:S(2)}) collective-permute-start(bf16[18,1,512]{2,1,0:T(2,128)(2,1)S(1)} %get-tuple-element.4), channel_id=1, source_target_pairs={{0,1},{1,2},{2,3},{3,4},{4,5},{5,6},{6,7},{7,8},{8,9},{9,10},{10,1... | collective-permute-start | bytes 55304 | tf_op jit(solution)/shard_map/ppermute | solution.py:17
  79.8 7.3 %collective-permute-start.7 = (bf16[18,1,512]{2,1,0:T(2,128)(2,1)S(1)}, bf16[18,1,512]{2,1,0:T(2,128)(2,1)S(1)}, u32[]{:S(2)}, u32[]{:S(2)}) collective-permute-start(bf16[18,1,512]{2,1,0:T(2,128)(2,1)S(1)} %get-tuple-element.5), channel_id=1, source_target_pairs={{1,0},{2,1},{3,2},{4,3},{5,4},{6,5},{7,6},{8,7},{9,8},{10,9},{11,1... | collective-permute-start | bytes 55304 | tf_op jit(solution)/shard_map/ppermute | solution.py:18
  86.7 157.4 %reduce-scatter.13.cloned.1.call-start = ((), (), s32[]{:S(2)}) async-start(), calls=%async_computation.7 | async-start | bytes 294912
  96.9 8.8 %slice-start = ((s8[8388608]{0:T(1024)(128)(4,1)}), s8[4194304]{0:T(1024)(128)(4,1)S(1)}, s32[]{:S(2)}) async-start(s8[8388608]{0:T(1024)(128)(4,1)} %bitcast.188), calls=%async_computation.8 | async-start | bytes 8388608
  99.2 10.1 %copy-start.1 = (bf16[9,2,65,2,512]{4,2,0,3,1:T(8,128)(2,1)}, bf16[9,2,65,2,512]{4,2,0,3,1:T(8,128)(2,1)S(1)}, u32[]{:S(2)}) copy-start(bf16[9,2,65,2,512]{4,2,0,3,1:T(8,128)(2,1)S(1)} %copy.17) | copy-start | bytes 7188484
  101.1 4.6 %slice-start.1 = ((s8[8388608]{0:T(1024)(128)(4,1)}), s8[4194304]{0:T(1024)(128)(4,1)S(1)}, s32[]{:S(2)}) async-start(s8[8388608]{0:T(1024)(128)(4,1)} %bitcast.188), calls=%async_computation.9 | async-start | bytes 8388608
  136.4 146.8 %reduce-scatter.9.cloned.1.call-start = ((), (), s32[]{:S(2)}) async-start(), calls=%async_computation.5 | async-start | bytes 294912 | tf_op jit(solution)/shard_map/reduce_scatter | solution.py:105
Sparse Core Ops, SparseCore 0:
  65.3 69.3 reduce-scatter.10
  138.6 70.1 reduce-scatter.6
  211.1 32.9 reduce-scatter.12
  246.9 36.1 reduce-scatter.8
where the time goes:
time: 295 us; the launch traced here: 290 us
  waiting for transfers between devices  162 us (55%)
  matrix products  65.3 us (22%)
  local copies, waits for them, and re-layouts  21.8 us (7%)
  starting transfers between devices  19.2 us (7%)
  between operations  14.3 us (5%)
  other arithmetic  6.88 us (2%)
    reduce_scatter x1, waiting for transfers between devices, shards(): lax.psum_scatter(in_local.astype(jnp.bfloat16), 'lon', scatter_dimension=...  69.7 us
    reduce_scatter x1, waiting for transfers between devices, shards(): lax.psum_scatter(in_part, 'lat', scatter_dimension=1, tiled=True)  37.6 us
    unnamed x5, waiting for transfers between devices  29.1 us
    reduce_scatter x1, waiting for transfers between devices, shards(): lax.psum_scatter(out_local.astype(jnp.bfloat16), 'lon', scatter_dimension...  24.9 us
    dot_general x16, matrix products, shards(): lax.dot_general(window, kernels[kernel_row * 4 + kernel_col], (((2,), (0,...  17.7 us
    ppermute x4, starting transfers between devices, with_halo(): before = lax.ppermute(last, axis, up)  16 us
    dot_general x16, matrix products, shards(): lax.dot_general(source, kernels[kernel_row * 4 + kernel_col], (((2,), (1,...  12.6 us
    dot_general x1, matrix products, shards(): lax.dot_general(joined, pre_grad, (((0,), (0,)), ((), ())), preferred_ele...  9.4 us
  transfers between devices with their start and end apart: 12, of which 5 were waited for; matrix products, arithmetic and copies ran while one was open for 23% of the time, Pallas kernels for 0%

commit v1 on v0

v1 whole, which is shorter than its diff:
```python
import jax
import jax.numpy as jnp
from jax import lax
from jax.experimental import pallas as pl
from jax.experimental.pallas import tpu as pltpu
from jax.sharding import PartitionSpec as P

BF16 = jnp.bfloat16
F32 = jnp.float32
BOTH = ("lat", "lon")


def dot_nn(a, b):
    return lax.dot_general(a, b, (((1,), (0,)), ((), ())), preferred_element_type=F32)


def dot_nt(a, b):
    return lax.dot_general(a, b, (((1,), (1,)), ((), ())), preferred_element_type=F32)


def dot_tn(a, b):
    return lax.dot_general(a, b, (((0,), (0,)), ((), ())), preferred_element_type=F32)


def cost(flops, nbytes):
    return pl.CostEstimate(flops=flops, bytes_accessed=nbytes, transcendentals=0)


def params():
    return pltpu.CompilerParams(vmem_limit_bytes=60 << 20)


def iota(shape, dim):
    return lax.broadcasted_iota(jnp.int32, shape, dim)


def upsample_body(lat, before, after, left, right, w_a, w_b, out, shifts):
    parity, half = pl.program_id(0), pl.program_id(1)
    rows, cols, width = lat.shape

    @pl.when((parity == 0) & (half == 0))
    def _():
        lefts, rights = left[...].astype(F32), right[...].astype(F32)
        place = iota((cols, width), 0)
        for r in range(rows + 2):
            row = before[0] if r == 0 else after[0] if r == rows + 1 else lat[r - 1]
            wide = row.astype(F32)
            shifts[1, r] = row
            shifts[0, r] = jnp.where(
                place == 0, lefts[r : r + 1], pltpu.roll(wide, 1, 0)
            ).astype(BF16)
            shifts[2, r] = jnp.where(
                place == cols - 1, rights[r : r + 1], pltpu.roll(wide, cols - 1, 0)
            ).astype(BF16)

    planes = []
    for taps in (((1, 0), (3, -1)), ((0, 1), (2, 0))):
        total = None
        for weight, start in ((w_a, 1 + parity), (w_b, parity)):
            for tap, step in taps:
                source = shifts[step + 1, pl.ds(start, rows)].reshape(rows * cols, width)
                term = dot_nt(source, weight[0, tap])
                total = term if total is None else total + term
        planes.append(total.astype(BF16))
    size = 2 * cols
    r, k = iota((size, size), 0), iota((size, size), 1)
    spread = (k == (r % 2) * cols + r // 2).astype(F32).astype(BF16)
    for m in range(rows):
        pair = jnp.concatenate([z[m * cols : (m + 1) * cols] for z in planes], axis=0)
        out[m, 0] = dot_nn(spread, pair).astype(BF16)


def upsample(lat, before, after, left, right, weight):
    rows, cols, width = lat.shape
    model = weight.shape[0] // 16
    half = model // 2
    whole = lambda *shape: pl.BlockSpec(shape, lambda p, h: (0,) * len(shape))
    return pl.pallas_call(
        upsample_body,
        grid=(2, 2),
        in_specs=[
            whole(rows, cols, width),
            whole(1, cols, width),
            whole(1, cols, width),
            whole(rows + 2, width),
            whole(rows + 2, width),
            pl.BlockSpec((1, 4, half, width), lambda p, h: (1 - p, 0, h, 0)),
            pl.BlockSpec((1, 4, half, width), lambda p, h: (3 - p, 0, h, 0)),
        ],
        out_specs=pl.BlockSpec((rows, 1, 2 * cols, half), lambda p, h: (0, p, 0, h)),
        out_shape=jax.ShapeDtypeStruct((rows, 2, 2 * cols, model), BF16),
        scratch_shapes=[pltpu.VMEM((3, rows + 2, cols, width), BF16)],
        compiler_params=params(),
        cost_estimate=cost(5 << 30, 12 << 20),
        name="upsample",
    )(lat, before, after, left, right, *[weight.reshape(4, 4, model, width)] * 2)


def middle_body(tokens, up, cot, w_in, w_out, act, pre, up_cot):
    hidden, model = w_out.shape
    step = 256
    for n in range(0, hidden, step):
        cols = slice(n, n + step)
        h = dot_nn(tokens[...], w_in[:model, cols]) + dot_nn(up[...], w_in[model:, cols])
        a = dot_nt(cot[...], w_out[cols, :])
        g = 0.5 * jnp.tanh(0.5 * h) + 0.5
        y = h * g
        act[:, cols] = y.astype(BF16)
        pre[:, cols] = (a * (g + y * (1.0 - g))).astype(BF16)
    up_cot[...] = dot_nt(pre[...], w_in[model:, :]).astype(BF16)


def middle(tokens, up, cot, w_in, w_out):
    count, model = tokens.shape
    hidden = w_out.shape[0]
    block = count // 4
    rows = lambda width: pl.BlockSpec((block, width), lambda i: (i, 0))
    whole = lambda a: pl.BlockSpec(a.shape, lambda i: (0, 0))
    return pl.pallas_call(
        middle_body,
        grid=(4,),
        in_specs=[rows(model)] * 3 + [whole(w_in), whole(w_out)],
        out_specs=[rows(hidden), rows(hidden), rows(model)],
        out_shape=[
            jax.ShapeDtypeStruct((count, hidden), BF16),
            jax.ShapeDtypeStruct((count, hidden), BF16),
            jax.ShapeDtypeStruct((count, model), BF16),
        ],
        compiler_params=params(),
        cost_estimate=cost(10 << 30, 20 << 20),
        name="middle",
    )(tokens, up, cot, w_in, w_out)


def out_grad_body(core, act, cot, keep, send, total):
    total[...] = dot_tn(act[...], cot[...])
    low = iota((32, 128), 1) < 64
    for which, ref in ((core[0], keep), (1 - core[0], send)):
        for y_hi in range(2):
            base = pl.multiple_of(y_hi * 128 + which * 64, 64)
            for x in range(4):
                cols = slice(x * 128, (x + 1) * 128)
                a = total[pl.ds(base, 32), cols]
                b = total[pl.ds(base + 32, 32), cols]
                at = x * 4 + y_hi * 2
                ref[at] = jnp.where(low, a, pltpu.roll(b, 64, 1)).astype(BF16)
                ref[at + 1] = jnp.where(low, pltpu.roll(a, 64, 1), b).astype(BF16)


def out_grad_blocks(core, act, cot):
    count, hidden = act.shape
    model = cot.shape[1]
    spec = pl.BlockSpec((16, 32, 128), lambda j, c: (j, 0, 0))
    return pl.pallas_call(
        out_grad_body,
        grid_spec=pltpu.PrefetchScalarGridSpec(
            num_scalar_prefetch=1,
            grid=(4,),
            in_specs=[
                pl.BlockSpec((count, hidden // 4), lambda j, c: (0, j)),
                pl.BlockSpec((count, model), lambda j, c: (0, 0)),
            ],
            out_specs=[spec, spec],
            scratch_shapes=[pltpu.VMEM((hidden // 4, model), F32)],
        ),
        out_shape=[jax.ShapeDtypeStruct((64, 32, 128), BF16)] * 2,
        compiler_params=params(),
        cost_estimate=cost(2 << 30, 7 << 20),
        name="out_grad",
    )(core, act, cot)


def in_grad_body(core, tokens, up, pre, keep, send, total):
    model = tokens.shape[1]
    total[:model] = dot_tn(tokens[...], pre[...])
    total[model:] = dot_tn(up[...], pre[...])
    for which, ref in ((core[0], keep), (1 - core[0], send)):
        for z in range(4):
            for y_hi in range(2):
                base = pl.multiple_of((z * 2 + y_hi) * 128 + which * 64, 64)
                for y_lo in range(2):
                    ref[z, 0, y_hi * 2 + y_lo] = total[
                        pl.ds(base, 64), y_lo * 128 : (y_lo + 1) * 128
                    ].astype(BF16)


def in_grad_blocks(core, tokens, up, pre):
    count, hidden = pre.shape
    model = tokens.shape[1]
    spec = pl.BlockSpec((4, 1, 4, 64, 128), lambda j, c: (0, j, 0, 0, 0))
    return pl.pallas_call(
        in_grad_body,
        grid_spec=pltpu.PrefetchScalarGridSpec(
            num_scalar_prefetch=1,
            grid=(4,),
            in_specs=[
                pl.BlockSpec((count, model), lambda j, c: (0, 0)),
                pl.BlockSpec((count, model), lambda j, c: (0, 0)),
                pl.BlockSpec((count, hidden // 4), lambda j, c: (0, j)),
            ],
            out_specs=[spec, spec],
            scratch_shapes=[pltpu.VMEM((2 * model, hidden // 4), F32)],
        ),
        out_shape=[jax.ShapeDtypeStruct((4, 4, 4, 64, 128), BF16)] * 2,
        compiler_params=params(),
        cost_estimate=cost(4 << 30, 10 << 20),
        name="in_grad",
    )(core, tokens, up, pre)


def united_body(tokens, act, w_out, out):
    out[...] = (tokens[...].astype(F32) + dot_nn(act[...], w_out[...])).astype(BF16)


def unite(tokens, act, w_out):
    count, model = tokens.shape
    hidden = act.shape[1]
    block = count // 4
    return pl.pallas_call(
        united_body,
        grid=(4,),
        in_specs=[
            pl.BlockSpec((block, model), lambda i: (i, 0)),
            pl.BlockSpec((block, hidden), lambda i: (i, 0)),
            pl.BlockSpec((hidden, model), lambda i: (0, 0)),
        ],
        out_specs=pl.BlockSpec((block, model), lambda i: (i, 0)),
        out_shape=jax.ShapeDtypeStruct((count, model), BF16),
        compiler_params=params(),
        cost_estimate=cost(2 << 30, 9 << 20),
        name="unite",
    )(tokens, act, w_out)


def pair_body(in_a, in_b, out_a, out_b, both):
    both[:, :64] = (in_a[...].astype(F32) + in_b[...].astype(F32)).astype(BF16)
    both[:, 64:] = (out_a[...].astype(F32) + out_b[...].astype(F32)).astype(BF16)


def add_pair(in_a, in_b, out_a, out_b):
    spec = lambda rows: pl.BlockSpec((32, rows, 128), lambda i: (i, 0, 0))
    return pl.pallas_call(
        pair_body,
        grid=(2,),
        in_specs=[spec(64), spec(64), spec(32), spec(32)],
        out_specs=spec(96),
        out_shape=jax.ShapeDtypeStruct((64, 96, 128), BF16),
        compiler_params=params(),
        cost_estimate=cost(1 << 20, 5 << 20),
        name="add_pair",
    )(in_a, in_b, out_a, out_b)


def sum_body(parts, in_grad, out_grad):
    total = parts[0].astype(F32)
    for i in range(1, parts.shape[0]):
        total = total + parts[i].astype(F32)
    in_grad[...] = total[:64]
    out_grad[:32] = total[64:, :64]
    out_grad[32:] = pltpu.roll(total[64:], 64, 1)[:, :64]


def sum_blocks(parts):
    return pl.pallas_call(
        sum_body,
        out_shape=[
            jax.ShapeDtypeStruct((64, 128), F32),
            jax.ShapeDtypeStruct((64, 64), F32),
        ],
        compiler_params=params(),
        cost_estimate=cost(1 << 20, 2 << 20),
        name="sum_blocks",
    )(parts)


def latent_body(cot, before, after, sides, weight, out, planes):
    step = pl.program_id(0)
    fine_rows, fine_cols, model = cot.shape
    cols = fine_cols // 2

    @pl.when(step == 0)
    def _():
        r, c = iota((4 * cols, fine_cols), 0), iota((4 * cols, fine_cols), 1)
        pick = (c == 2 * (r % cols) + r // cols - 1).astype(F32).astype(BF16)
        r, c = iota((4 * cols, 16), 0), iota((4 * cols, 16), 1)
        edge = ((r == 0) & (c == 0)) | ((r == 4 * cols - 1) & (c == 1))
        edge = edge.astype(F32).astype(BF16)
        for e in range(fine_rows + 2):
            row = before[0] if e == 0 else after[0] if e == fine_rows + 1 else cot[e - 1]
            found = (dot_nn(pick, row) + dot_nn(edge, sides[e])).astype(BF16)
            for tap in range(4):
                planes[e % 2, e // 2, :, tap * model : (tap + 1) * model] = found[
                    tap * cols : (tap + 1) * cols
                ]

    rows = fine_rows // 2
    source = planes[step % 2, pl.ds(step // 2, rows)].reshape(rows * cols, 4 * model)
    term = dot_nn(source, weight[0])

    @pl.when(step == 0)
    def _():
        out[...] = term

    @pl.when(step != 0)
    def _():
        out[...] += term


def latent_gradient(cot, before, after, sides, weight):
    fine_rows, fine_cols, model = cot.shape
    width = weight.shape[1]
    whole = lambda a: pl.BlockSpec(a.shape, lambda i: (0, 0, 0))
    size = fine_rows * fine_cols // 4
    return pl.pallas_call(
        latent_body,
        grid=(4,),
        in_specs=[
            whole(cot),
            whole(before),
            whole(after),
            whole(sides),
            pl.BlockSpec((1, 4 * model, width), lambda i: (i, 0, 0)),
        ],
        out_specs=pl.BlockSpec((size, width), lambda i: (0, 0)),
        out_shape=jax.ShapeDtypeStruct((size, width), F32),
        scratch_shapes=[
            pltpu.VMEM((2, fine_rows // 2 + 1, fine_cols // 2, 4 * model), BF16)
        ],
        compiler_params=params(),
        cost_estimate=cost(5 << 30, 12 << 20),
        name="latent_gradient",
    )(cot, before, after, sides, weight.reshape(4, 4 * model, width))


def neighbours(array, axis, dim, wrap):
    devices = lax.axis_size(axis)
    up = [(i, (i + 1) % devices) for i in range(devices if wrap else devices - 1)]
    down = [(j, i) for i, j in up]
    length = array.shape[dim]
    last = lax.slice_in_dim(array, length - 1, length, axis=dim)
    first = lax.slice_in_dim(array, 0, 1, axis=dim)
    return lax.ppermute(last, axis, up), lax.ppermute(first, axis, down)


def side_columns(array, before, after):
    devices = lax.axis_size("lon")
    up = [(i, (i + 1) % devices) for i in range(devices)]
    down = [(j, i) for i, j in up]
    column = lambda c: jnp.concatenate([before[:, c], array[:, c], after[:, c]], axis=0)
    return lax.ppermute(column(-1), "lon", up), lax.ppermute(column(0), "lon", down)


def chip_groups():
    return [
        [
            (x * 2 + y_lo) * 16 + z * 4 + y_hi * 2 + core
            for z in range(4)
            for x in range(4)
            for y_hi in range(2)
            for y_lo in range(2)
        ]
        for core in range(2)
    ]


def other_core(array):
    return lax.ppermute(array, "lon", [(i, i ^ 1) for i in range(16)])


def shards(fine_tokens, latents, upsample_weight, uniting_in, uniting_out, cotangent):
    count = fine_tokens.shape[0] * fine_tokens.shape[1]
    model = fine_tokens.shape[2]
    core = (lax.axis_index("lon") % 2).astype(jnp.int32).reshape(1)
    tokens = fine_tokens.reshape(count, model)
    cot = cotangent.reshape(count, model)

    before, after = neighbours(latents, "lat", 0, False)
    left, right = side_columns(latents, before, after)
    up = upsample(latents, before, after, left, right, upsample_weight)
    up = up.reshape(count, model)
    act, pre, up_cot = middle(tokens, up, cot, uniting_in, uniting_out)

    up_cot = up_cot.reshape(fine_tokens.shape)
    cot_before, cot_after = neighbours(up_cot, "lat", 0, False)
    out_keep, out_send = out_grad_blocks(core, act, cot)
    out_other = other_core(out_send)
    sides = side_columns(up_cot, cot_before, cot_after)
    in_keep, in_send = in_grad_blocks(core, tokens, up, pre)
    in_other = other_core(in_send)
    united = unite(tokens, act, uniting_out)
    flat = lambda a: a.reshape(64, 64, 128)
    halves = add_pair(flat(in_keep), flat(in_other), out_keep, out_other)
    parts = lax.all_to_all(halves, BOTH, 0, 0, axis_index_groups=chip_groups(), tiled=True)

    sides = jnp.pad(jnp.stack(sides, axis=1), ((0, 0), (0, 14), (0, 0)))
    latent_grad = latent_gradient(up_cot, cot_before, cot_after, sides, upsample_weight)
    in_grad, out_grad = sum_blocks(parts)
    return (
        united.reshape(fine_tokens.shape),
        latent_grad.reshape(latents.shape),
        in_grad,
        out_grad,
    )


def solution(mesh):
    return jax.shard_map(
        shards,
        mesh=mesh,
        in_specs=(
            P("lat", "lon", None),
            P("lat", "lon", None),
            P(),
            P(),
            P(),
            P("lat", "lon", None),
        ),
        out_specs=(P("lat", "lon", None), P("lat", "lon", None), P("lon", "lat"), P("lon", "lat")),
        check_vma=False,
    )
```

time: 295 us -> 126 us (0.43)
  the two profiles are of different devices: /device:TPU:1 before, /device:TPU:4 now
where the time goes in v1:
time: 126 us
  Pallas kernels  61.3 us (49%)
  starting transfers between devices  33.2 us (26%)
  waiting for transfers between devices  22.4 us (18%)
  local copies, waits for them, and re-layouts  6.83 us (5%)
    ppermute x4, waiting for transfers between devices, neighbours(): return (lax.ppermute(last, axis, up), lax.ppermute(first, axis, down))  20.7 us
    pallas_call x1, Pallas kernels, middle(): pl.pallas_call(middle_body, grid=(4,), in_specs=[rows(model)] * 3 + [whol...  13.4 us
    pallas_call x1, Pallas kernels, latent_gradient(): pl.pallas_call(latent_body, grid=(4,), in_specs=[whole(cot), whole(before...  11.5 us
    all_to_all x1, starting transfers between devices, shards(): lax.all_to_all(halves, BOTH, 0, 0, axis_index_groups=chip_groups(), tiled...  11.3 us
    ppermute x4, starting transfers between devices, neighbours(): return (lax.ppermute(last, axis, up), lax.ppermute(first, axis, down))  11.1 us
    ppermute x2, starting transfers between devices, side_columns(): lax.ppermute(column(0), 'lon', down)  9.54 us
    pallas_call x1, Pallas kernels, upsample(): pl.pallas_call(upsample_body, grid=(2, 2), in_specs=[whole(rows, cols, wi...  9.02 us
    pallas_call x1, Pallas kernels, in_grad_blocks(): pl.pallas_call(in_grad_body, grid_spec=pltpu.PrefetchScalarGridSpec(num_s...  8.93 us
  transfers between devices with their start and end apart: 11, of which 5 were waited for; matrix products, arithmetic and copies ran while one was open for 3% of the time, Pallas kernels for 22%

profile of v1, /device:TPU:4, one launch (start us, length us, event | category | flops | bytes accessed | tf_op | source)
XLA Modules:
  0.0 125.5 jit_solution(12273369011441767626)
XLA Ops:
  0.6 0.9 fusion.5
  1.5 3.5 %collective-permute-start.1 = (bf16[1,64,512]{2,1,0:T(8,128)(2,1)S(1)}, bf16[1,64,512]{2,1,0:T(8,128)(2,1)S(1)}, u32[]{:S(2)}, u32[]{:S(2)}) collective-permute-start(bf16[1,64,512]{2,1,0:T(8,128)(2,1)S(1)} %get-tuple-element.28), channel_id=1, source_target_pairs={{16,0},{32,16},{48,32},{64,48},{80,64},{96,80},{112,96},{17,1},{33... | collective-permute-start | bytes 196616 | tf_op jit(solution)/shard_map/ppermute | solution.py:342
  5.0 2.4 %collective-permute-start = (bf16[1,64,512]{2,1,0:T(8,128)(2,1)S(1)}, bf16[1,64,512]{2,1,0:T(8,128)(2,1)S(1)}, u32[]{:S(2)}, u32[]{:S(2)}) collective-permute-start(bf16[1,64,512]{2,1,0:T(8,128)(2,1)S(1)} %get-tuple-element.29), channel_id=1, source_target_pairs={{0,16},{16,32},{32,48},{48,64},{64,80},{80,96},{96,112},{1,17},{17... | collective-permute-start | bytes 196616 | tf_op jit(solution)/shard_map/ppermute | solution.py:342
  7.4 0.9 fusion.4
  8.3 3.7 %collective-permute-done.before = bf16[1,64,512]{2,1,0:T(8,128)(2,1)S(1)} collective-permute-done((bf16[1,64,512]{2,1,0:T(8,128)(2,1)S(1)}, bf16[1,64,512]{2,1,0:T(8,128)(2,1)S(1)}, u32[]{:S(2)}, u32[]{:S(2)}) %collective-permute-start) | collective-permute-done | bytes 65568 | tf_op jit(solution)/shard_map/ppermute | solution.py:342
  12.2 5.4 %collective-permute-start.3 = (bf16[10,512]{1,0:T(8,128)(2,1)S(1)}, bf16[10,512]{1,0:T(8,128)(2,1)S(1)}, u32[]{:S(2)}, u32[]{:S(2)}) collective-permute-start(bf16[10,512]{1,0:T(8,128)(2,1)S(1)} %pad_maximum_fusion.3), channel_id=1, source_target_pairs={{1,0},{2,1},{3,2},{4,3},{5,4},{6,5},{7,6},{8,7},{9,8},{10,9},{11,1... | collective-permute-start | bytes 30728 | tf_op jit(solution)/shard_map/ppermute | solution.py:350
  17.6 1.3 %collective-permute-done.2.left = bf16[10,512]{1,0:T(8,128)(2,1)S(1)} collective-permute-done((bf16[10,512]{1,0:T(8,128)(2,1)S(1)}, bf16[10,512]{1,0:T(8,128)(2,1)S(1)}, u32[]{:S(2)}, u32[]{:S(2)}) %collective-permute-start.2) | collective-permute-done | bytes 10272 | tf_op jit(solution)/shard_map/ppermute | solution.py:350
  19.6 9.0 %upsample.1 = bf16[8,2,128,512]{3,2,1,0:T(8,128)(2,1)} custom-call(bf16[8,64,512]{2,1,0:T(8,128)(2,1)} %lat.1, bf16[1,64,512]{2,1,0:T(8,128)(2,1)} %copy-done.4, bf16[1,64,512]{2,1,0:T(8,128)(2,1)} %copy-done.3, bf16[10,512]{1,0:T(8,128)(2,1)} %copy-done.7, bf16[10,512]{1,0:T(8,128)(2,1)} %copy-done.8, bf16[4,4,512,512]{3,2,1,0:T(8,128)(2,1)} %bitcast.59, ...), custom_call_target="tpu_custom_call" | custom-call | flops 5368709120 | bytes 12582912 | tf_op jit(solution)/shard_map/upsample/pallas_call | solution.py:78
  28.7 13.4 %middle.1 = (bf16[2048,1024]{1,0:T(8,128)(2,1)}, bf16[2048,1024]{1,0:T(8,128)(2,1)}, bf16[2048,512]{1,0:T(8,128)(2,1)}) custom-call(bf16[2048,512]{1,0:T(8,128)(2,1)} %bitcast.45, bf16[2048,512]{1,0:T(8,128)(2,1)} %bitcast.64, bf16[2048,512]{1,0:T(8,128)(2,1)} %bitcast.62, bf16[1024,1024]{1,0:T(8,128)(2,1)} %w_in.1, bf16[1024,512]{1,0:T(8,128)(2,1)} %w_out.3), custom_call_target="tpu_custom_call" | custom-call | flops 10737418240 | bytes 20971520 | tf_op jit(solution)/shard_map/middle/pallas_call | solution.py:119
  42.1 8.9 %in_grad.1 = (bf16[4,4,4,64,128]{4,3,2,1,0:T(8,128)(2,1)}, bf16[4,4,4,64,128]{4,3,2,1,0:T(8,128)(2,1)}) custom-call(s32[1]{0:T(128)} %bitcast.22.core, bf16[2048,512]{1,0:T(8,128)(2,1)} %bitcast.46, bf16[2048,512]{1,0:T(8,128)(2,1)} %bitcast.65, bf16[2048,1024]{1,0:T(8,128)(2,1)} %get-tuple-element.15.pre), custom_call_target="tpu_custom_call" | custom-call | flops 4294967296 | bytes 10485760 | tf_op jit(solution)/shard_map/in_grad/pallas_call | solution.py:191
  51.0 0.9 collective-permute-start.8
  51.9 6.6 %out_grad.1 = (bf16[64,32,128]{2,1,0:T(8,128)(2,1)}, bf16[64,32,128]{2,1,0:T(8,128)(2,1)}) custom-call(s32[1]{0:T(128)} %bitcast.22.core, bf16[2048,1024]{1,0:T(8,128)(2,1)} %get-tuple-element.13.act, bf16[2048,512]{1,0:T(8,128)(2,1)} %bitcast.63), custom_call_target="tpu_custom_call" | custom-call | flops 2147483648 | bytes 7340032 | tf_op jit(solution)/shard_map/out_grad/pallas_call | solution.py:154
  58.5 1.0 slice_bitcast_fusion
  59.5 1.9 %collective-permute-start.5 = (bf16[1,128,512]{2,1,0:T(8,128)(2,1)S(1)}, bf16[1,128,512]{2,1,0:T(8,128)(2,1)S(1)}, u32[]{:S(2)}, u32[]{:S(2)}) collective-permute-start(bf16[1,128,512]{2,1,0:T(8,128)(2,1)S(1)} %get-tuple-element.24), channel_id=1, source_target_pairs={{16,0},{32,16},{48,32},{64,48},{80,64},{96,80},{112,96},{17,1},{33... | collective-permute-start | bytes 393224 | tf_op jit(solution)/shard_map/ppermute | solution.py:342
  62.6 2.9 %add_pair.1 = bf16[64,96,128]{2,1,0:T(8,128)(2,1)} custom-call(bf16[64,64,128]{2,1,0:T(8,128)(2,1)} %bitcast.49, bf16[64,64,128]{2,1,0:T(8,128)(2,1)} %bitcast.50, bf16[64,32,128]{2,1,0:T(8,128)(2,1)} %get-tuple-element.18.out_a, bf16[64,32,128]{2,1,0:T(8,128)(2,1)} %copy-done.2), custom_call_target="tpu_custom_call" | custom-call | flops 1048576 | bytes 5242880 | tf_op jit(solution)/shard_map/add_pair/pallas_call | solution.py:242
  65.6 11.3 %all-to-all-start = ((bf16[64,96,128]{2,1,0:T(8,128)(2,1)}), bf16[64,96,128]{2,1,0:T(8,128)(2,1)S(1)}, u32[]{:S(2)}, u32[]{:S(2)}) async-start(bf16[64,96,128]{2,1,0:T(8,128)(2,1)} %add_pair.1), calls=%async_computation | async-start | bytes 3145728 | tf_op jit(solution)/shard_map/all_to_all | solution.py:393
  76.9 1.0 fusion.3
  77.9 3.4 %collective-permute-start.4 = (bf16[1,128,512]{2,1,0:T(8,128)(2,1)S(1)}, bf16[1,128,512]{2,1,0:T(8,128)(2,1)S(1)}, u32[]{:S(2)}, u32[]{:S(2)}) collective-permute-start(bf16[1,128,512]{2,1,0:T(8,128)(2,1)S(1)} %get-tuple-element.25), channel_id=1, source_target_pairs={{0,16},{16,32},{32,48},{48,64},{64,80},{80,96},{96,112},{1,17},{17... | collective-permute-start | bytes 393224 | tf_op jit(solution)/shard_map/ppermute | solution.py:342
  81.3 17.0 %collective-permute-done.4.before = bf16[1,128,512]{2,1,0:T(8,128)(2,1)S(1)} collective-permute-done((bf16[1,128,512]{2,1,0:T(8,128)(2,1)S(1)}, bf16[1,128,512]{2,1,0:T(8,128)(2,1)S(1)}, u32[]{:S(2)}, u32[]{:S(2)}) %collective-permute-start.4) | collective-permute-done | bytes 131104 | tf_op jit(solution)/shard_map/ppermute | solution.py:342
  98.4 4.1 %collective-permute-start.7 = (bf16[18,512]{1,0:T(8,128)(2,1)S(1)}, bf16[18,512]{1,0:T(8,128)(2,1)S(1)}, u32[]{:S(2)}, u32[]{:S(2)}) collective-permute-start(bf16[18,512]{1,0:T(8,128)(2,1)S(1)} %pad_maximum_fusion.1), channel_id=1, source_target_pairs={{1,0},{2,1},{3,2},{4,3},{5,4},{6,5},{7,6},{8,7},{9,8},{10,9},{11,1... | collective-permute-start | bytes 55304 | tf_op jit(solution)/shard_map/ppermute | solution.py:350
  102.8 6.5 %unite.1 = bf16[2048,512]{1,0:T(8,128)(2,1)} custom-call(bf16[2048,512]{1,0:T(8,128)(2,1)} %bitcast.47, bf16[2048,1024]{1,0:T(8,128)(2,1)} %get-tuple-element.13.act, bf16[1024,512]{1,0:T(8,128)(2,1)} %w_out.3), custom_call_target="tpu_custom_call" | custom-call | flops 2147483648 | bytes 9437184 | tf_op jit(solution)/shard_map/unite/pallas_call | solution.py:219
  110.5 11.5 %latent_gradient.1 = f32[512,512]{1,0:T(8,128)} custom-call(bf16[16,128,512]{2,1,0:T(8,128)(2,1)} %bitcast.54, bf16[1,128,512]{2,1,0:T(8,128)(2,1)} %copy-done.6, bf16[1,128,512]{2,1,0:T(8,128)(2,1)} %copy-done.5, bf16[18,16,512]{2,1,0:T(8,128)(2,1)} %fusion.2.sides, bf16[4,2048,512]{2,1,0:T(8,128)(2,1)} %bitcast.61), custom_call_target="tpu_custom_call" | custom-call | flops 5368709120 | bytes 12582912 | tf_op jit(solution)/shard_map/latent_gradient/pallas_call | solution.py:314
  122.1 1.2 copy-done
  123.2 2.3 %sum_blocks.1 = (f32[64,128]{1,0:T(8,128)}, f32[64,64]{1,0:T(8,128)}) custom-call(bf16[64,96,128]{2,1,0:T(8,128)(2,1)} %copy-done), custom_call_target="tpu_custom_call" | custom-call | flops 1048576 | bytes 2097152 | tf_op jit(solution)/shard_map/sum_blocks/pallas_call | solution.py:264
  (43 shorter events, 3.5 us)
Async XLA Ops:
  1.5 6.8 %collective-permute-start.1 = (bf16[1,64,512]{2,1,0:T(8,128)(2,1)S(1)}, bf16[1,64,512]{2,1,0:T(8,128)(2,1)S(1)}, u32[]{:S(2)}, u32[]{:S(2)}) collective-permute-start(bf16[1,64,512]{2,1,0:T(8,128)(2,1)S(1)} %get-tuple-element.28), channel_id=1, source_target_pairs={{16,0},{32,16},{48,32},{64,48},{80,64},{96,80},{112,96},{17,1},{33... | collective-permute-start | bytes 196616 | tf_op jit(solution)/shard_map/ppermute | solution.py:342
  5.0 7.1 %collective-permute-start = (bf16[1,64,512]{2,1,0:T(8,128)(2,1)S(1)}, bf16[1,64,512]{2,1,0:T(8,128)(2,1)S(1)}, u32[]{:S(2)}, u32[]{:S(2)}) collective-permute-start(bf16[1,64,512]{2,1,0:T(8,128)(2,1)S(1)} %get-tuple-element.29), channel_id=1, source_target_pairs={{0,16},{16,32},{32,48},{48,64},{64,80},{80,96},{96,112},{1,17},{17... | collective-permute-start | bytes 196616 | tf_op jit(solution)/shard_map/ppermute | solution.py:342
  8.3 10.7 %copy-start.3 = (bf16[1,64,512]{2,1,0:T(8,128)(2,1)}, bf16[1,64,512]{2,1,0:T(8,128)(2,1)S(1)}, u32[]{:S(2)}) copy-start(bf16[1,64,512]{2,1,0:T(8,128)(2,1)S(1)} %collective-permute-done.1.after) | copy-start | bytes 196612
  12.0 7.0 %copy-start.4 = (bf16[1,64,512]{2,1,0:T(8,128)(2,1)}, bf16[1,64,512]{2,1,0:T(8,128)(2,1)S(1)}, u32[]{:S(2)}) copy-start(bf16[1,64,512]{2,1,0:T(8,128)(2,1)S(1)} %collective-permute-done.before) | copy-start | bytes 196612
  12.1 6.8 %collective-permute-start.2 = (bf16[10,512]{1,0:T(8,128)(2,1)S(1)}, bf16[10,512]{1,0:T(8,128)(2,1)S(1)}, u32[]{:S(2)}, u32[]{:S(2)}) collective-permute-start(bf16[10,512]{1,0:T(8,128)(2,1)S(1)} %pad_maximum_fusion.2), channel_id=1, source_target_pairs={{0,1},{1,2},{2,3},{3,4},{4,5},{5,6},{6,7},{7,8},{8,9},{9,10},{10,1... | collective-permute-start | bytes 30728 | tf_op jit(solution)/shard_map/ppermute | solution.py:350
  12.2 6.9 %collective-permute-start.3 = (bf16[10,512]{1,0:T(8,128)(2,1)S(1)}, bf16[10,512]{1,0:T(8,128)(2,1)S(1)}, u32[]{:S(2)}, u32[]{:S(2)}) collective-permute-start(bf16[10,512]{1,0:T(8,128)(2,1)S(1)} %pad_maximum_fusion.3), channel_id=1, source_target_pairs={{1,0},{2,1},{3,2},{4,3},{5,4},{6,5},{7,6},{8,7},{9,8},{10,9},{11,1... | collective-permute-start | bytes 30728 | tf_op jit(solution)/shard_map/ppermute | solution.py:350
  18.9 0.6 copy-start.7
  19.0 0.6 copy-start.8
  51.0 10.5 %collective-permute-start.8 = (bf16[4,4,4,64,128]{4,3,2,1,0:T(8,128)(2,1)}, bf16[4,4,4,64,128]{4,3,2,1,0:T(8,128)(2,1)S(1)}, u32[]{:S(2)}, u32[]{:S(2)}) collective-permute-start(bf16[4,4,4,64,128]{4,3,2,1,0:T(8,128)(2,1)} %get-tuple-element.17), channel_id=1, source_target_pairs={{0,1},{1,0},{2,3},{3,2},{4,5},{5,4},{6,7},{7,6},{8,9},{9,8},{10,11... | collective-permute-start | bytes 3145736 | tf_op jit(solution)/shard_map/ppermute | solution.py:367
  58.5 2.9 %collective-permute-start.9 = (bf16[64,32,128]{2,1,0:T(8,128)(2,1)}, bf16[64,32,128]{2,1,0:T(8,128)(2,1)S(1)}, u32[]{:S(2)}, u32[]{:S(2)}) collective-permute-start(bf16[64,32,128]{2,1,0:T(8,128)(2,1)} %get-tuple-element.19), channel_id=1, source_target_pairs={{0,1},{1,0},{2,3},{3,2},{4,5},{5,4},{6,7},{7,6},{8,9},{9,8},{10,11... | collective-permute-start | bytes 1572872 | tf_op jit(solution)/shard_map/ppermute | solution.py:367
  59.5 21.8 %collective-permute-start.5 = (bf16[1,128,512]{2,1,0:T(8,128)(2,1)S(1)}, bf16[1,128,512]{2,1,0:T(8,128)(2,1)S(1)}, u32[]{:S(2)}, u32[]{:S(2)}) collective-permute-start(bf16[1,128,512]{2,1,0:T(8,128)(2,1)S(1)} %get-tuple-element.24), channel_id=1, source_target_pairs={{16,0},{32,16},{48,32},{64,48},{80,64},{96,80},{112,96},{17,1},{33... | collective-permute-start | bytes 393224 | tf_op jit(solution)/shard_map/ppermute | solution.py:342
  61.5 0.8 copy-start.2
  61.5 1.1 copy-start.1
  65.6 56.5 %all-to-all-start = ((bf16[64,96,128]{2,1,0:T(8,128)(2,1)}), bf16[64,96,128]{2,1,0:T(8,128)(2,1)S(1)}, u32[]{:S(2)}, u32[]{:S(2)}) async-start(bf16[64,96,128]{2,1,0:T(8,128)(2,1)} %add_pair.1), calls=%async_computation | async-start | bytes 3145728 | tf_op jit(solution)/shard_map/all_to_all | solution.py:393
  77.9 20.5 %collective-permute-start.4 = (bf16[1,128,512]{2,1,0:T(8,128)(2,1)S(1)}, bf16[1,128,512]{2,1,0:T(8,128)(2,1)S(1)}, u32[]{:S(2)}, u32[]{:S(2)}) collective-permute-start(bf16[1,128,512]{2,1,0:T(8,128)(2,1)S(1)} %get-tuple-element.25), channel_id=1, source_target_pairs={{0,16},{16,32},{32,48},{48,64},{64,80},{80,96},{96,112},{1,17},{17... | collective-permute-start | bytes 393224 | tf_op jit(solution)/shard_map/ppermute | solution.py:342
  81.3 28.1 %copy-start.5 = (bf16[1,128,512]{2,1,0:T(8,128)(2,1)}, bf16[1,128,512]{2,1,0:T(8,128)(2,1)S(1)}, u32[]{:S(2)}) copy-start(bf16[1,128,512]{2,1,0:T(8,128)(2,1)S(1)} %collective-permute-done.5.after) | copy-start | bytes 393220
  98.4 11.0 %copy-start.6 = (bf16[1,128,512]{2,1,0:T(8,128)(2,1)}, bf16[1,128,512]{2,1,0:T(8,128)(2,1)S(1)}, u32[]{:S(2)}) copy-start(bf16[1,128,512]{2,1,0:T(8,128)(2,1)S(1)} %collective-permute-done.4.before) | copy-start | bytes 393220
  98.4 11.0 %collective-permute-start.7 = (bf16[18,512]{1,0:T(8,128)(2,1)S(1)}, bf16[18,512]{1,0:T(8,128)(2,1)S(1)}, u32[]{:S(2)}, u32[]{:S(2)}) collective-permute-start(bf16[18,512]{1,0:T(8,128)(2,1)S(1)} %pad_maximum_fusion.1), channel_id=1, source_target_pairs={{1,0},{2,1},{3,2},{4,3},{5,4},{6,5},{7,6},{8,7},{9,8},{10,9},{11,1... | collective-permute-start | bytes 55304 | tf_op jit(solution)/shard_map/ppermute | solution.py:350
  102.5 7.1 %collective-permute-start.6 = (bf16[18,512]{1,0:T(8,128)(2,1)S(1)}, bf16[18,512]{1,0:T(8,128)(2,1)S(1)}, u32[]{:S(2)}, u32[]{:S(2)}) collective-permute-start(bf16[18,512]{1,0:T(8,128)(2,1)S(1)} %pad_maximum_fusion), channel_id=1, source_target_pairs={{0,1},{1,2},{2,3},{3,4},{4,5},{5,6},{6,7},{7,8},{8,9},{9,10},{10,1... | collective-permute-start | bytes 55304 | tf_op jit(solution)/shard_map/ppermute | solution.py:350
  122.1 1.2 copy-start

commit v2 on v0

v2 whole, which is shorter than its diff:
```python
import jax
import jax.numpy as jnp
from jax import lax
from jax.experimental import pallas as pl
from jax.experimental.pallas import tpu as pltpu
from jax.sharding import PartitionSpec as P

BF16 = jnp.bfloat16
F32 = jnp.float32
BOTH = ("lat", "lon")


def dot_nn(a, b):
    return lax.dot_general(a, b, (((1,), (0,)), ((), ())), preferred_element_type=F32)


def dot_nt(a, b):
    return lax.dot_general(a, b, (((1,), (1,)), ((), ())), preferred_element_type=F32)


def dot_tn(a, b):
    return lax.dot_general(a, b, (((0,), (0,)), ((), ())), preferred_element_type=F32)


def cost(flops, nbytes):
    return pl.CostEstimate(flops=flops, bytes_accessed=nbytes, transcendentals=0)


def params():
    return pltpu.CompilerParams(vmem_limit_bytes=60 << 20)


def iota(shape, dim):
    return lax.broadcasted_iota(jnp.int32, shape, dim)


def main_body(
    core, lat, before, after, left, right, w_a, w_b, h_top, a_top, tokens_hbm, cot_hbm, w_hbm,
    act_out, up_cot, keep, send,
    shifts, tokens, cot, w_low, up, act, pre, turned, sems,
):
    step = pl.program_id(0)
    rows, cols, width = lat.shape
    model, hidden = w_low.shape
    block = h_top.shape[0]
    copies = [
        pltpu.make_async_copy(w_hbm.at[pl.ds(model, model)], w_low, sems.at[0]),
        pltpu.make_async_copy(tokens_hbm, tokens, sems.at[1]),
        pltpu.make_async_copy(cot_hbm, cot, sems.at[2]),
    ]

    @pl.when(step == 0)
    def _():
        for copy in copies:
            copy.start()
        lefts, rights = left[...].astype(F32), right[...].astype(F32)
        place = iota((cols, width), 0)
        for r in range(rows + 2):
            row = before[0] if r == 0 else after[0] if r == rows + 1 else lat[r - 1]
            wide = row.astype(F32)
            shifts[1, r] = row
            shifts[0, r] = jnp.where(
                place == 0, lefts[r : r + 1], pltpu.roll(wide, 1, 0)
            ).astype(BF16)
            shifts[2, r] = jnp.where(
                place == cols - 1, rights[r : r + 1], pltpu.roll(wide, cols - 1, 0)
            ).astype(BF16)

    @pl.when(step < 4)
    def _():
        parity, half = step // 2, step % 2
        planes = []
        for taps in (((1, 0), (3, -1)), ((0, 1), (2, 0))):
            total = None
            for weight, start in ((w_a, 1 + parity), (w_b, parity)):
                for tap, move in taps:
                    source = shifts[move + 1, pl.ds(start, rows)].reshape(rows * cols, width)
                    term = dot_nt(source, weight[0, tap])
                    total = term if total is None else total + term
            planes.append(total.astype(BF16))
        size = 2 * cols
        r, k = iota((size, size), 0), iota((size, size), 1)
        spread = (k == (r % 2) * cols + r // 2).astype(F32).astype(BF16)
        for m in range(rows):
            pair = jnp.concatenate([z[m * cols : (m + 1) * cols] for z in planes], axis=0)
            value = dot_nn(spread, pair).astype(BF16)
            at = pl.ds(pl.multiple_of((2 * m + parity) * size, size), size)
            for side in range(2):
                @pl.when(half == side)
                def _():
                    up[at, side * (model // 2) : (side + 1) * (model // 2)] = value

    @pl.when(step == 4)
    def _():
        for copy in copies:
            copy.wait()

    @pl.when((step >= 4) & (step < 8))
    def _():
        at = pl.ds(pl.multiple_of((step - 4) * block, block), block)
        for n in range(0, hidden, 256):
            span = slice(n, n + 256)
            h = h_top[:, span].astype(F32) + dot_nn(up[at, :], w_low[:, span])
            g = 0.5 * jnp.tanh(0.5 * h) + 0.5
            y = h * g
            wide = y.astype(BF16)
            act[at, span] = wide
            act_out[:, span] = wide
            a = a_top[:, span].astype(F32)
            pre[at, span] = (a * (g + y * (1.0 - g))).astype(BF16)
        up_cot[...] = dot_nt(pre[at, :], w_low[...]).astype(BF16)
        turned[0:model, at] = tokens[at, :].T
        turned[model : 2 * model, at] = up[at, :].T
        turned[2 * model :, at] = cot[at, :].T

    for j in range(4):

        @pl.when(step == 8 + j)
        def _():
            span = slice(j * 256, (j + 1) * 256)
            mine = core[0]
            total = dot_nn(turned[: 2 * model], pre[:, span])
            for z in range(4):
                for y_hi in range(2):
                    base = (z * 2 + y_hi) * 128
                    first, second = total[base : base + 64], total[base + 64 : base + 128]
                    own = jnp.where(mine == 0, first, second).astype(BF16)
                    other = jnp.where(mine == 0, second, first).astype(BF16)
                    for y_lo in range(2):
                        lanes = slice(y_lo * 128, (y_lo + 1) * 128)
                        keep[z, j, y_hi * 2 + y_lo, 0:64] = own[:, lanes]
                        send[z, j, y_hi * 2 + y_lo, 0:64] = other[:, lanes]
            total = dot_nn(turned[2 * model :], act[:, span])
            low = iota((32, 128), 1) < 64
            for lat_id in range(8):
                for y_hi in range(2):
                    lanes = slice(y_hi * 128, (y_hi + 1) * 128)
                    a = total[lat_id * 64 : lat_id * 64 + 32, lanes]
                    b = total[lat_id * 64 + 32 : lat_id * 64 + 64, lanes]
                    first = jnp.where(low, a, pltpu.roll(b, 64, 1))
                    second = jnp.where(low, pltpu.roll(a, 64, 1), b)
                    at = y_hi * 2 + lat_id % 2
                    keep[j, lat_id // 2, at, 64:96] = jnp.where(
                        mine == 0, first, second
                    ).astype(BF16)
                    send[j, lat_id // 2, at, 64:96] = jnp.where(
                        mine == 0, second, first
                    ).astype(BF16)


def main_kernel(core, lat, before, after, left, right, weight, h_top, a_top, tokens, cot, w_in):
    rows, cols, width = lat.shape
    model = weight.shape[0] // 16
    half = model // 2
    count, hidden = h_top.shape
    block = count // 4
    clamp = lambda i, low: jnp.clip(i - low, 0, 3)
    whole = lambda *shape: pl.BlockSpec(shape, lambda i, c: (0,) * len(shape))
    kernel_row = lambda i, top: (top - clamp(i, 0) // 2, 0, clamp(i, 0) % 2, 0)
    tokens_of = lambda w: pl.BlockSpec((block, w), lambda i, c: (clamp(i, 4), 0))
    blocks = (4, 4, 4, 96, 128)
    return pl.pallas_call(
        main_body,
        grid_spec=pltpu.PrefetchScalarGridSpec(
            num_scalar_prefetch=1,
            grid=(12,),
            in_specs=[
                whole(rows, cols, width),
                whole(1, cols, width),
                whole(1, cols, width),
                whole(rows + 2, width),
                whole(rows + 2, width),
                pl.BlockSpec((1, 4, half, width), lambda i, c: kernel_row(i, 1)),
                pl.BlockSpec((1, 4, half, width), lambda i, c: kernel_row(i, 3)),
                tokens_of(hidden),
                tokens_of(hidden),
                pl.BlockSpec(memory_space=pl.ANY),
                pl.BlockSpec(memory_space=pl.ANY),
                pl.BlockSpec(memory_space=pl.ANY),
            ],
            out_specs=[tokens_of(hidden), tokens_of(model), whole(*blocks), whole(*blocks)],
            scratch_shapes=[
                pltpu.VMEM((3, rows + 2, cols, width), BF16),
                pltpu.VMEM((count, model), BF16),
                pltpu.VMEM((count, model), BF16),
                pltpu.VMEM((model, hidden), BF16),
                pltpu.VMEM((count, model), BF16),
                pltpu.VMEM((count, hidden), BF16),
                pltpu.VMEM((count, hidden), BF16),
                pltpu.VMEM((3 * model, count), BF16),
                pltpu.SemaphoreType.DMA((3,)),
            ],
        ),
        out_shape=[
            jax.ShapeDtypeStruct((count, hidden), BF16),
            jax.ShapeDtypeStruct((count, model), BF16),
            jax.ShapeDtypeStruct(blocks, BF16),
            jax.ShapeDtypeStruct(blocks, BF16),
        ],
        compiler_params=params(),
        cost_estimate=cost(18 << 30, 36 << 20),
        name="main",
    )(
        core, lat, before, after, left, right, *[weight.reshape(4, 4, model, width)] * 2,
        h_top, a_top, tokens, cot, w_in,
    )


def tail_body(
    tokens, act, w_out, cot_hbm, before, after, left, right, weight, united, out,
    cot, planes, sem,
):
    step = pl.program_id(0)
    fine_rows, fine_cols, model = cot.shape
    cols = fine_cols // 2
    rows = fine_rows // 2
    copy = pltpu.make_async_copy(cot_hbm, cot, sem.at[0])

    @pl.when(step == 0)
    def _():
        copy.start()

    @pl.when(step < 4)
    def _():
        united[...] = (tokens[...].astype(F32) + dot_nn(act[...], w_out[...])).astype(BF16)

    @pl.when(step == 4)
    def _():
        copy.wait()
        r, c = iota((fine_cols, fine_cols), 0), iota((fine_cols, fine_cols), 1)
        pick = (c == 2 * (r % cols) + r // cols).astype(F32).astype(BF16)
        lefts, rights = left[...].astype(F32), right[...].astype(F32)
        place = iota((cols, model), 0)
        for e in range(fine_rows + 2):
            row = before[0] if e == 0 else after[0] if e == fine_rows + 1 else cot[e - 1]
            found = dot_nn(pick, row)
            even, odd = found[:cols], found[cols:]
            taps = (
                jnp.where(place == 0, lefts[e : e + 1], pltpu.roll(odd, 1, 0)),
                even,
                odd,
                jnp.where(place == cols - 1, rights[e : e + 1], pltpu.roll(even, cols - 1, 0)),
            )
            for tap in range(4):
                planes[e % 2, e // 2, :, tap * model : (tap + 1) * model] = taps[tap].astype(BF16)

    @pl.when(step >= 4)
    def _():
        k = step - 4
        source = planes[k % 2, pl.ds(k // 2, rows)].reshape(rows * cols, 4 * model)
        term = dot_nn(source, weight[0])

        @pl.when(k == 0)
        def _():
            out[...] = term

        @pl.when(k != 0)
        def _():
            out[...] += term


def tail_kernel(tokens, act, w_out, cot, before, after, left, right, weight):
    fine_rows, fine_cols, model = cot.shape
    width = weight.shape[1]
    count, hidden = act.shape
    block = count // 4
    whole = lambda a: pl.BlockSpec(a.shape, lambda i: (0,) * a.ndim)
    size = fine_rows * fine_cols // 4
    tokens_of = lambda w: pl.BlockSpec((block, w), lambda i: (jnp.minimum(i, 3), 0))
    return pl.pallas_call(
        tail_body,
        grid=(8,),
        in_specs=[
            tokens_of(model),
            tokens_of(hidden),
            whole(w_out),
            pl.BlockSpec(memory_space=pl.ANY),
            whole(before),
            whole(after),
            whole(left),
            whole(right),
            pl.BlockSpec((1, 4 * model, width), lambda i: (jnp.maximum(i - 4, 0), 0, 0)),
        ],
        out_specs=[tokens_of(model), pl.BlockSpec((size, width), lambda i: (0, 0))],
        out_shape=[
            jax.ShapeDtypeStruct((count, model), BF16),
            jax.ShapeDtypeStruct((size, width), F32),
        ],
        scratch_shapes=[
            pltpu.VMEM((fine_rows, fine_cols, model), BF16),
            pltpu.VMEM((2, fine_rows // 2 + 1, fine_cols // 2, 4 * model), BF16),
            pltpu.SemaphoreType.DMA((1,)),
        ],
        compiler_params=pltpu.CompilerParams(vmem_limit_bytes=40 << 20),
        cost_estimate=cost(7 << 30, 22 << 20),
        name="tail",
    )(tokens, act, w_out, cot, before, after, left, right, weight.reshape(4, 4 * model, width))


def sum_body(parts, in_grad, out_grad):
    total = parts[0].astype(F32)
    for i in range(1, parts.shape[0]):
        total = total + parts[i].astype(F32)
    in_grad[...] = total[:64]
    packed = total[64:]
    out_grad[...] = jnp.concatenate(
        [packed, pltpu.roll(packed, 64, 1)], axis=0
    ).T[:64, :]


def sum_blocks(parts):
    return pl.pallas_call(
        sum_body,
        out_shape=[
            jax.ShapeDtypeStruct((64, 128), F32),
            jax.ShapeDtypeStruct((64, 64), F32),
        ],
        compiler_params=pltpu.CompilerParams(vmem_limit_bytes=8 << 20),
        cost_estimate=cost(1 << 20, 2 << 20),
        name="sum_blocks",
    )(parts)


def neighbours(array, axis, dim, wrap):
    devices = lax.axis_size(axis)
    up = [(i, (i + 1) % devices) for i in range(devices if wrap else devices - 1)]
    down = [(j, i) for i, j in up]
    length = array.shape[dim]
    last = lax.slice_in_dim(array, length - 1, length, axis=dim)
    first = lax.slice_in_dim(array, 0, 1, axis=dim)
    return lax.ppermute(last, axis, up), lax.ppermute(first, axis, down)


def side_columns(array, before, after):
    devices = lax.axis_size("lon")
    up = [(i, (i + 1) % devices) for i in range(devices)]
    down = [(j, i) for i, j in up]
    column = lambda c: jnp.concatenate([before[:, c], array[:, c], after[:, c]], axis=0)
    return lax.ppermute(column(-1), "lon", up), lax.ppermute(column(0), "lon", down)


def chip_groups():
    return [
        [
            (x * 2 + y_lo) * 16 + z * 4 + y_hi * 2 + core
            for z in range(4)
            for x in range(4)
            for y_hi in range(2)
            for y_lo in range(2)
        ]
        for core in range(2)
    ]


def other_core(array):
    return lax.ppermute(array, "lon", [(i, i ^ 1) for i in range(16)])


def shards(fine_tokens, latents, upsample_weight, uniting_in, uniting_out, cotangent):
    count = fine_tokens.shape[0] * fine_tokens.shape[1]
    model = fine_tokens.shape[2]
    core = (lax.axis_index("lon") % 2).astype(jnp.int32).reshape(1)
    tokens = fine_tokens.reshape(count, model)
    cot = cotangent.reshape(count, model)

    before, after = neighbours(latents, "lat", 0, False)
    left, right = side_columns(latents, before, after)
    a_top = dot_nt(cot, uniting_out).astype(BF16)
    h_top = dot_nn(tokens, uniting_in[:model]).astype(BF16)
    act, up_cot, keep, send = main_kernel(
        core, latents, before, after, left, right, upsample_weight,
        h_top, a_top, tokens, cot, uniting_in,
    )

    up_cot = up_cot.reshape(fine_tokens.shape)
    cot_before, cot_after = neighbours(up_cot, "lat", 0, False)
    other = other_core(send)
    cot_left, cot_right = side_columns(up_cot, cot_before, cot_after)
    halves = (keep.astype(F32) + other.astype(F32)).astype(BF16).reshape(64, 96, 128)
    halves, cot_left, cot_right = lax.optimization_barrier((halves, cot_left, cot_right))
    parts = lax.all_to_all(halves, BOTH, 0, 0, axis_index_groups=chip_groups(), tiled=True)

    united, latent_grad = tail_kernel(
        tokens, act, uniting_out, up_cot, cot_before, cot_after, cot_left, cot_right,
        upsample_weight,
    )
    in_grad, out_grad = sum_blocks(parts)
    return (
        united.reshape(fine_tokens.shape),
        latent_grad.reshape(latents.shape),
        in_grad,
        out_grad,
    )


def solution(mesh):
    return jax.shard_map(
        shards,
        mesh=mesh,
        in_specs=(
            P("lat", "lon", None),
            P("lat", "lon", None),
            P(),
            P(),
            P(),
            P("lat", "lon", None),
        ),
        out_specs=(P("lat", "lon", None), P("lat", "lon", None), P("lon", "lat"), P("lon", "lat")),
        check_vma=False,
    )
```

time: 295 us -> 116 us (0.39); the launches traced: 290 us -> 115 us
  waiting for transfers between devices: 162 us -> 12 us
  matrix products: 65.3 us -> 10.7 us
  Pallas kernels: 0 us -> 45.1 us
  starting transfers between devices: 19.2 us -> 33.6 us
  between operations: 14.3 us -> 0.88 us
  local copies, waits for them, and re-layouts: 21.8 us -> 9.84 us
  other arithmetic: 6.88 us -> 3.1 us
    reduce_scatter x3 -> x0, waiting for transfers between devices: 132 us -> none  [the longest x1 69.7 us: shards(): lax.psum_scatter(in_local.astype(jnp.bfloat16), 'lon', scatter_dimension=...]
    dot_general x38 -> x2, matrix products: 65.3 us -> 10.7 us  [the longest x1 6.37 us: dot_nn(): lax.dot_general(a, b, (((1,), (0,)), ((), ())), preferred_element_type=F32)]
    pallas_call x0 -> x3, Pallas kernels: none -> 45.1 us  [the longest x1 31.9 us: main_kernel(): pl.pallas_call(main_body, grid_spec=pltpu.PrefetchScalarGridSpec(num_scal...]
    unnamed x5 -> x0, waiting for transfers between devices: 29.1 us -> none
    all_to_all x0 -> x1, starting transfers between devices: none -> 13.4 us  [shards(): lax.all_to_all(halves, BOTH, 0, 0, axis_index_groups=chip_groups(), tiled...]
    reshape x2 -> x0, local copies, waits for them, and re-layouts: 8.3 us -> none  [shards(): cot_ext.reshape(lat_rows + 1, 2, lat_cols + 1, 2, model_width)]
    another operation x2 -> x0, local copies, waits for them, and re-layouts: 7.68 us -> none  [the longest x1 4.2 us: shards(): upsampled.reshape(token_count, model_width)]
    all_to_all x0 -> x1, waiting for transfers between devices: none -> 5.85 us  [shards(): lax.all_to_all(halves, BOTH, 0, 0, axis_index_groups=chip_groups(), tiled...]
  transfers between devices with their start and end apart: 12 -> 10, of which waited for: 5 -> 5; matrix products, arithmetic and copies ran while one was open for 23% -> 15% of each run, Pallas kernels for 0% -> 11%
where the time goes in v2:
time: 116 us; the launch traced here: 115 us
  Pallas kernels  45.1 us (39%)
  starting transfers between devices  33.6 us (29%)
  waiting for transfers between devices  12 us (10%)
  matrix products  10.7 us (9%)
  local copies, waits for them, and re-layouts  9.84 us (8%)
  other arithmetic  3.1 us (3%)
    pallas_call x1, Pallas kernels, main_kernel(): pl.pallas_call(main_body, grid_spec=pltpu.PrefetchScalarGridSpec(num_scal...  31.9 us
    all_to_all x1, starting transfers between devices, shards(): lax.all_to_all(halves, BOTH, 0, 0, axis_index_groups=chip_groups(), tiled...  13.4 us
    pallas_call x1, Pallas kernels, tail_kernel(): pl.pallas_call(tail_body, grid=(8,), in_specs=[tokens_of(model), tokens_o...  12.4 us
    ppermute x4, starting transfers between devices, neighbours(): return (lax.ppermute(last, axis, up), lax.ppermute(first, axis, down))  12 us
    dot_general x1, matrix products, dot_nn(): lax.dot_general(a, b, (((1,), (0,)), ((), ())), preferred_element_type=F32)  6.37 us
    unnamed x22, local copies, waits for them, and re-layouts  6.02 us
    all_to_all x1, waiting for transfers between devices, shards(): lax.all_to_all(halves, BOTH, 0, 0, axis_index_groups=chip_groups(), tiled...  5.85 us
    ppermute x2, starting transfers between devices, side_columns(): lax.ppermute(column(-1), 'lon', up)  5.28 us
  transfers between devices with their start and end apart: 10, of which 5 were waited for; matrix products, arithmetic and copies ran while one was open for 15% of the time, Pallas kernels for 11%

profile of v2, /device:TPU:1, one launch (start us, length us, event | category | flops | bytes accessed | tf_op | source)
XLA Modules:
  0.0 115.3 jit_solution(7124821257273812054)
XLA Ops:
  0.6 0.9 fusion.3
  1.5 1.3 %collective-permute-start.1 = (bf16[1,64,512]{2,1,0:T(8,128)(2,1)S(1)}, bf16[1,64,512]{2,1,0:T(8,128)(2,1)S(1)}, u32[]{:S(2)}, u32[]{:S(2)}) collective-permute-start(bf16[1,64,512]{2,1,0:T(8,128)(2,1)S(1)} %get-tuple-element.32), channel_id=1, source_target_pairs={{16,0},{32,16},{48,32},{64,48},{80,64},{96,80},{112,96},{17,1},{33... | collective-permute-start | bytes 196616 | tf_op jit(solution)/shard_map/ppermute | solution.py:331
  2.8 4.7 %collective-permute-start = (bf16[1,64,512]{2,1,0:T(8,128)(2,1)S(1)}, bf16[1,64,512]{2,1,0:T(8,128)(2,1)S(1)}, u32[]{:S(2)}, u32[]{:S(2)}) collective-permute-start(bf16[1,64,512]{2,1,0:T(8,128)(2,1)S(1)} %get-tuple-element.33), channel_id=1, source_target_pairs={{0,16},{16,32},{32,48},{48,64},{64,80},{80,96},{96,112},{1,17},{17... | collective-permute-start | bytes 196616 | tf_op jit(solution)/shard_map/ppermute | solution.py:331
  7.5 6.4 %convolution_convert_fusion.1.h_top = bf16[2048,1024]{1,0:T(8,128)(2,1)} fusion(bf16[2048,512]{1,0:T(8,128)(2,1)} %bitcast.46, bf16[1024,1024]{1,0:T(8,128)(2,1)} %w_hbm.1), kind=kOutput, calls=%fused_computation.1 | convolution fusion | flops 2149580800 | bytes 7340032 | tf_op jit(solution)/shard_map/dot_general | solution.py:14
  13.9 0.9 fusion.2
  14.9 4.3 %collective-permute-start.2 = (bf16[10,512]{1,0:T(8,128)(2,1)S(1)}, bf16[10,512]{1,0:T(8,128)(2,1)S(1)}, u32[]{:S(2)}, u32[]{:S(2)}) collective-permute-start(bf16[10,512]{1,0:T(8,128)(2,1)S(1)} %pad_maximum_fusion.2), channel_id=1, source_target_pairs={{0,1},{1,2},{2,3},{3,4},{4,5},{5,6},{6,7},{7,8},{8,9},{9,10},{10,1... | collective-permute-start | bytes 30728 | tf_op jit(solution)/shard_map/ppermute | solution.py:339
  19.5 4.4 %convolution_convert_fusion.a_top = bf16[2048,1024]{1,0:T(8,128)(2,1)} fusion(bf16[2048,512]{1,0:T(8,128)(2,1)S(1)} %bitcast.58, bf16[1024,512]{1,0:T(8,128)(2,1)S(1)} %copy-done.2), kind=kOutput, calls=%fused_computation | convolution fusion | flops 2149580800 | bytes 7340032 | tf_op jit(solution)/shard_map/dot_general | solution.py:18
  24.7 31.9 %main.1 = (bf16[2048,1024]{1,0:T(8,128)(2,1)}, bf16[2048,512]{1,0:T(8,128)(2,1)}, bf16[4,4,4,96,128]{4,3,2,1,0:T(8,128)(2,1)}, bf16[4,4,4,96,128]{4,3,2,1,0:T(8,128)(2,1)}) custom-call(s32[1]{0:T(128)} %bitcast.1.core, bf16[8,64,512]{2,1,0:T(8,128)(2,1)} %lat.1, bf16[1,64,512]{2,1,0:T(8,128)(2,1)} %copy-done.5, bf16[1,64,512]{2,1,0:T(8,128)(2,1)} %copy-done.4, ...), custom_call_target="tpu_custom_call" | custom-call | flops 19327352832 | bytes 37748736 | tf_op jit(solution)/shard_map/main/pallas_call | solution.py:162
  56.6 2.6 %collective-permute-start.6 = (bf16[4,4,4,96,128]{4,3,2,1,0:T(8,128)(2,1)}, bf16[4,4,4,96,128]{4,3,2,1,0:T(8,128)(2,1)S(1)}, u32[]{:S(2)}, u32[]{:S(2)}) collective-permute-start(bf16[4,4,4,96,128]{4,3,2,1,0:T(8,128)(2,1)} %get-tuple-element.18), channel_id=1, source_target_pairs={{0,1},{1,0},{2,3},{3,2},{4,5},{5,4},{6,7},{7,6},{8,9},{9,8},{10,11... | collective-permute-start | bytes 4718600 | tf_op jit(solution)/shard_map/ppermute | solution.py:356
  59.2 1.0 slice_bitcast_fusion
  60.2 1.5 %collective-permute-start.5 = (bf16[1,128,512]{2,1,0:T(8,128)(2,1)S(1)}, bf16[1,128,512]{2,1,0:T(8,128)(2,1)S(1)}, u32[]{:S(2)}, u32[]{:S(2)}) collective-permute-start(bf16[1,128,512]{2,1,0:T(8,128)(2,1)S(1)} %get-tuple-element.28), channel_id=1, source_target_pairs={{16,0},{32,16},{48,32},{64,48},{80,64},{96,80},{112,96},{17,1},{33... | collective-permute-start | bytes 393224 | tf_op jit(solution)/shard_map/ppermute | solution.py:331
  61.7 1.0 fusion.1
  62.8 4.5 %collective-permute-start.4 = (bf16[1,128,512]{2,1,0:T(8,128)(2,1)S(1)}, bf16[1,128,512]{2,1,0:T(8,128)(2,1)S(1)}, u32[]{:S(2)}, u32[]{:S(2)}) collective-permute-start(bf16[1,128,512]{2,1,0:T(8,128)(2,1)S(1)} %get-tuple-element.29), channel_id=1, source_target_pairs={{0,16},{16,32},{32,48},{48,64},{64,80},{80,96},{96,112},{1,17},{17... | collective-permute-start | bytes 393224 | tf_op jit(solution)/shard_map/ppermute | solution.py:331
  67.3 0.9 collective-permute-done.5.after
  68.1 3.1 %collective-permute-done.4.before = bf16[1,128,512]{2,1,0:T(8,128)(2,1)S(1)} collective-permute-done((bf16[1,128,512]{2,1,0:T(8,128)(2,1)S(1)}, bf16[1,128,512]{2,1,0:T(8,128)(2,1)S(1)}, u32[]{:S(2)}, u32[]{:S(2)}) %collective-permute-start.4) | collective-permute-done | bytes 131104 | tf_op jit(solution)/shard_map/ppermute | solution.py:331
  71.3 1.0 collective-permute-start.7
  72.4 3.0 %add_convert_fusion = bf16[4,4,4,96,128]{4,3,2,1,0:T(8,128)(2,1)} fusion(bf16[4,4,4,96,128]{4,3,2,1,0:T(8,128)(2,1)S(1)} %collective-permute-done.6, bf16[4,4,4,96,128]{4,3,2,1,0:T(8,128)(2,1)} %get-tuple-element.17), kind=kLoop, calls=%fused_computation.2 | loop fusion | flops 3145728 | bytes 4718592 | tf_op jit(solution)/shard_map/convert_element_type | solution.py:379
  75.5 2.0 %collective-permute-done.8.right = bf16[18,512]{1,0:T(8,128)(2,1)S(1)} collective-permute-done((bf16[18,512]{1,0:T(8,128)(2,1)S(1)}, bf16[18,512]{1,0:T(8,128)(2,1)S(1)}, u32[]{:S(2)}, u32[]{:S(2)}) %collective-permute-start.8) | collective-permute-done | bytes 18464 | tf_op jit(solution)/shard_map/ppermute | solution.py:339
  77.4 13.4 %all-to-all-start = ((bf16[64,96,128]{2,1,0:T(8,128)(2,1)}), bf16[64,96,128]{2,1,0:T(8,128)(2,1)S(1)}, u32[]{:S(2)}, u32[]{:S(2)}) async-start(bf16[64,96,128]{2,1,0:T(8,128)(2,1)} %bitcast.49), calls=%async_computation | async-start | bytes 3145728 | tf_op jit(solution)/shard_map/all_to_all | solution.py:381
  90.8 1.6 %copy-done = bf16[2048,512]{1,0:T(8,128)(2,1)S(1)} copy-done((bf16[2048,512]{1,0:T(8,128)(2,1)S(1)}, bf16[2048,512]{1,0:T(8,128)(2,1)}, u32[]{:S(2)}) %copy-start) | copy-done | bytes 2097176
  92.4 1.6 %copy-done.1 = bf16[16,128,512]{2,1,0:T(8,128)(2,1)S(1)} copy-done((bf16[16,128,512]{2,1,0:T(8,128)(2,1)S(1)}, bf16[16,128,512]{2,1,0:T(8,128)(2,1)}, u32[]{:S(2)}) %copy-start.1) | copy-done | bytes 2097176
  94.0 2.2 %copy-done.3 = bf16[2048,1024]{1,0:T(8,128)(2,1)S(1)} copy-done((bf16[2048,1024]{1,0:T(8,128)(2,1)S(1)}, bf16[2048,1024]{1,0:T(8,128)(2,1)}, u32[]{:S(2)}) %copy-start.3) | copy-done | bytes 4194328
  96.2 12.4 %tail.1 = (bf16[2048,512]{1,0:T(8,128)(2,1)}, f32[512,512]{1,0:T(8,128)}) custom-call(bf16[2048,512]{1,0:T(8,128)(2,1)S(1)} %bitcast.48, bf16[2048,1024]{1,0:T(8,128)(2,1)S(1)} %copy-done.3, bf16[1024,512]{1,0:T(8,128)(2,1)S(1)} %copy-done.2, bf16[16,128,512]{2,1,0:T(8,128)(2,1)S(1)} %bitcast.45, bf16[1,128,512]{2,1,0:T(8,128)(2,1)S(1)} %collective-permute-done.4.before, ...), custom_call_target="tpu_custom_call" | custom-call | flops 7516192768 | bytes 23068672 | tf_op jit(solution)/shard_map/tail/pallas_call | solution.py:270
  108.6 5.8 %all-to-all-done.parts = bf16[64,96,128]{2,1,0:T(8,128)(2,1)S(1)} async-done(((bf16[64,96,128]{2,1,0:T(8,128)(2,1)}), bf16[64,96,128]{2,1,0:T(8,128)(2,1)S(1)}, u32[]{:S(2)}, u32[]{:S(2)}) %all-to-all-start) | async-done | bytes 1572896 | tf_op jit(solution)/shard_map/all_to_all | solution.py:381
  (36 shorter events, 2.2 us)
Async XLA Ops:
  1.5 13.3 %collective-permute-start.1 = (bf16[1,64,512]{2,1,0:T(8,128)(2,1)S(1)}, bf16[1,64,512]{2,1,0:T(8,128)(2,1)S(1)}, u32[]{:S(2)}, u32[]{:S(2)}) collective-permute-start(bf16[1,64,512]{2,1,0:T(8,128)(2,1)S(1)} %get-tuple-element.32), channel_id=1, source_target_pairs={{16,0},{32,16},{48,32},{64,48},{80,64},{96,80},{112,96},{17,1},{33... | collective-permute-start | bytes 196616 | tf_op jit(solution)/shard_map/ppermute | solution.py:331
  2.8 12.0 %collective-permute-start = (bf16[1,64,512]{2,1,0:T(8,128)(2,1)S(1)}, bf16[1,64,512]{2,1,0:T(8,128)(2,1)S(1)}, u32[]{:S(2)}, u32[]{:S(2)}) collective-permute-start(bf16[1,64,512]{2,1,0:T(8,128)(2,1)S(1)} %get-tuple-element.33), channel_id=1, source_target_pairs={{0,16},{16,32},{32,48},{48,64},{64,80},{80,96},{96,112},{1,17},{17... | collective-permute-start | bytes 196616 | tf_op jit(solution)/shard_map/ppermute | solution.py:331
  7.5 12.0 %copy-start.2 = (bf16[1024,512]{1,0:T(8,128)(2,1)S(1)}, bf16[1024,512]{1,0:T(8,128)(2,1)}, u32[]{:S(2)}) copy-start(bf16[1024,512]{1,0:T(8,128)(2,1)} %w_out.1) | copy-start | bytes 3145732
  7.5 12.0 %copy-start.6 = (bf16[16,128,512]{2,1,0:T(8,128)(2,1)S(1)}, bf16[16,128,512]{2,1,0:T(8,128)(2,1)}, u32[]{:S(2)}) copy-start(bf16[16,128,512]{2,1,0:T(8,128)(2,1)} %param.11) | copy-start | bytes 6291460
  14.8 9.0 %copy-start.4 = (bf16[1,64,512]{2,1,0:T(8,128)(2,1)}, bf16[1,64,512]{2,1,0:T(8,128)(2,1)S(1)}, u32[]{:S(2)}) copy-start(bf16[1,64,512]{2,1,0:T(8,128)(2,1)S(1)} %collective-permute-done.1.after) | copy-start | bytes 196612
  14.8 9.0 %copy-start.5 = (bf16[1,64,512]{2,1,0:T(8,128)(2,1)}, bf16[1,64,512]{2,1,0:T(8,128)(2,1)S(1)}, u32[]{:S(2)}) copy-start(bf16[1,64,512]{2,1,0:T(8,128)(2,1)S(1)} %collective-permute-done.before) | copy-start | bytes 196612
  14.9 8.9 %collective-permute-start.2 = (bf16[10,512]{1,0:T(8,128)(2,1)S(1)}, bf16[10,512]{1,0:T(8,128)(2,1)S(1)}, u32[]{:S(2)}, u32[]{:S(2)}) collective-permute-start(bf16[10,512]{1,0:T(8,128)(2,1)S(1)} %pad_maximum_fusion.2), channel_id=1, source_target_pairs={{0,1},{1,2},{2,3},{3,4},{4,5},{5,6},{6,7},{7,8},{8,9},{9,10},{10,1... | collective-permute-start | bytes 30728 | tf_op jit(solution)/shard_map/ppermute | solution.py:339
  19.2 4.9 %collective-permute-start.3 = (bf16[10,512]{1,0:T(8,128)(2,1)S(1)}, bf16[10,512]{1,0:T(8,128)(2,1)S(1)}, u32[]{:S(2)}, u32[]{:S(2)}) collective-permute-start(bf16[10,512]{1,0:T(8,128)(2,1)S(1)} %pad_maximum_fusion.3), channel_id=1, source_target_pairs={{1,0},{2,1},{3,2},{4,3},{5,4},{6,5},{7,6},{8,7},{9,8},{10,9},{11,1... | collective-permute-start | bytes 30728 | tf_op jit(solution)/shard_map/ppermute | solution.py:339
  23.8 0.6 copy-start.7
  24.1 0.6 copy-start.8
  56.6 15.8 %collective-permute-start.6 = (bf16[4,4,4,96,128]{4,3,2,1,0:T(8,128)(2,1)}, bf16[4,4,4,96,128]{4,3,2,1,0:T(8,128)(2,1)S(1)}, u32[]{:S(2)}, u32[]{:S(2)}) collective-permute-start(bf16[4,4,4,96,128]{4,3,2,1,0:T(8,128)(2,1)} %get-tuple-element.18), channel_id=1, source_target_pairs={{0,1},{1,0},{2,3},{3,2},{4,5},{5,4},{6,7},{7,6},{8,9},{9,8},{10,11... | collective-permute-start | bytes 4718600 | tf_op jit(solution)/shard_map/ppermute | solution.py:356
  60.2 8.0 %collective-permute-start.5 = (bf16[1,128,512]{2,1,0:T(8,128)(2,1)S(1)}, bf16[1,128,512]{2,1,0:T(8,128)(2,1)S(1)}, u32[]{:S(2)}, u32[]{:S(2)}) collective-permute-start(bf16[1,128,512]{2,1,0:T(8,128)(2,1)S(1)} %get-tuple-element.28), channel_id=1, source_target_pairs={{16,0},{32,16},{48,32},{64,48},{80,64},{96,80},{112,96},{17,1},{33... | collective-permute-start | bytes 393224 | tf_op jit(solution)/shard_map/ppermute | solution.py:331
  62.8 8.5 %collective-permute-start.4 = (bf16[1,128,512]{2,1,0:T(8,128)(2,1)S(1)}, bf16[1,128,512]{2,1,0:T(8,128)(2,1)S(1)}, u32[]{:S(2)}, u32[]{:S(2)}) collective-permute-start(bf16[1,128,512]{2,1,0:T(8,128)(2,1)S(1)} %get-tuple-element.29), channel_id=1, source_target_pairs={{0,16},{16,32},{32,48},{48,64},{64,80},{80,96},{96,112},{1,17},{17... | collective-permute-start | bytes 393224 | tf_op jit(solution)/shard_map/ppermute | solution.py:331
  71.3 4.2 %collective-permute-start.7 = (bf16[18,512]{1,0:T(8,128)(2,1)S(1)}, bf16[18,512]{1,0:T(8,128)(2,1)S(1)}, u32[]{:S(2)}, u32[]{:S(2)}) collective-permute-start(bf16[18,512]{1,0:T(8,128)(2,1)S(1)} %pad_maximum_fusion), channel_id=1, source_target_pairs={{0,1},{1,2},{2,3},{3,4},{4,5},{5,6},{6,7},{7,8},{8,9},{9,10},{10,1... | collective-permute-start | bytes 55304 | tf_op jit(solution)/shard_map/ppermute | solution.py:339
  72.3 5.1 %collective-permute-start.8 = (bf16[18,512]{1,0:T(8,128)(2,1)S(1)}, bf16[18,512]{1,0:T(8,128)(2,1)S(1)}, u32[]{:S(2)}, u32[]{:S(2)}) collective-permute-start(bf16[18,512]{1,0:T(8,128)(2,1)S(1)} %pad_maximum_fusion.1), channel_id=1, source_target_pairs={{1,0},{2,1},{3,2},{4,3},{5,4},{6,5},{7,6},{8,7},{9,8},{10,9},{11,1... | collective-permute-start | bytes 55304 | tf_op jit(solution)/shard_map/ppermute | solution.py:339
  77.4 37.0 %all-to-all-start = ((bf16[64,96,128]{2,1,0:T(8,128)(2,1)}), bf16[64,96,128]{2,1,0:T(8,128)(2,1)S(1)}, u32[]{:S(2)}, u32[]{:S(2)}) async-start(bf16[64,96,128]{2,1,0:T(8,128)(2,1)} %bitcast.49), calls=%async_computation | async-start | bytes 3145728 | tf_op jit(solution)/shard_map/all_to_all | solution.py:381
  90.8 1.6 %copy-start = (bf16[2048,512]{1,0:T(8,128)(2,1)S(1)}, bf16[2048,512]{1,0:T(8,128)(2,1)}, u32[]{:S(2)}) copy-start(bf16[2048,512]{1,0:T(8,128)(2,1)} %get-tuple-element.16) | copy-start | bytes 6291460
  92.4 1.6 %copy-start.1 = (bf16[16,128,512]{2,1,0:T(8,128)(2,1)S(1)}, bf16[16,128,512]{2,1,0:T(8,128)(2,1)}, u32[]{:S(2)}) copy-start(bf16[16,128,512]{2,1,0:T(8,128)(2,1)} %param.6) | copy-start | bytes 6291460
  94.0 2.2 %copy-start.3 = (bf16[2048,1024]{1,0:T(8,128)(2,1)S(1)}, bf16[2048,1024]{1,0:T(8,128)(2,1)}, u32[]{:S(2)}) copy-start(bf16[2048,1024]{1,0:T(8,128)(2,1)} %get-tuple-element.15.act) | copy-start | bytes 12582916

commit v3 on v2

--- a/solution.py
+++ b/solution.py
@@ -35,18 +35,20 @@
 
 
 def main_body(
-    core, lat, before, after, left, right, w_a, w_b, h_top, a_top, tokens_hbm, cot_hbm, w_hbm,
+    core, lat, before, after, left, right, w_a, w_b, tokens_hbm, cot_hbm, w_in_hbm, w_out_hbm,
     act_out, up_cot, keep, send,
-    shifts, tokens, cot, w_low, up, act, pre, turned, sems,
+    shifts, tokens, cot, w_in, w_out, up, act, pre, turned, sems,
 ):
     step = pl.program_id(0)
     rows, cols, width = lat.shape
-    model, hidden = w_low.shape
-    block = h_top.shape[0]
+    hidden, model = w_out.shape
+    half_model = model // 2
+    block = act_out.shape[0]
     copies = [
-        pltpu.make_async_copy(w_hbm.at[pl.ds(model, model)], w_low, sems.at[0]),
-        pltpu.make_async_copy(tokens_hbm, tokens, sems.at[1]),
-        pltpu.make_async_copy(cot_hbm, cot, sems.at[2]),
+        pltpu.make_async_copy(source, target, sems.at[i])
+        for i, (source, target) in enumerate(
+            ((w_in_hbm, w_in), (w_out_hbm, w_out), (tokens_hbm, tokens), (cot_hbm, cot))
+        )
     ]
 
     @pl.when(step == 0)
@@ -84,11 +86,7 @@
         for m in range(rows):
             pair = jnp.concatenate([z[m * cols : (m + 1) * cols] for z in planes], axis=0)
             value = dot_nn(spread, pair).astype(BF16)
-            at = pl.ds(pl.multiple_of((2 * m + parity) * size, size), size)
-            for side in range(2):
-                @pl.when(half == side)
-                def _():
-                    up[at, side * (model // 2) : (side + 1) * (model // 2)] = value
+            up[half, pl.ds(pl.multiple_of((2 * m + parity) * size, size), size)] = value
 
     @pl.when(step == 4)
     def _():
@@ -100,17 +98,20 @@
         at = pl.ds(pl.multiple_of((step - 4) * block, block), block)
         for n in range(0, hidden, 256):
             span = slice(n, n + 256)
-            h = h_top[:, span].astype(F32) + dot_nn(up[at, :], w_low[:, span])
+            h = dot_nn(tokens[at, :], w_in[:model, span])
+            h += dot_nn(up[0, at], w_in[model : model + half_model, span])
+            h += dot_nn(up[1, at], w_in[model + half_model :, span])
             g = 0.5 * jnp.tanh(0.5 * h) + 0.5
             y = h * g
             wide = y.astype(BF16)
             act[at, span] = wide
             act_out[:, span] = wide
-            a = a_top[:, span].astype(F32)
+            a = dot_nt(cot[at, :], w_out[span, :])
             pre[at, span] = (a * (g + y * (1.0 - g))).astype(BF16)
-        up_cot[...] = dot_nt(pre[at, :], w_low[...]).astype(BF16)
+        up_cot[...] = dot_nt(pre[at, :], w_in[model:, :]).astype(BF16)
         turned[0:model, at] = tokens[at, :].T
-        turned[model : 2 * model, at] = up[at, :].T
+        turned[model : model + half_model, at] = up[0, at].T
+        turned[model + half_model : 2 * model, at] = up[1, at].T
         turned[2 * model :, at] = cot[at, :].T
 
     for j in range(4):
@@ -148,11 +149,12 @@
                     ).astype(BF16)
 
 
-def main_kernel(core, lat, before, after, left, right, weight, h_top, a_top, tokens, cot, w_in):
+def main_kernel(core, lat, before, after, left, right, weight, tokens, cot, w_in, w_out):
     rows, cols, width = lat.shape
     model = weight.shape[0] // 16
     half = model // 2
-    count, hidden = h_top.shape
+    count = tokens.shape[0]
+    hidden = w_out.shape[0]
     block = count // 4
     clamp = lambda i, low: jnp.clip(i - low, 0, 3)
     whole = lambda *shape: pl.BlockSpec(shape, lambda i, c: (0,) * len(shape))
@@ -172,8 +174,7 @@
                 whole(rows + 2, width),
                 pl.BlockSpec((1, 4, half, width), lambda i, c: kernel_row(i, 1)),
                 pl.BlockSpec((1, 4, half, width), lambda i, c: kernel_row(i, 3)),
-                tokens_of(hidden),
-                tokens_of(hidden),
+                pl.BlockSpec(memory_space=pl.ANY),
                 pl.BlockSpec(memory_space=pl.ANY),
                 pl.BlockSpec(memory_space=pl.ANY),
                 pl.BlockSpec(memory_space=pl.ANY),
@@ -183,12 +184,13 @@
                 pltpu.VMEM((3, rows + 2, cols, width), BF16),
                 pltpu.VMEM((count, model), BF16),
                 pltpu.VMEM((count, model), BF16),
-                pltpu.VMEM((model, hidden), BF16),
-                pltpu.VMEM((count, model), BF16),
+                pltpu.VMEM((2 * model, hidden), BF16),
+                pltpu.VMEM((hidden, model), BF16),
+                pltpu.VMEM((2, count, half), BF16),
                 pltpu.VMEM((count, hidden), BF16),
                 pltpu.VMEM((count, hidden), BF16),
                 pltpu.VMEM((3 * model, count), BF16),
-                pltpu.SemaphoreType.DMA((3,)),
+                pltpu.SemaphoreType.DMA((4,)),
             ],
         ),
         out_shape=[
@@ -202,7 +204,7 @@
         name="main",
     )(
         core, lat, before, after, left, right, *[weight.reshape(4, 4, model, width)] * 2,
-        h_top, a_top, tokens, cot, w_in,
+        tokens, cot, w_in, w_out,
     )
 
 
@@ -291,7 +293,7 @@
             pltpu.VMEM((2, fine_rows // 2 + 1, fine_cols // 2, 4 * model), BF16),
             pltpu.SemaphoreType.DMA((1,)),
         ],
-        compiler_params=pltpu.CompilerParams(vmem_limit_bytes=40 << 20),
+        compiler_params=pltpu.CompilerParams(vmem_limit_bytes=58 << 20),
         cost_estimate=cost(7 << 30, 22 << 20),
         name="tail",
     )(tokens, act, w_out, cot, before, after, left, right, weight.reshape(4, 4 * model, width))
@@ -365,11 +367,9 @@
 
     before, after = neighbours(latents, "lat", 0, False)
     left, right = side_columns(latents, before, after)
-    a_top = dot_nt(cot, uniting_out).astype(BF16)
-    h_top = dot_nn(tokens, uniting_in[:model]).astype(BF16)
     act, up_cot, keep, send = main_kernel(
         core, latents, before, after, left, right, upsample_weight,
-        h_top, a_top, tokens, cot, uniting_in,
+        tokens, cot, uniting_in, uniting_out,
     )
 
     up_cot = up_cot.reshape(fine_tokens.shape)

time: 116 us -> 107 us (0.922)
  matrix products: 10.7 us -> 0 us
  waiting for transfers between devices: 12 us -> 22.4 us
  local copies, waits for them, and re-layouts: 9.84 us -> 4.48 us
  starting transfers between devices: 33.6 us -> 30.6 us
    dot_general x2 -> x0, matrix products: 10.7 us -> none  [the longest x1 6.37 us: dot_nn(): lax.dot_general(a, b, (((1,), (0,)), ((), ())), preferred_element_type=F32)]
    unnamed x22 -> x20, local copies, waits for them, and re-layouts: 6.02 us -> 0.65 us
    ppermute x2, starting transfers between devices: 5.28 us -> 9.79 us  [side_columns(): lax.ppermute(column(-1), 'lon', up)]
    all_to_all x1, waiting for transfers between devices: 5.85 us -> 9.43 us  [shards(): lax.all_to_all(halves, BOTH, 0, 0, axis_index_groups=chip_groups(), tiled...]
    ppermute x2, waiting for transfers between devices: 2.22 us -> 5.56 us  [side_columns(): lax.ppermute(column(0), 'lon', down)]
    all_to_all x1, starting transfers between devices: 13.4 us -> 10.2 us  [shards(): lax.all_to_all(halves, BOTH, 0, 0, axis_index_groups=chip_groups(), tiled...]
    ppermute x4, waiting for transfers between devices: 3.97 us -> 6.6 us  [neighbours(): return (lax.ppermute(last, axis, up), lax.ppermute(first, axis, down))]
    pallas_call x1, Pallas kernels: 31.9 us -> 29.3 us  [main_kernel(): pl.pallas_call(main_body, grid_spec=pltpu.PrefetchScalarGridSpec(num_scal...]
  transfers between devices with their start and end apart: 10 -> 10, of which waited for: 5 -> 6; matrix products, arithmetic and copies ran while one was open for 15% -> 6% of each run, Pallas kernels for 11% -> 14%
where the time goes in v3:
time: 107 us; the launch traced here: 106 us
  Pallas kernels  44.6 us (42%)
  starting transfers between devices  30.6 us (29%)
  waiting for transfers between devices  22.4 us (21%)
  local copies, waits for them, and re-layouts  4.48 us (4%)
  other arithmetic  3.09 us (3%)
    pallas_call x1, Pallas kernels, main_kernel(): pl.pallas_call(main_body, grid_spec=pltpu.PrefetchScalarGridSpec(num_scal...  29.3 us
    pallas_call x1, Pallas kernels, tail_kernel(): pl.pallas_call(tail_body, grid=(8,), in_specs=[tokens_of(model), tokens_o...  14.4 us
    ppermute x4, starting transfers between devices, neighbours(): return (lax.ppermute(last, axis, up), lax.ppermute(first, axis, down))  10.2 us
    all_to_all x1, starting transfers between devices, shards(): lax.all_to_all(halves, BOTH, 0, 0, axis_index_groups=chip_groups(), tiled...  10.2 us
    ppermute x2, starting transfers between devices, side_columns(): lax.ppermute(column(-1), 'lon', up)  9.79 us
    all_to_all x1, waiting for transfers between devices, shards(): lax.all_to_all(halves, BOTH, 0, 0, axis_index_groups=chip_groups(), tiled...  9.43 us
    ppermute x4, waiting for transfers between devices, neighbours(): return (lax.ppermute(last, axis, up), lax.ppermute(first, axis, down))  6.6 us
    ppermute x2, waiting for transfers between devices, side_columns(): lax.ppermute(column(0), 'lon', down)  5.56 us
  transfers between devices with their start and end apart: 10, of which 6 were waited for; matrix products, arithmetic and copies ran while one was open for 6% of the time, Pallas kernels for 14%

profile of v3, /device:TPU:1, one launch (start us, length us, event | category | flops | bytes accessed | tf_op | source)
XLA Modules:
  0.0 106.0 jit_solution(18186965624489272628)
XLA Ops:
  0.6 0.9 fusion.2
  1.5 4.0 %collective-permute-start = (bf16[1,64,512]{2,1,0:T(8,128)(2,1)S(1)}, bf16[1,64,512]{2,1,0:T(8,128)(2,1)S(1)}, u32[]{:S(2)}, u32[]{:S(2)}) collective-permute-start(bf16[1,64,512]{2,1,0:T(8,128)(2,1)S(1)} %get-tuple-element.33), channel_id=1, source_target_pairs={{0,16},{16,32},{32,48},{48,64},{64,80},{80,96},{96,112},{1,17},{17... | collective-permute-start | bytes 196616 | tf_op jit(solution)/shard_map/ppermute | solution.py:333
  5.5 1.3 %collective-permute-start.1 = (bf16[1,64,512]{2,1,0:T(8,128)(2,1)S(1)}, bf16[1,64,512]{2,1,0:T(8,128)(2,1)S(1)}, u32[]{:S(2)}, u32[]{:S(2)}) collective-permute-start(bf16[1,64,512]{2,1,0:T(8,128)(2,1)S(1)} %get-tuple-element.32), channel_id=1, source_target_pairs={{16,0},{32,16},{48,32},{64,48},{80,64},{96,80},{112,96},{17,1},{33... | collective-permute-start | bytes 196616 | tf_op jit(solution)/shard_map/ppermute | solution.py:333
  6.8 0.9 fusion.1
  7.8 2.8 %collective-permute-done.1.after = bf16[1,64,512]{2,1,0:T(8,128)(2,1)S(1)} collective-permute-done((bf16[1,64,512]{2,1,0:T(8,128)(2,1)S(1)}, bf16[1,64,512]{2,1,0:T(8,128)(2,1)S(1)}, u32[]{:S(2)}, u32[]{:S(2)}) %collective-permute-start.1) | collective-permute-done | bytes 65568 | tf_op jit(solution)/shard_map/ppermute | solution.py:333
  10.6 4.7 %collective-permute-start.2 = (bf16[10,512]{1,0:T(8,128)(2,1)S(1)}, bf16[10,512]{1,0:T(8,128)(2,1)S(1)}, u32[]{:S(2)}, u32[]{:S(2)}) collective-permute-start(bf16[10,512]{1,0:T(8,128)(2,1)S(1)} %pad_maximum_fusion.2), channel_id=1, source_target_pairs={{0,1},{1,2},{2,3},{3,4},{4,5},{5,6},{6,7},{7,8},{8,9},{9,10},{10,1... | collective-permute-start | bytes 30728 | tf_op jit(solution)/shard_map/ppermute | solution.py:341
  15.4 0.8 collective-permute-done.2.left
  16.2 3.9 %collective-permute-done.3.right = bf16[10,512]{1,0:T(8,128)(2,1)S(1)} collective-permute-done((bf16[10,512]{1,0:T(8,128)(2,1)S(1)}, bf16[10,512]{1,0:T(8,128)(2,1)S(1)}, u32[]{:S(2)}, u32[]{:S(2)}) %collective-permute-start.3) | collective-permute-done | bytes 10272 | tf_op jit(solution)/shard_map/ppermute | solution.py:341
  20.1 0.6 copy-done.7
  20.7 29.3 %main.1 = (bf16[2048,1024]{1,0:T(8,128)(2,1)}, bf16[2048,512]{1,0:T(8,128)(2,1)}, bf16[4,4,4,96,128]{4,3,2,1,0:T(8,128)(2,1)}, bf16[4,4,4,96,128]{4,3,2,1,0:T(8,128)(2,1)}) custom-call(s32[1]{0:T(128)} %bitcast.1.core, bf16[8,64,512]{2,1,0:T(8,128)(2,1)} %lat.1, bf16[1,64,512]{2,1,0:T(8,128)(2,1)} %copy-done, bf16[1,64,512]{2,1,0:T(8,128)(2,1)} %copy-done.1, ...), custom_call_target="tpu_custom_call" | custom-call | flops 19327352832 | bytes 37748736 | tf_op jit(solution)/shard_map/main/pallas_call | solution.py:164
  50.0 0.1 collective-permute-start.6
  50.1 1.0 slice_bitcast_fusion
  51.0 3.6 %collective-permute-start.4 = (bf16[1,128,512]{2,1,0:T(8,128)(2,1)S(1)}, bf16[1,128,512]{2,1,0:T(8,128)(2,1)S(1)}, u32[]{:S(2)}, u32[]{:S(2)}) collective-permute-start(bf16[1,128,512]{2,1,0:T(8,128)(2,1)S(1)} %get-tuple-element.29), channel_id=1, source_target_pairs={{0,16},{16,32},{32,48},{48,64},{64,80},{80,96},{96,112},{1,17},{17... | collective-permute-start | bytes 393224 | tf_op jit(solution)/shard_map/ppermute | solution.py:333
  54.6 1.3 %collective-permute-start.5 = (bf16[1,128,512]{2,1,0:T(8,128)(2,1)S(1)}, bf16[1,128,512]{2,1,0:T(8,128)(2,1)S(1)}, u32[]{:S(2)}, u32[]{:S(2)}) collective-permute-start(bf16[1,128,512]{2,1,0:T(8,128)(2,1)S(1)} %get-tuple-element.28), channel_id=1, source_target_pairs={{16,0},{32,16},{48,32},{64,48},{80,64},{96,80},{112,96},{17,1},{33... | collective-permute-start | bytes 393224 | tf_op jit(solution)/shard_map/ppermute | solution.py:333
  56.0 1.0 fusion
  57.0 3.8 %collective-permute-done.5.after = bf16[1,128,512]{2,1,0:T(8,128)(2,1)S(1)} collective-permute-done((bf16[1,128,512]{2,1,0:T(8,128)(2,1)S(1)}, bf16[1,128,512]{2,1,0:T(8,128)(2,1)S(1)}, u32[]{:S(2)}, u32[]{:S(2)}) %collective-permute-start.5) | collective-permute-done | bytes 131104 | tf_op jit(solution)/shard_map/ppermute | solution.py:333
  60.9 5.1 %collective-permute-start.7 = (bf16[18,512]{1,0:T(8,128)(2,1)S(1)}, bf16[18,512]{1,0:T(8,128)(2,1)S(1)}, u32[]{:S(2)}, u32[]{:S(2)}) collective-permute-start(bf16[18,512]{1,0:T(8,128)(2,1)S(1)} %pad_maximum_fusion), channel_id=1, source_target_pairs={{0,1},{1,2},{2,3},{3,4},{4,5},{5,6},{6,7},{7,8},{8,9},{9,10},{10,1... | collective-permute-start | bytes 55304 | tf_op jit(solution)/shard_map/ppermute | solution.py:341
  66.0 0.3 collective-permute-start.8
  66.3 3.0 %add_convert_fusion = bf16[4,4,4,96,128]{4,3,2,1,0:T(8,128)(2,1)} fusion(bf16[4,4,4,96,128]{4,3,2,1,0:T(8,128)(2,1)S(1)} %collective-permute-done.6, bf16[4,4,4,96,128]{4,3,2,1,0:T(8,128)(2,1)} %get-tuple-element.17), kind=kLoop, calls=%fused_computation | loop fusion | flops 3145728 | bytes 4718592 | tf_op jit(solution)/shard_map/convert_element_type | solution.py:379
  69.3 1.7 %collective-permute-done.8.right = bf16[18,512]{1,0:T(8,128)(2,1)S(1)} collective-permute-done((bf16[18,512]{1,0:T(8,128)(2,1)S(1)}, bf16[18,512]{1,0:T(8,128)(2,1)S(1)}, u32[]{:S(2)}, u32[]{:S(2)}) %collective-permute-start.8) | collective-permute-done | bytes 18464 | tf_op jit(solution)/shard_map/ppermute | solution.py:341
  71.0 10.2 %all-to-all-start = ((bf16[64,96,128]{2,1,0:T(8,128)(2,1)}), bf16[64,96,128]{2,1,0:T(8,128)(2,1)S(1)}, u32[]{:S(2)}, u32[]{:S(2)}) async-start(bf16[64,96,128]{2,1,0:T(8,128)(2,1)} %bitcast.13), calls=%async_computation | async-start | bytes 3145728 | tf_op jit(solution)/shard_map/all_to_all | solution.py:381
  81.3 14.4 %tail.1 = (bf16[2048,512]{1,0:T(8,128)(2,1)}, f32[512,512]{1,0:T(8,128)}) custom-call(bf16[2048,512]{1,0:T(8,128)(2,1)} %bitcast.52, bf16[2048,1024]{1,0:T(8,128)(2,1)} %get-tuple-element.15.act, bf16[1024,512]{1,0:T(8,128)(2,1)} %w_out.1, bf16[16,128,512]{2,1,0:T(8,128)(2,1)} %bitcast.44, bf16[1,128,512]{2,1,0:T(8,128)(2,1)} %copy-done.2, ...), custom_call_target="tpu_custom_call" | custom-call | flops 7516192768 | bytes 23068672 | tf_op jit(solution)/shard_map/tail/pallas_call | solution.py:272
  95.7 9.4 %all-to-all-done.parts = bf16[64,96,128]{2,1,0:T(8,128)(2,1)S(1)} async-done(((bf16[64,96,128]{2,1,0:T(8,128)(2,1)}), bf16[64,96,128]{2,1,0:T(8,128)(2,1)S(1)}, u32[]{:S(2)}, u32[]{:S(2)}) %all-to-all-start) | async-done | bytes 1572896 | tf_op jit(solution)/shard_map/all_to_all | solution.py:381
  105.1 0.9 sum_blocks.1
  (32 shorter events, 0.2 us)
Async XLA Ops:
  1.5 9.1 %collective-permute-start = (bf16[1,64,512]{2,1,0:T(8,128)(2,1)S(1)}, bf16[1,64,512]{2,1,0:T(8,128)(2,1)S(1)}, u32[]{:S(2)}, u32[]{:S(2)}) collective-permute-start(bf16[1,64,512]{2,1,0:T(8,128)(2,1)S(1)} %get-tuple-element.33), channel_id=1, source_target_pairs={{0,16},{16,32},{32,48},{48,64},{64,80},{80,96},{96,112},{1,17},{17... | collective-permute-start | bytes 196616 | tf_op jit(solution)/shard_map/ppermute | solution.py:333
  5.5 5.0 %collective-permute-start.1 = (bf16[1,64,512]{2,1,0:T(8,128)(2,1)S(1)}, bf16[1,64,512]{2,1,0:T(8,128)(2,1)S(1)}, u32[]{:S(2)}, u32[]{:S(2)}) collective-permute-start(bf16[1,64,512]{2,1,0:T(8,128)(2,1)S(1)} %get-tuple-element.32), channel_id=1, source_target_pairs={{16,0},{32,16},{48,32},{64,48},{80,64},{96,80},{112,96},{17,1},{33... | collective-permute-start | bytes 196616 | tf_op jit(solution)/shard_map/ppermute | solution.py:333
  10.6 9.5 %copy-start.1 = (bf16[1,64,512]{2,1,0:T(8,128)(2,1)}, bf16[1,64,512]{2,1,0:T(8,128)(2,1)S(1)}, u32[]{:S(2)}) copy-start(bf16[1,64,512]{2,1,0:T(8,128)(2,1)S(1)} %collective-permute-done.1.after) | copy-start | bytes 196612
  10.6 9.5 %copy-start = (bf16[1,64,512]{2,1,0:T(8,128)(2,1)}, bf16[1,64,512]{2,1,0:T(8,128)(2,1)S(1)}, u32[]{:S(2)}) copy-start(bf16[1,64,512]{2,1,0:T(8,128)(2,1)S(1)} %collective-permute-done.before) | copy-start | bytes 196612
  10.6 5.5 %collective-permute-start.2 = (bf16[10,512]{1,0:T(8,128)(2,1)S(1)}, bf16[10,512]{1,0:T(8,128)(2,1)S(1)}, u32[]{:S(2)}, u32[]{:S(2)}) collective-permute-start(bf16[10,512]{1,0:T(8,128)(2,1)S(1)} %pad_maximum_fusion.2), channel_id=1, source_target_pairs={{0,1},{1,2},{2,3},{3,4},{4,5},{5,6},{6,7},{7,8},{8,9},{9,10},{10,1... | collective-permute-start | bytes 30728 | tf_op jit(solution)/shard_map/ppermute | solution.py:341
  15.3 4.7 %collective-permute-start.3 = (bf16[10,512]{1,0:T(8,128)(2,1)S(1)}, bf16[10,512]{1,0:T(8,128)(2,1)S(1)}, u32[]{:S(2)}, u32[]{:S(2)}) collective-permute-start(bf16[10,512]{1,0:T(8,128)(2,1)S(1)} %pad_maximum_fusion.3), channel_id=1, source_target_pairs={{1,0},{2,1},{3,2},{4,3},{5,4},{6,5},{7,6},{8,7},{9,8},{10,9},{11,1... | collective-permute-start | bytes 30728 | tf_op jit(solution)/shard_map/ppermute | solution.py:341
  16.2 3.9 %copy-start.6 = (bf16[10,512]{1,0:T(8,128)(2,1)}, bf16[10,512]{1,0:T(8,128)(2,1)S(1)}, u32[]{:S(2)}) copy-start(bf16[10,512]{1,0:T(8,128)(2,1)S(1)} %collective-permute-done.2.left) | copy-start | bytes 30724
  20.1 0.6 copy-start.7
  50.0 16.3 %collective-permute-start.6 = (bf16[4,4,4,96,128]{4,3,2,1,0:T(8,128)(2,1)}, bf16[4,4,4,96,128]{4,3,2,1,0:T(8,128)(2,1)S(1)}, u32[]{:S(2)}, u32[]{:S(2)}) collective-permute-start(bf16[4,4,4,96,128]{4,3,2,1,0:T(8,128)(2,1)} %get-tuple-element.18), channel_id=1, source_target_pairs={{0,1},{1,0},{2,3},{3,2},{4,5},{5,4},{6,7},{7,6},{8,9},{9,8},{10,11... | collective-permute-start | bytes 4718600 | tf_op jit(solution)/shard_map/ppermute | solution.py:358
  51.0 9.8 %collective-permute-start.4 = (bf16[1,128,512]{2,1,0:T(8,128)(2,1)S(1)}, bf16[1,128,512]{2,1,0:T(8,128)(2,1)S(1)}, u32[]{:S(2)}, u32[]{:S(2)}) collective-permute-start(bf16[1,128,512]{2,1,0:T(8,128)(2,1)S(1)} %get-tuple-element.29), channel_id=1, source_target_pairs={{0,16},{16,32},{32,48},{48,64},{64,80},{80,96},{96,112},{1,17},{17... | collective-permute-start | bytes 393224 | tf_op jit(solution)/shard_map/ppermute | solution.py:333
  54.6 6.2 %collective-permute-start.5 = (bf16[1,128,512]{2,1,0:T(8,128)(2,1)S(1)}, bf16[1,128,512]{2,1,0:T(8,128)(2,1)S(1)}, u32[]{:S(2)}, u32[]{:S(2)}) collective-permute-start(bf16[1,128,512]{2,1,0:T(8,128)(2,1)S(1)} %get-tuple-element.28), channel_id=1, source_target_pairs={{16,0},{32,16},{48,32},{64,48},{80,64},{96,80},{112,96},{17,1},{33... | collective-permute-start | bytes 393224 | tf_op jit(solution)/shard_map/ppermute | solution.py:333
  60.8 8.5 %copy-start.3 = (bf16[1,128,512]{2,1,0:T(8,128)(2,1)}, bf16[1,128,512]{2,1,0:T(8,128)(2,1)S(1)}, u32[]{:S(2)}) copy-start(bf16[1,128,512]{2,1,0:T(8,128)(2,1)S(1)} %collective-permute-done.5.after) | copy-start | bytes 393220
  60.8 8.5 %copy-start.2 = (bf16[1,128,512]{2,1,0:T(8,128)(2,1)}, bf16[1,128,512]{2,1,0:T(8,128)(2,1)S(1)}, u32[]{:S(2)}) copy-start(bf16[1,128,512]{2,1,0:T(8,128)(2,1)S(1)} %collective-permute-done.4.before) | copy-start | bytes 393220
  60.9 8.4 %collective-permute-start.7 = (bf16[18,512]{1,0:T(8,128)(2,1)S(1)}, bf16[18,512]{1,0:T(8,128)(2,1)S(1)}, u32[]{:S(2)}, u32[]{:S(2)}) collective-permute-start(bf16[18,512]{1,0:T(8,128)(2,1)S(1)} %pad_maximum_fusion), channel_id=1, source_target_pairs={{0,1},{1,2},{2,3},{3,4},{4,5},{5,6},{6,7},{7,8},{8,9},{9,10},{10,1... | collective-permute-start | bytes 55304 | tf_op jit(solution)/shard_map/ppermute | solution.py:341
  66.0 5.0 %collective-permute-start.8 = (bf16[18,512]{1,0:T(8,128)(2,1)S(1)}, bf16[18,512]{1,0:T(8,128)(2,1)S(1)}, u32[]{:S(2)}, u32[]{:S(2)}) collective-permute-start(bf16[18,512]{1,0:T(8,128)(2,1)S(1)} %pad_maximum_fusion.1), channel_id=1, source_target_pairs={{1,0},{2,1},{3,2},{4,3},{5,4},{6,5},{7,6},{8,7},{9,8},{10,9},{11,1... | collective-permute-start | bytes 55304 | tf_op jit(solution)/shard_map/ppermute | solution.py:341
  69.3 11.9 %copy-start.4 = (bf16[18,512]{1,0:T(8,128)(2,1)}, bf16[18,512]{1,0:T(8,128)(2,1)S(1)}, u32[]{:S(2)}) copy-start(bf16[18,512]{1,0:T(8,128)(2,1)S(1)} %collective-permute-done.7.left) | copy-start | bytes 55300
  71.0 10.2 %copy-start.5 = (bf16[18,512]{1,0:T(8,128)(2,1)}, bf16[18,512]{1,0:T(8,128)(2,1)S(1)}, u32[]{:S(2)}) copy-start(bf16[18,512]{1,0:T(8,128)(2,1)S(1)} %collective-permute-done.8.right) | copy-start | bytes 55300
  71.0 34.1 %all-to-all-start = ((bf16[64,96,128]{2,1,0:T(8,128)(2,1)}), bf16[64,96,128]{2,1,0:T(8,128)(2,1)S(1)}, u32[]{:S(2)}, u32[]{:S(2)}) async-start(bf16[64,96,128]{2,1,0:T(8,128)(2,1)} %bitcast.13), calls=%async_computation | async-start | bytes 3145728 | tf_op jit(solution)/shard_map/all_to_all | solution.py:381

commit v4 on v3

--- a/solution.py
+++ b/solution.py
@@ -18,10 +18,6 @@
     return lax.dot_general(a, b, (((1,), (1,)), ((), ())), preferred_element_type=F32)
 
 
-def dot_tn(a, b):
-    return lax.dot_general(a, b, (((0,), (0,)), ((), ())), preferred_element_type=F32)
-
-
 def cost(flops, nbytes):
     return pl.CostEstimate(flops=flops, bytes_accessed=nbytes, transcendentals=0)
 
@@ -36,14 +32,17 @@
 
 def main_body(
     core, lat, before, after, left, right, w_a, w_b, tokens_hbm, cot_hbm, w_in_hbm, w_out_hbm,
-    act_out, up_cot, keep, send,
-    shifts, tokens, cot, w_in, w_out, up, act, pre, turned, sems,
+    act_out, up_cot, up_cot_edge, keep, send,
+    sources, edges, tokens, cot, tokens_edge, cot_edge, w_in, w_out, up, act, pre, pre_edge,
+    turned, sems,
 ):
     step = pl.program_id(0)
     rows, cols, width = lat.shape
     hidden, model = w_out.shape
     half_model = model // 2
     block = act_out.shape[0]
+    count = tokens.shape[0]
+    fine_cols = 2 * cols
     copies = [
         pltpu.make_async_copy(source, target, sems.at[i])
         for i, (source, target) in enumerate(
@@ -55,59 +54,93 @@
     def _():
         for copy in copies:
             copy.start()
-        lefts, rights = left[...].astype(F32), right[...].astype(F32)
+        lefts, rights = left[0:16].astype(F32), right[0:16].astype(F32)
+        edges[...] = jnp.zeros_like(edges)
         place = iota((cols, width), 0)
         for r in range(rows + 2):
-            row = before[0] if r == 0 else after[0] if r == rows + 1 else lat[r - 1]
+            row = before[0:cols] if r == 0 else after[0:cols] if r == rows + 1 else lat[r - 1]
             wide = row.astype(F32)
-            shifts[1, r] = row
-            shifts[0, r] = jnp.where(
+            at = slice(16 + r * cols, 16 + (r + 1) * cols)
+            sources[0, at] = row
+            sources[1, at] = jnp.where(
                 place == 0, lefts[r : r + 1], pltpu.roll(wide, 1, 0)
             ).astype(BF16)
-            shifts[2, r] = jnp.where(
+            sources[2, at] = jnp.where(
                 place == cols - 1, rights[r : r + 1], pltpu.roll(wide, cols - 1, 0)
             ).astype(BF16)
+            sources[3, at] = row
+            edges[0, r : r + 1] = wide[cols - 1 : cols]
+            edges[1, r : r + 1] = wide[0:1]
+        last = 16 + (rows + 2) * cols
+        for i, edge in enumerate((rights, edges[0], edges[1], lefts)):
+            sources[i, 0:16] = edge.astype(BF16)
+            sources[i, last : last + 16] = pltpu.roll(edge, 15, 0).astype(BF16)
+        for ref, lane, part in ((tokens_edge, cols, 16), (cot_edge, cols + fine_cols, 48)):
+            ref[0:fine_cols] = before[lane : lane + fine_cols]
+            ref[fine_cols : 2 * fine_cols] = after[lane : lane + fine_cols]
+            ref[2 * fine_cols : 2 * fine_cols + 32] = left[part : part + 32]
+            ref[2 * fine_cols + 32 :] = right[part : part + 32]
 
     @pl.when(step < 4)
     def _():
         parity, half = step // 2, step % 2
+        size = (rows + 1) * cols
         planes = []
-        for taps in (((1, 0), (3, -1)), ((0, 1), (2, 0))):
-            total = None
-            for weight, start in ((w_a, 1 + parity), (w_b, parity)):
-                for tap, move in taps:
-                    source = shifts[move + 1, pl.ds(start, rows)].reshape(rows * cols, width)
-                    term = dot_nt(source, weight[0, tap])
-                    total = term if total is None else total + term
-            planes.append(total.astype(BF16))
-        size = 2 * cols
-        r, k = iota((size, size), 0), iota((size, size), 1)
+        for q, taps in enumerate((((1, 0), (3, 1)), ((0, 2), (2, 3)))):
+            total_a = total_b = None
+            for tap, i in taps:
+                term_a = dot_nt(sources[i, 16 + cols : 32 + cols + size], w_a[0, tap])
+                term_b = dot_nt(sources[i, 0 : 16 + size], w_b[0, tap])
+                total_a = term_a if total_a is None else total_a + term_a
+                total_b = term_b if total_b is None else total_b + term_b
+            planes.append((total_a[:size] + total_b[16:]).astype(BF16))
+            side = (total_a[size:] + total_b[:16]).astype(BF16)
+            at = count + 2 * fine_cols + (1 - q) * 32 + (1 - parity) * 16
+            up[half, pl.ds(pl.multiple_of(at, 16), 16)] = side
+        r, k = iota((fine_cols, fine_cols), 0), iota((fine_cols, fine_cols), 1)
         spread = (k == (r % 2) * cols + r // 2).astype(F32).astype(BF16)
-        for m in range(rows):
+        for m in range(rows + 1):
             pair = jnp.concatenate([z[m * cols : (m + 1) * cols] for z in planes], axis=0)
             value = dot_nn(spread, pair).astype(BF16)
-            up[half, pl.ds(pl.multiple_of((2 * m + parity) * size, size), size)] = value
+            even = 2 * m * fine_cols if m < rows else count + fine_cols
+            odd = (2 * m - 1) * fine_cols if m > 0 else count
+            at = even + parity * (odd - even)
+            up[half, pl.ds(pl.multiple_of(at, 128), fine_cols)] = value
 
     @pl.when(step == 4)
     def _():
         for copy in copies:
             copy.wait()
 
-    @pl.when((step >= 4) & (step < 8))
-    def _():
-        at = pl.ds(pl.multiple_of((step - 4) * block, block), block)
+    def network(tokens_of, up_of, cot_of, span):
+        h = dot_nn(tokens_of(), w_in[:model, span])
+        h += dot_nn(up_of(0), w_in[model : model + half_model, span])
+        h += dot_nn(up_of(1), w_in[model + half_model :, span])
+        g = 0.5 * jnp.tanh(0.5 * h) + 0.5
+        y = h * g
+        a = dot_nt(cot_of(), w_out[span, :])
+        return y.astype(BF16), (a * (g + y * (1.0 - g))).astype(BF16)
+
+    @pl.when(step == 4)
+    def _():
         for n in range(0, hidden, 256):
             span = slice(n, n + 256)
-            h = dot_nn(tokens[at, :], w_in[:model, span])
-            h += dot_nn(up[0, at], w_in[model : model + half_model, span])
-            h += dot_nn(up[1, at], w_in[model + half_model :, span])
-            g = 0.5 * jnp.tanh(0.5 * h) + 0.5
-            y = h * g
-            wide = y.astype(BF16)
+            _, pre_edge[:, span] = network(
+                lambda: tokens_edge[...], lambda i: up[i, count:], lambda: cot_edge[...], span
+            )
+        up_cot_edge[...] = dot_nt(pre_edge[...], w_in[model:, :]).astype(BF16)
+
+    @pl.when((step > 4) & (step < 9))
+    def _():
+        at = pl.ds(pl.multiple_of((step - 5) * block, block), block)
+        for n in range(0, hidden, 256):
+            span = slice(n, n + 256)
+            wide, grad = network(
+                lambda: tokens[at, :], lambda i: up[i, at], lambda: cot[at, :], span
+            )
             act[at, span] = wide
             act_out[:, span] = wide
-            a = dot_nt(cot[at, :], w_out[span, :])
-            pre[at, span] = (a * (g + y * (1.0 - g))).astype(BF16)
+            pre[at, span] = grad
         up_cot[...] = dot_nt(pre[at, :], w_in[model:, :]).astype(BF16)
         turned[0:model, at] = tokens[at, :].T
         turned[model : model + half_model, at] = up[0, at].T
@@ -116,7 +149,7 @@
 
     for j in range(4):
 
-        @pl.when(step == 8 + j)
+        @pl.when(step == 9 + j)
         def _():
             span = slice(j * 256, (j + 1) * 256)
             mine = core[0]
@@ -156,22 +189,23 @@
     count = tokens.shape[0]
     hidden = w_out.shape[0]
     block = count // 4
+    edge = 4 * cols + 64
     clamp = lambda i, low: jnp.clip(i - low, 0, 3)
     whole = lambda *shape: pl.BlockSpec(shape, lambda i, c: (0,) * len(shape))
     kernel_row = lambda i, top: (top - clamp(i, 0) // 2, 0, clamp(i, 0) % 2, 0)
-    tokens_of = lambda w: pl.BlockSpec((block, w), lambda i, c: (clamp(i, 4), 0))
+    tokens_of = lambda w: pl.BlockSpec((block, w), lambda i, c: (clamp(i, 5), 0))
     blocks = (4, 4, 4, 96, 128)
     return pl.pallas_call(
         main_body,
         grid_spec=pltpu.PrefetchScalarGridSpec(
             num_scalar_prefetch=1,
-            grid=(12,),
+            grid=(13,),
             in_specs=[
                 whole(rows, cols, width),
-                whole(1, cols, width),
-                whole(1, cols, width),
-                whole(rows + 2, width),
-                whole(rows + 2, width),
+                whole(*before.shape),
+                whole(*after.shape),
+                whole(*left.shape),
+                whole(*right.shape),
                 pl.BlockSpec((1, 4, half, width), lambda i, c: kernel_row(i, 1)),
                 pl.BlockSpec((1, 4, half, width), lambda i, c: kernel_row(i, 3)),
                 pl.BlockSpec(memory_space=pl.ANY),
@@ -179,16 +213,26 @@
                 pl.BlockSpec(memory_space=pl.ANY),
                 pl.BlockSpec(memory_space=pl.ANY),
             ],
-            out_specs=[tokens_of(hidden), tokens_of(model), whole(*blocks), whole(*blocks)],
+            out_specs=[
+                tokens_of(hidden),
+                tokens_of(model),
+                whole(edge, model),
+                whole(*blocks),
+                whole(*blocks),
+            ],
             scratch_shapes=[
-                pltpu.VMEM((3, rows + 2, cols, width), BF16),
+                pltpu.VMEM((4, (rows + 2) * cols + 32, width), BF16),
+                pltpu.VMEM((2, 16, width), F32),
                 pltpu.VMEM((count, model), BF16),
                 pltpu.VMEM((count, model), BF16),
+                pltpu.VMEM((edge, model), BF16),
+                pltpu.VMEM((edge, model), BF16),
                 pltpu.VMEM((2 * model, hidden), BF16),
                 pltpu.VMEM((hidden, model), BF16),
-                pltpu.VMEM((2, count, half), BF16),
+                pltpu.VMEM((2, count + edge, half), BF16),
                 pltpu.VMEM((count, hidden), BF16),
                 pltpu.VMEM((count, hidden), BF16),
+                pltpu.VMEM((edge, hidden), BF16),
                 pltpu.VMEM((3 * model, count), BF16),
                 pltpu.SemaphoreType.DMA((4,)),
             ],
@@ -196,11 +240,12 @@
         out_shape=[
             jax.ShapeDtypeStruct((count, hidden), BF16),
             jax.ShapeDtypeStruct((count, model), BF16),
+            jax.ShapeDtypeStruct((edge, model), BF16),
             jax.ShapeDtypeStruct(blocks, BF16),
             jax.ShapeDtypeStruct(blocks, BF16),
         ],
         compiler_params=params(),
-        cost_estimate=cost(18 << 30, 36 << 20),
+        cost_estimate=cost(20 << 30, 36 << 20),
         name="main",
     )(
         core, lat, before, after, left, right, *[weight.reshape(4, 4, model, width)] * 2,
@@ -209,7 +254,7 @@
 
 
 def tail_body(
-    tokens, act, w_out, cot_hbm, before, after, left, right, weight, united, out,
+    tokens, act, w_out, cot_hbm, edge, weight, united, out,
     cot, planes, sem,
 ):
     step = pl.program_id(0)
@@ -231,17 +276,25 @@
         copy.wait()
         r, c = iota((fine_cols, fine_cols), 0), iota((fine_cols, fine_cols), 1)
         pick = (c == 2 * (r % cols) + r // cols).astype(F32).astype(BF16)
-        lefts, rights = left[...].astype(F32), right[...].astype(F32)
+        lefts, rights = [
+            edge[2 * fine_cols + i : 2 * fine_cols + i + 32].astype(F32) for i in (0, 32)
+        ]
         place = iota((cols, model), 0)
         for e in range(fine_rows + 2):
-            row = before[0] if e == 0 else after[0] if e == fine_rows + 1 else cot[e - 1]
+            if e == 0:
+                row = edge[0:fine_cols]
+            elif e == fine_rows + 1:
+                row = edge[fine_cols : 2 * fine_cols]
+            else:
+                row = cot[e - 1]
+            at = e // 2 + 16 * (e % 2)
             found = dot_nn(pick, row)
             even, odd = found[:cols], found[cols:]
             taps = (
-                jnp.where(place == 0, lefts[e : e + 1], pltpu.roll(odd, 1, 0)),
+                jnp.where(place == 0, lefts[at : at + 1], pltpu.roll(odd, 1, 0)),
                 even,
                 odd,
-                jnp.where(place == cols - 1, rights[e : e + 1], pltpu.roll(even, cols - 1, 0)),
+                jnp.where(place == cols - 1, rights[at : at + 1], pltpu.roll(even, cols - 1, 0)),
             )
             for tap in range(4):
                 planes[e % 2, e // 2, :, tap * model : (tap + 1) * model] = taps[tap].astype(BF16)
@@ -261,7 +314,7 @@
             out[...] += term
 
 
-def tail_kernel(tokens, act, w_out, cot, before, after, left, right, weight):
+def tail_kernel(tokens, act, w_out, cot, edge, weight):
     fine_rows, fine_cols, model = cot.shape
     width = weight.shape[1]
     count, hidden = act.shape
@@ -277,10 +330,7 @@
             tokens_of(hidden),
             whole(w_out),
             pl.BlockSpec(memory_space=pl.ANY),
-            whole(before),
-            whole(after),
-            whole(left),
-            whole(right),
+            whole(edge),
             pl.BlockSpec((1, 4 * model, width), lambda i: (jnp.maximum(i - 4, 0), 0, 0)),
         ],
         out_specs=[tokens_of(model), pl.BlockSpec((size, width), lambda i: (0, 0))],
@@ -296,7 +346,7 @@
         compiler_params=pltpu.CompilerParams(vmem_limit_bytes=58 << 20),
         cost_estimate=cost(7 << 30, 22 << 20),
         name="tail",
-    )(tokens, act, w_out, cot, before, after, left, right, weight.reshape(4, 4 * model, width))
+    )(tokens, act, w_out, cot, edge, weight.reshape(4, 4 * model, width))
 
 
 def sum_body(parts, in_grad, out_grad):
@@ -323,22 +373,33 @@
     )(parts)
 
 
-def neighbours(array, axis, dim, wrap):
+def swap(last, first, axis, wrap):
     devices = lax.axis_size(axis)
     up = [(i, (i + 1) % devices) for i in range(devices if wrap else devices - 1)]
     down = [(j, i) for i, j in up]
-    length = array.shape[dim]
-    last = lax.slice_in_dim(array, length - 1, length, axis=dim)
-    first = lax.slice_in_dim(array, 0, 1, axis=dim)
     return lax.ppermute(last, axis, up), lax.ppermute(first, axis, down)
 
 
-def side_columns(array, before, after):
-    devices = lax.axis_size("lon")
-    up = [(i, (i + 1) % devices) for i in range(devices)]
-    down = [(j, i) for i, j in up]
-    column = lambda c: jnp.concatenate([before[:, c], array[:, c], after[:, c]], axis=0)
-    return lax.ppermute(column(-1), "lon", up), lax.ppermute(column(0), "lon", down)
+def halos(latents, tokens, cot):
+    cols, fine_cols = latents.shape[1], tokens.shape[1]
+    row = lambda i: jnp.concatenate([latents[i], tokens[i], cot[i]], axis=0)
+    before, after = swap(row(-1), row(0), "lat", False)
+
+    def column(c):
+        parts = []
+        place = c % cols
+        pad = lambda a: jnp.pad(a, ((0, 16 - a.shape[0]), (0, 0)))
+        ends = [a[place : place + 1] for a in (before, after)]
+        parts.append(pad(jnp.concatenate([ends[0], latents[:, c], ends[1]], axis=0)))
+        for fine, start in ((tokens, cols), (cot, cols + fine_cols)):
+            place = start + c % fine_cols
+            ends = [a[place : place + 1] for a in (before, after)]
+            parts.append(pad(jnp.concatenate([ends[0], fine[1::2, c]], axis=0)))
+            parts.append(pad(jnp.concatenate([fine[0::2, c], ends[1]], axis=0)))
+        return jnp.concatenate(parts, axis=0)
+
+    left, right = swap(column(-1), column(0), "lon", True)
+    return before, after, left, right
 
 
 def chip_groups():
@@ -365,23 +426,18 @@
     tokens = fine_tokens.reshape(count, model)
     cot = cotangent.reshape(count, model)
 
-    before, after = neighbours(latents, "lat", 0, False)
-    left, right = side_columns(latents, before, after)
-    act, up_cot, keep, send = main_kernel(
+    before, after, left, right = halos(latents, fine_tokens, cotangent)
+    act, up_cot, up_cot_edge, keep, send = main_kernel(
         core, latents, before, after, left, right, upsample_weight,
         tokens, cot, uniting_in, uniting_out,
     )
-
-    up_cot = up_cot.reshape(fine_tokens.shape)
-    cot_before, cot_after = neighbours(up_cot, "lat", 0, False)
     other = other_core(send)
-    cot_left, cot_right = side_columns(up_cot, cot_before, cot_after)
     halves = (keep.astype(F32) + other.astype(F32)).astype(BF16).reshape(64, 96, 128)
-    halves, cot_left, cot_right = lax.optimization_barrier((halves, cot_left, cot_right))
-    parts = lax.all_to_all(halves, BOTH, 0, 0, axis_index_groups=chip_groups(), tiled=True)
-
+    parts = lax.all_to_all(
+        halves, BOTH, 0, 0, axis_index_groups=chip_groups(), tiled=True
+    )
     united, latent_grad = tail_kernel(
-        tokens, act, uniting_out, up_cot, cot_before, cot_after, cot_left, cot_right,
+        tokens, act, uniting_out, up_cot.reshape(fine_tokens.shape), up_cot_edge,
         upsample_weight,
     )
     in_grad, out_grad = sum_blocks(parts)

time: 107 us -> 107 us (level)
  starting transfers between devices: 30.6 us -> 22.7 us
  waiting for transfers between devices: 22.4 us -> 26.1 us
  Pallas kernels: 44.6 us -> 46.8 us
  local copies, waits for them, and re-layouts: 4.48 us -> 5.62 us
    ppermute x8 -> x4, starting transfers between devices: 20.3 us -> 9.35 us  [swap(): return (lax.ppermute(last, axis, up), lax.ppermute(first, axis, down))]
    ppermute x1, starting transfers between devices: 0.08 us -> 6.96 us  [other_core(): return lax.ppermute(array, 'lon', [(i, i ^ 1) for i in range(16)])]
    all_to_all x1, starting transfers between devices: 10.2 us -> 6.34 us  [shards(): lax.all_to_all(halves, BOTH, 0, 0, axis_index_groups=chip_groups(), tiled...]
    ppermute x1, waiting for transfers between devices: 0.01 us -> 3.25 us  [other_core(): return lax.ppermute(array, 'lon', [(i, i ^ 1) for i in range(16)])]
    pallas_call x1, Pallas kernels: 29.3 us -> 31.6 us  [main_kernel(): pl.pallas_call(main_body, grid_spec=pltpu.PrefetchScalarGridSpec(num_scal...]
    squeeze x4 -> x5, local copies, waits for them, and re-layouts: 0.03 us -> 2.04 us  [the longest x2 2.02 us: halos(): row = lambda i: jnp.concatenate([latents[i], tokens[i], cot[i]], axis=0)]
    ppermute x8 -> x4, waiting for transfers between devices: 12.9 us -> 14.3 us  [swap(): return (lax.ppermute(last, axis, up), lax.ppermute(first, axis, down))]
    slice x4 -> x5, local copies, waits for them, and re-layouts: 3.8 us -> 2.92 us  [the longest x2 1.99 us: column(): parts.append(pad(jnp.concatenate([fine[0::2, c], ends[1]], axis=0)))]
  transfers between devices with their start and end apart: 10 -> 6, of which waited for: 6 -> 6; matrix products, arithmetic and copies ran while one was open for 6% -> 3% of each run, Pallas kernels for 14% -> 14%
where the time goes in v4:
time: 107 us; the launch traced here: 105 us
  Pallas kernels  46.8 us (44%)
  waiting for transfers between devices  26.1 us (24%)
  starting transfers between devices  22.7 us (21%)
  local copies, waits for them, and re-layouts  5.62 us (5%)
  other arithmetic  3.18 us (3%)
    pallas_call x1, Pallas kernels, main_kernel(): pl.pallas_call(main_body, grid_spec=pltpu.PrefetchScalarGridSpec(num_scal...  31.6 us
    ppermute x4, waiting for transfers between devices, swap(): return (lax.ppermute(last, axis, up), lax.ppermute(first, axis, down))  14.3 us
    pallas_call x1, Pallas kernels, tail_kernel(): pl.pallas_call(tail_body, grid=(8,), in_specs=[tokens_of(model), tokens_o...  14.3 us
    ppermute x4, starting transfers between devices, swap(): return (lax.ppermute(last, axis, up), lax.ppermute(first, axis, down))  9.35 us
    all_to_all x1, waiting for transfers between devices, shards(): lax.all_to_all(halves, BOTH, 0, 0, axis_index_groups=chip_groups(), tiled...  8.47 us
    ppermute x1, starting transfers between devices, other_core(): return lax.ppermute(array, 'lon', [(i, i ^ 1) for i in range(16)])  6.96 us
    all_to_all x1, starting transfers between devices, shards(): lax.all_to_all(halves, BOTH, 0, 0, axis_index_groups=chip_groups(), tiled...  6.34 us
    ppermute x1, waiting for transfers between devices, other_core(): return lax.ppermute(array, 'lon', [(i, i ^ 1) for i in range(16)])  3.25 us
  transfers between devices with their start and end apart: 6, of which 6 were waited for; matrix products, arithmetic and copies ran while one was open for 3% of the time, Pallas kernels for 14%

profile of v4, /device:TPU:1, one launch (start us, length us, event | category | flops | bytes accessed | tf_op | source)
XLA Modules:
  0.0 105.2 jit_solution(14323848298875868443)
XLA Ops:
  0.6 0.9 slice_bitcast_fusion.4
  1.5 1.1 %slice_bitcast_fusion = (bf16[128,512]{1,0:T(8,128)(2,1)S(1)}, bf16[128,512]{1,0:T(8,128)(2,1)S(1)}, bf16[128,512]{1,0:T(8,128)(2,1)S(1)}, bf16[128,512]{1,0:T(8,128)(2,1)S(1)}) fusion(bf16[16,128,512]{2,1,0:T(8,128)(2,1)} %param.11, bf16[16,128,512]{2,1,0:T(8,128)(2,1)} %param.6), kind=kLoop, calls=%fused_computation.3 | loop fusion | bytes 1048576 | tf_op jit(solution)/shard_map/squeeze | solution.py:385
  2.7 1.3 %collective-permute-start.1 = (bf16[320,512]{1,0:T(8,128)(2,1)S(1)}, bf16[320,512]{1,0:T(8,128)(2,1)S(1)}, u32[]{:S(2)}, u32[]{:S(2)}) collective-permute-start(bf16[320,512]{1,0:T(8,128)(2,1)S(1)} %pad_maximum_fusion.1), channel_id=1, source_target_pairs={{16,0},{32,16},{48,32},{64,48},{80,64},{96,80},{112,96},{17,1},{33... | collective-permute-start | bytes 983048 | tf_op jit(solution)/shard_map/ppermute | solution.py:380
  4.0 4.7 %collective-permute-start = (bf16[320,512]{1,0:T(8,128)(2,1)S(1)}, bf16[320,512]{1,0:T(8,128)(2,1)S(1)}, u32[]{:S(2)}, u32[]{:S(2)}) collective-permute-start(bf16[320,512]{1,0:T(8,128)(2,1)S(1)} %pad_maximum_fusion), channel_id=1, source_target_pairs={{0,16},{16,32},{32,48},{48,64},{64,80},{80,96},{96,112},{1,17},{17... | collective-permute-start | bytes 983048 | tf_op jit(solution)/shard_map/ppermute | solution.py:380
  8.7 0.9 fusion.36
  9.6 1.0 fusion.35
  10.6 1.0 fusion.34
  11.7 2.1 %collective-permute-done.1.after = bf16[320,512]{1,0:T(8,128)(2,1)S(1)} collective-permute-done((bf16[320,512]{1,0:T(8,128)(2,1)S(1)}, bf16[320,512]{1,0:T(8,128)(2,1)S(1)}, u32[]{:S(2)}, u32[]{:S(2)}) %collective-permute-start.1) | collective-permute-done | bytes 327712 | tf_op jit(solution)/shard_map/ppermute | solution.py:380
  13.8 8.2 %collective-permute-done.before = bf16[320,512]{1,0:T(8,128)(2,1)S(1)} collective-permute-done((bf16[320,512]{1,0:T(8,128)(2,1)S(1)}, bf16[320,512]{1,0:T(8,128)(2,1)S(1)}, u32[]{:S(2)}, u32[]{:S(2)}) %collective-permute-start) | collective-permute-done | bytes 327712 | tf_op jit(solution)/shard_map/ppermute | solution.py:380
  22.2 0.6 collective-permute-start.3
  22.8 2.8 %collective-permute-start.2 = (bf16[80,512]{1,0:T(8,128)(2,1)S(1)}, bf16[80,512]{1,0:T(8,128)(2,1)S(1)}, u32[]{:S(2)}, u32[]{:S(2)}) collective-permute-start(bf16[80,512]{1,0:T(8,128)(2,1)S(1)} %constant_dynamic-update-slice_fusion), channel_id=1, source_target_pairs={{0,1},{1,2},{2,3},{3,4},{4,5},{5,6},{6,7},{7,8},{8,9},{9,10},{10,1... | collective-permute-start | bytes 245768 | tf_op jit(solution)/shard_map/ppermute | solution.py:380
  25.6 2.0 %collective-permute-done.3.right = bf16[80,512]{1,0:T(8,128)(2,1)S(1)} collective-permute-done((bf16[80,512]{1,0:T(8,128)(2,1)S(1)}, bf16[80,512]{1,0:T(8,128)(2,1)S(1)}, u32[]{:S(2)}, u32[]{:S(2)}) %collective-permute-start.3) | collective-permute-done | bytes 81952 | tf_op jit(solution)/shard_map/ppermute | solution.py:380
  27.6 2.1 %collective-permute-done.2.left = bf16[80,512]{1,0:T(8,128)(2,1)S(1)} collective-permute-done((bf16[80,512]{1,0:T(8,128)(2,1)S(1)}, bf16[80,512]{1,0:T(8,128)(2,1)S(1)}, u32[]{:S(2)}, u32[]{:S(2)}) %collective-permute-start.2) | collective-permute-done | bytes 81952 | tf_op jit(solution)/shard_map/ppermute | solution.py:380
  29.7 0.0 copy-done
  29.7 0.0 copy-done.1
  29.7 0.6 copy-done.3
  30.3 31.6 %main.1 = (bf16[2048,1024]{1,0:T(8,128)(2,1)}, bf16[2048,512]{1,0:T(8,128)(2,1)}, bf16[320,512]{1,0:T(8,128)(2,1)}, bf16[4,4,4,96,128]{4,3,2,1,0:T(8,128)(2,1)}, bf16[4,4,4,96,128]{4,3,2,1,0:T(8,128)(2,1)}) custom-call(s32[1]{0:T(128)} %bitcast.1.core, bf16[8,64,512]{2,1,0:T(8,128)(2,1)} %lat.1, bf16[320,512]{1,0:T(8,128)(2,1)} %copy-done.1, ...), custom_call_target="tpu_custom_call" | custom-call | flops 21474836480 | bytes 37748736 | tf_op jit(solution)/shard_map/main/pallas_call | solution.py:198
  61.9 7.0 %collective-permute-start.4 = (bf16[4,4,4,96,128]{4,3,2,1,0:T(8,128)(2,1)}, bf16[4,4,4,96,128]{4,3,2,1,0:T(8,128)(2,1)S(1)}, u32[]{:S(2)}, u32[]{:S(2)}) collective-permute-start(bf16[4,4,4,96,128]{4,3,2,1,0:T(8,128)(2,1)} %get-tuple-element.19), channel_id=1, source_target_pairs={{0,1},{1,0},{2,3},{3,2},{4,5},{5,4},{6,7},{7,6},{8,9},{9,8},{10,11... | collective-permute-start | bytes 4718600 | tf_op jit(solution)/shard_map/ppermute | solution.py:419
  68.9 3.2 %collective-permute-done.4 = bf16[4,4,4,96,128]{4,3,2,1,0:T(8,128)(2,1)S(1)} collective-permute-done((bf16[4,4,4,96,128]{4,3,2,1,0:T(8,128)(2,1)}, bf16[4,4,4,96,128]{4,3,2,1,0:T(8,128)(2,1)S(1)}, u32[]{:S(2)}, u32[]{:S(2)}) %collective-permute-start.4) | collective-permute-done | bytes 1572896 | tf_op jit(solution)/shard_map/ppermute | solution.py:419
  72.1 3.0 %add_convert_fusion = bf16[4,4,4,96,128]{4,3,2,1,0:T(8,128)(2,1)} fusion(bf16[4,4,4,96,128]{4,3,2,1,0:T(8,128)(2,1)S(1)} %collective-permute-done.4, bf16[4,4,4,96,128]{4,3,2,1,0:T(8,128)(2,1)} %get-tuple-element.18), kind=kLoop, calls=%fused_computation | loop fusion | flops 3145728 | bytes 4718592 | tf_op jit(solution)/shard_map/convert_element_type | solution.py:435
  75.1 6.3 %all-to-all-start = ((bf16[64,96,128]{2,1,0:T(8,128)(2,1)}), bf16[64,96,128]{2,1,0:T(8,128)(2,1)S(1)}, u32[]{:S(2)}, u32[]{:S(2)}) async-start(bf16[64,96,128]{2,1,0:T(8,128)(2,1)} %bitcast.24), calls=%async_computation | async-start | bytes 3145728 | tf_op jit(solution)/shard_map/all_to_all | solution.py:436
  81.5 14.3 %tail.1 = (bf16[2048,512]{1,0:T(8,128)(2,1)}, f32[512,512]{1,0:T(8,128)}) custom-call(bf16[2048,512]{1,0:T(8,128)(2,1)} %bitcast.47, bf16[2048,1024]{1,0:T(8,128)(2,1)} %get-tuple-element.13.act, bf16[1024,512]{1,0:T(8,128)(2,1)} %w_out.1, bf16[16,128,512]{2,1,0:T(8,128)(2,1)} %bitcast.55, bf16[320,512]{1,0:T(8,128)(2,1)} %get-tuple-element.15.edge, ...), custom_call_target="tpu_custom_call" | custom-call | flops 7516192768 | bytes 23068672 | tf_op jit(solution)/shard_map/tail/pallas_call | solution.py:325
  95.8 8.5 %all-to-all-done.parts = bf16[64,96,128]{2,1,0:T(8,128)(2,1)S(1)} async-done(((bf16[64,96,128]{2,1,0:T(8,128)(2,1)}), bf16[64,96,128]{2,1,0:T(8,128)(2,1)S(1)}, u32[]{:S(2)}, u32[]{:S(2)}) %all-to-all-start) | async-done | bytes 1572896 | tf_op jit(solution)/shard_map/all_to_all | solution.py:436
  104.3 0.9 sum_blocks.1
  (26 shorter events, 0.2 us)
Async XLA Ops:
  2.7 11.1 %collective-permute-start.1 = (bf16[320,512]{1,0:T(8,128)(2,1)S(1)}, bf16[320,512]{1,0:T(8,128)(2,1)S(1)}, u32[]{:S(2)}, u32[]{:S(2)}) collective-permute-start(bf16[320,512]{1,0:T(8,128)(2,1)S(1)} %pad_maximum_fusion.1), channel_id=1, source_target_pairs={{16,0},{32,16},{48,32},{64,48},{80,64},{96,80},{112,96},{17,1},{33... | collective-permute-start | bytes 983048 | tf_op jit(solution)/shard_map/ppermute | solution.py:380
  4.0 18.0 %collective-permute-start = (bf16[320,512]{1,0:T(8,128)(2,1)S(1)}, bf16[320,512]{1,0:T(8,128)(2,1)S(1)}, u32[]{:S(2)}, u32[]{:S(2)}) collective-permute-start(bf16[320,512]{1,0:T(8,128)(2,1)S(1)} %pad_maximum_fusion), channel_id=1, source_target_pairs={{0,16},{16,32},{32,48},{48,64},{64,80},{80,96},{96,112},{1,17},{17... | collective-permute-start | bytes 983048 | tf_op jit(solution)/shard_map/ppermute | solution.py:380
  13.8 15.9 %copy-start = (bf16[320,512]{1,0:T(8,128)(2,1)}, bf16[320,512]{1,0:T(8,128)(2,1)S(1)}, u32[]{:S(2)}) copy-start(bf16[320,512]{1,0:T(8,128)(2,1)S(1)} %collective-permute-done.1.after) | copy-start | bytes 983044
  22.0 7.6 %copy-start.1 = (bf16[320,512]{1,0:T(8,128)(2,1)}, bf16[320,512]{1,0:T(8,128)(2,1)S(1)}, u32[]{:S(2)}) copy-start(bf16[320,512]{1,0:T(8,128)(2,1)S(1)} %collective-permute-done.before) | copy-start | bytes 983044
  22.2 5.4 %collective-permute-start.3 = (bf16[80,512]{1,0:T(8,128)(2,1)S(1)}, bf16[80,512]{1,0:T(8,128)(2,1)S(1)}, u32[]{:S(2)}, u32[]{:S(2)}) collective-permute-start(bf16[80,512]{1,0:T(8,128)(2,1)S(1)} %constant_dynamic-update-slice_fusion.5), channel_id=1, source_target_pairs={{1,0},{2,1},{3,2},{4,3},{5,4},{6,5},{7,6},{8,7},{9,8},{10,9},{11,1... | collective-permute-start | bytes 245768 | tf_op jit(solution)/shard_map/ppermute | solution.py:380
  22.8 6.8 %collective-permute-start.2 = (bf16[80,512]{1,0:T(8,128)(2,1)S(1)}, bf16[80,512]{1,0:T(8,128)(2,1)S(1)}, u32[]{:S(2)}, u32[]{:S(2)}) collective-permute-start(bf16[80,512]{1,0:T(8,128)(2,1)S(1)} %constant_dynamic-update-slice_fusion), channel_id=1, source_target_pairs={{0,1},{1,2},{2,3},{3,4},{4,5},{5,6},{6,7},{7,8},{8,9},{9,10},{10,1... | collective-permute-start | bytes 245768 | tf_op jit(solution)/shard_map/ppermute | solution.py:380
  27.6 2.1 %copy-start.2 = (bf16[80,512]{1,0:T(8,128)(2,1)}, bf16[80,512]{1,0:T(8,128)(2,1)S(1)}, u32[]{:S(2)}) copy-start(bf16[80,512]{1,0:T(8,128)(2,1)S(1)} %collective-permute-done.3.right) | copy-start | bytes 245764
  29.7 0.6 copy-start.3
  61.9 10.2 %collective-permute-start.4 = (bf16[4,4,4,96,128]{4,3,2,1,0:T(8,128)(2,1)}, bf16[4,4,4,96,128]{4,3,2,1,0:T(8,128)(2,1)S(1)}, u32[]{:S(2)}, u32[]{:S(2)}) collective-permute-start(bf16[4,4,4,96,128]{4,3,2,1,0:T(8,128)(2,1)} %get-tuple-element.19), channel_id=1, source_target_pairs={{0,1},{1,0},{2,3},{3,2},{4,5},{5,4},{6,7},{7,6},{8,9},{9,8},{10,11... | collective-permute-start | bytes 4718600 | tf_op jit(solution)/shard_map/ppermute | solution.py:419
  75.1 29.2 %all-to-all-start = ((bf16[64,96,128]{2,1,0:T(8,128)(2,1)}), bf16[64,96,128]{2,1,0:T(8,128)(2,1)S(1)}, u32[]{:S(2)}, u32[]{:S(2)}) async-start(bf16[64,96,128]{2,1,0:T(8,128)(2,1)} %bitcast.24), calls=%async_computation | async-start | bytes 3145728 | tf_op jit(solution)/shard_map/all_to_all | solution.py:436

commit v5 on v4

--- a/solution.py
+++ b/solution.py
@@ -32,7 +32,7 @@
 
 def main_body(
     core, lat, before, after, left, right, w_a, w_b, tokens_hbm, cot_hbm, w_in_hbm, w_out_hbm,
-    act_out, up_cot, up_cot_edge, keep, send,
+    act_out, up_cot, up_cot_edge, first_row, last_row, keep, send,
     sources, edges, tokens, cot, tokens_edge, cot_edge, w_in, w_out, up, act, pre, pre_edge,
     turned, sems,
 ):
@@ -75,11 +75,9 @@
         for i, edge in enumerate((rights, edges[0], edges[1], lefts)):
             sources[i, 0:16] = edge.astype(BF16)
             sources[i, last : last + 16] = pltpu.roll(edge, 15, 0).astype(BF16)
-        for ref, lane, part in ((tokens_edge, cols, 16), (cot_edge, cols + fine_cols, 48)):
-            ref[0:fine_cols] = before[lane : lane + fine_cols]
-            ref[fine_cols : 2 * fine_cols] = after[lane : lane + fine_cols]
-            ref[2 * fine_cols : 2 * fine_cols + 32] = left[part : part + 32]
-            ref[2 * fine_cols + 32 :] = right[part : part + 32]
+        for ref, part in ((tokens_edge, 16), (cot_edge, 48)):
+            ref[0:32] = left[part : part + 32]
+            ref[32:] = right[part : part + 32]
 
     @pl.when(step < 4)
     def _():
@@ -95,14 +93,14 @@
                 total_b = term_b if total_b is None else total_b + term_b
             planes.append((total_a[:size] + total_b[16:]).astype(BF16))
             side = (total_a[size:] + total_b[:16]).astype(BF16)
-            at = count + 2 * fine_cols + (1 - q) * 32 + (1 - parity) * 16
+            at = count + fine_cols + (1 - q) * 32 + (1 - parity) * 16
             up[half, pl.ds(pl.multiple_of(at, 16), 16)] = side
         r, k = iota((fine_cols, fine_cols), 0), iota((fine_cols, fine_cols), 1)
         spread = (k == (r % 2) * cols + r // 2).astype(F32).astype(BF16)
         for m in range(rows + 1):
             pair = jnp.concatenate([z[m * cols : (m + 1) * cols] for z in planes], axis=0)
             value = dot_nn(spread, pair).astype(BF16)
-            even = 2 * m * fine_cols if m < rows else count + fine_cols
+            even = 2 * m * fine_cols if m < rows else count
             odd = (2 * m - 1) * fine_cols if m > 0 else count
             at = even + parity * (odd - even)
             up[half, pl.ds(pl.multiple_of(at, 128), fine_cols)] = value
@@ -126,9 +124,14 @@
         for n in range(0, hidden, 256):
             span = slice(n, n + 256)
             _, pre_edge[:, span] = network(
-                lambda: tokens_edge[...], lambda i: up[i, count:], lambda: cot_edge[...], span
+                lambda: tokens_edge[...], lambda i: up[i, count + fine_cols :], lambda: cot_edge[...], span
             )
-        up_cot_edge[...] = dot_nt(pre_edge[...], w_in[model:, :]).astype(BF16)
+        value = dot_nt(pre_edge[...], w_in[model:, :]).astype(BF16)
+        up_cot_edge[...] = value
+        for i in range(2):
+            at = slice(fine_cols + 16 * i, fine_cols + 16 * i + 16)
+            last_row[at] = value[32 * i : 32 * i + 16]
+            first_row[at] = value[32 * i + 16 : 32 * i + 32]
 
     @pl.when((step > 4) & (step < 9))
     def _():
@@ -141,7 +144,17 @@
             act[at, span] = wide
             act_out[:, span] = wide
             pre[at, span] = grad
-        up_cot[...] = dot_nt(pre[at, :], w_in[model:, :]).astype(BF16)
+        value = dot_nt(pre[at, :], w_in[model:, :]).astype(BF16)
+        up_cot[...] = value
+
+        @pl.when(step == 5)
+        def _():
+            first_row[0:fine_cols] = value[:fine_cols]
+
+        @pl.when(step == 8)
+        def _():
+            last_row[0:fine_cols] = value[block - fine_cols :]
+
         turned[0:model, at] = tokens[at, :].T
         turned[model : model + half_model, at] = up[0, at].T
         turned[model + half_model : 2 * model, at] = up[1, at].T
@@ -189,7 +202,8 @@
     count = tokens.shape[0]
     hidden = w_out.shape[0]
     block = count // 4
-    edge = 4 * cols + 64
+    edge = 64
+    pack = 2 * cols + 32
     clamp = lambda i, low: jnp.clip(i - low, 0, 3)
     whole = lambda *shape: pl.BlockSpec(shape, lambda i, c: (0,) * len(shape))
     kernel_row = lambda i, top: (top - clamp(i, 0) // 2, 0, clamp(i, 0) % 2, 0)
@@ -217,6 +231,8 @@
                 tokens_of(hidden),
                 tokens_of(model),
                 whole(edge, model),
+                whole(pack, model),
+                whole(pack, model),
                 whole(*blocks),
                 whole(*blocks),
             ],
@@ -229,7 +245,7 @@
                 pltpu.VMEM((edge, model), BF16),
                 pltpu.VMEM((2 * model, hidden), BF16),
                 pltpu.VMEM((hidden, model), BF16),
-                pltpu.VMEM((2, count + edge, half), BF16),
+                pltpu.VMEM((2, count + 2 * cols + edge, half), BF16),
                 pltpu.VMEM((count, hidden), BF16),
                 pltpu.VMEM((count, hidden), BF16),
                 pltpu.VMEM((edge, hidden), BF16),
@@ -241,6 +257,8 @@
             jax.ShapeDtypeStruct((count, hidden), BF16),
             jax.ShapeDtypeStruct((count, model), BF16),
             jax.ShapeDtypeStruct((edge, model), BF16),
+            jax.ShapeDtypeStruct((pack, model), BF16),
+            jax.ShapeDtypeStruct((pack, model), BF16),
             jax.ShapeDtypeStruct(blocks, BF16),
             jax.ShapeDtypeStruct(blocks, BF16),
         ],
@@ -254,7 +272,7 @@
 
 
 def tail_body(
-    tokens, act, w_out, cot_hbm, edge, weight, united, out,
+    tokens, act, w_out, cot_hbm, edge, before, after, weight, united, out,
     cot, planes, sem,
 ):
     step = pl.program_id(0)
@@ -276,25 +294,25 @@
         copy.wait()
         r, c = iota((fine_cols, fine_cols), 0), iota((fine_cols, fine_cols), 1)
         pick = (c == 2 * (r % cols) + r // cols).astype(F32).astype(BF16)
-        lefts, rights = [
-            edge[2 * fine_cols + i : 2 * fine_cols + i + 32].astype(F32) for i in (0, 32)
-        ]
+        sides, above, below = [ref.astype(F32) for ref in (
+            edge[...], before[fine_cols:], after[fine_cols:]
+        )]
         place = iota((cols, model), 0)
         for e in range(fine_rows + 2):
             if e == 0:
-                row = edge[0:fine_cols]
+                row, left, right = before[0:fine_cols], above[8:9], above[24:25]
             elif e == fine_rows + 1:
-                row = edge[fine_cols : 2 * fine_cols]
+                row, left, right = after[0:fine_cols], below[0:1], below[16:17]
             else:
-                row = cot[e - 1]
-            at = e // 2 + 16 * (e % 2)
+                at = e // 2 + 16 * (e % 2)
+                row, left, right = cot[e - 1], sides[at : at + 1], sides[at + 32 : at + 33]
             found = dot_nn(pick, row)
             even, odd = found[:cols], found[cols:]
             taps = (
-                jnp.where(place == 0, lefts[at : at + 1], pltpu.roll(odd, 1, 0)),
+                jnp.where(place == 0, left, pltpu.roll(odd, 1, 0)),
                 even,
                 odd,
-                jnp.where(place == cols - 1, rights[at : at + 1], pltpu.roll(even, cols - 1, 0)),
+                jnp.where(place == cols - 1, right, pltpu.roll(even, cols - 1, 0)),
             )
             for tap in range(4):
                 planes[e % 2, e // 2, :, tap * model : (tap + 1) * model] = taps[tap].astype(BF16)
@@ -314,7 +332,7 @@
             out[...] += term
 
 
-def tail_kernel(tokens, act, w_out, cot, edge, weight):
+def tail_kernel(tokens, act, w_out, cot, edge, before, after, weight):
     fine_rows, fine_cols, model = cot.shape
     width = weight.shape[1]
     count, hidden = act.shape
@@ -331,6 +349,8 @@
             whole(w_out),
             pl.BlockSpec(memory_space=pl.ANY),
             whole(edge),
+            whole(before),
+            whole(after),
             pl.BlockSpec((1, 4 * model, width), lambda i: (jnp.maximum(i - 4, 0), 0, 0)),
         ],
         out_specs=[tokens_of(model), pl.BlockSpec((size, width), lambda i: (0, 0))],
@@ -346,7 +366,7 @@
         compiler_params=pltpu.CompilerParams(vmem_limit_bytes=58 << 20),
         cost_estimate=cost(7 << 30, 22 << 20),
         name="tail",
-    )(tokens, act, w_out, cot, edge, weight.reshape(4, 4 * model, width))
+    )(tokens, act, w_out, cot, edge, before, after, weight.reshape(4, 4 * model, width))
 
 
 def sum_body(parts, in_grad, out_grad):
@@ -381,21 +401,15 @@
 
 
 def halos(latents, tokens, cot):
-    cols, fine_cols = latents.shape[1], tokens.shape[1]
-    row = lambda i: jnp.concatenate([latents[i], tokens[i], cot[i]], axis=0)
-    before, after = swap(row(-1), row(0), "lat", False)
+    before, after = swap(latents[-1], latents[0], "lat", False)
 
     def column(c):
-        parts = []
-        place = c % cols
-        pad = lambda a: jnp.pad(a, ((0, 16 - a.shape[0]), (0, 0)))
+        place = c % latents.shape[1]
         ends = [a[place : place + 1] for a in (before, after)]
-        parts.append(pad(jnp.concatenate([ends[0], latents[:, c], ends[1]], axis=0)))
-        for fine, start in ((tokens, cols), (cot, cols + fine_cols)):
-            place = start + c % fine_cols
-            ends = [a[place : place + 1] for a in (before, after)]
-            parts.append(pad(jnp.concatenate([ends[0], fine[1::2, c]], axis=0)))
-            parts.append(pad(jnp.concatenate([fine[0::2, c], ends[1]], axis=0)))
+        parts = [ends[0], latents[:, c], ends[1], jnp.zeros((6, latents.shape[2]), BF16)]
+        for fine in (tokens, cot):
+            parts.append(jnp.pad(fine[1::2, c], ((1, 7), (0, 0))))
+            parts.append(jnp.pad(fine[0::2, c], ((0, 8), (0, 0))))
         return jnp.concatenate(parts, axis=0)
 
     left, right = swap(column(-1), column(0), "lon", True)
@@ -427,18 +441,20 @@
     cot = cotangent.reshape(count, model)
 
     before, after, left, right = halos(latents, fine_tokens, cotangent)
-    act, up_cot, up_cot_edge, keep, send = main_kernel(
+    act, up_cot, up_cot_edge, first_row, last_row, keep, send = main_kernel(
         core, latents, before, after, left, right, upsample_weight,
         tokens, cot, uniting_in, uniting_out,
     )
     other = other_core(send)
+    above, below = swap(last_row, first_row, "lat", False)
     halves = (keep.astype(F32) + other.astype(F32)).astype(BF16).reshape(64, 96, 128)
+    halves, above, below = lax.optimization_barrier((halves, above, below))
     parts = lax.all_to_all(
         halves, BOTH, 0, 0, axis_index_groups=chip_groups(), tiled=True
     )
     united, latent_grad = tail_kernel(
         tokens, act, uniting_out, up_cot.reshape(fine_tokens.shape), up_cot_edge,
-        upsample_weight,
+        above, below, upsample_weight,
     )
     in_grad, out_grad = sum_blocks(parts)
     return (

time: 107 us -> 104 us (0.972)
  waiting for transfers between devices: 26.1 us -> 17.4 us
  starting transfers between devices: 22.7 us -> 28 us
  Pallas kernels: 46.8 us -> 48.2 us
    ppermute x1, starting transfers between devices: 6.96 us -> 0.08 us  [other_core(): return lax.ppermute(array, 'lon', [(i, i ^ 1) for i in range(16)])]
    all_to_all x1, starting transfers between devices: 6.34 us -> 13 us  [shards(): lax.all_to_all(halves, BOTH, 0, 0, axis_index_groups=chip_groups(), tiled...]
    ppermute x4 -> x6, starting transfers between devices: 9.35 us -> 14.9 us  [swap(): return (lax.ppermute(last, axis, up), lax.ppermute(first, axis, down))]
    ppermute x4 -> x6, waiting for transfers between devices: 14.3 us -> 9.1 us  [swap(): return (lax.ppermute(last, axis, up), lax.ppermute(first, axis, down))]
    ppermute x1, waiting for transfers between devices: 3.25 us -> 0.01 us  [other_core(): return lax.ppermute(array, 'lon', [(i, i ^ 1) for i in range(16)])]
    pallas_call x1, Pallas kernels: 31.6 us -> 33 us  [main_kernel(): pl.pallas_call(main_body, grid_spec=pltpu.PrefetchScalarGridSpec(num_scal...]
    squeeze x5, local copies, waits for them, and re-layouts: 2.04 us -> 0.91 us  [the longest x1 0.88 us: halos(): before, after = swap(latents[-1], latents[0], 'lat', False)]
  transfers between devices with their start and end apart: 6 -> 8, of which waited for: 6 -> 4; matrix products, arithmetic and copies ran while one was open for 3% -> 6% of each run, Pallas kernels for 14% -> 14%
where the time goes in v5:
time: 104 us; the launch traced here: 102 us
  Pallas kernels  48.2 us (46%)
  starting transfers between devices  28 us (27%)
  waiting for transfers between devices  17.4 us (17%)
  local copies, waits for them, and re-layouts  4.78 us (5%)
  other arithmetic  3.02 us (3%)
    pallas_call x1, Pallas kernels, main_kernel(): pl.pallas_call(main_body, grid_spec=pltpu.PrefetchScalarGridSpec(num_scal...  33 us
    ppermute x6, starting transfers between devices, swap(): return (lax.ppermute(last, axis, up), lax.ppermute(first, axis, down))  14.9 us
    pallas_call x1, Pallas kernels, tail_kernel(): pl.pallas_call(tail_body, grid=(8,), in_specs=[tokens_of(model), tokens_o...  14.4 us
    all_to_all x1, starting transfers between devices, shards(): lax.all_to_all(halves, BOTH, 0, 0, axis_index_groups=chip_groups(), tiled...  13 us
    ppermute x6, waiting for transfers between devices, swap(): return (lax.ppermute(last, axis, up), lax.ppermute(first, axis, down))  9.1 us
    all_to_all x1, waiting for transfers between devices, shards(): lax.all_to_all(halves, BOTH, 0, 0, axis_index_groups=chip_groups(), tiled...  8.29 us
    convert_element_type x1, other arithmetic, shards(): (keep.astype(F32) + other.astype(F32)).astype(BF16).reshape(64, 96, 128)  3.02 us
  transfers between devices with their start and end apart: 8, of which 4 were waited for; matrix products, arithmetic and copies ran while one was open for 6% of the time, Pallas kernels for 14%

profile of v5, /device:TPU:1, one launch (start us, length us, event | category | flops | bytes accessed | tf_op | source)
XLA Modules:
  0.0 102.3 jit_solution(4194825528649361138)
XLA Ops:
  0.6 0.9 slice_bitcast_fusion
  1.5 1.3 %collective-permute-start.1 = (bf16[64,512]{1,0:T(8,128)(2,1)S(1)}, bf16[64,512]{1,0:T(8,128)(2,1)S(1)}, u32[]{:S(2)}, u32[]{:S(2)}) collective-permute-start(bf16[64,512]{1,0:T(8,128)(2,1)S(1)} %get-tuple-element.42), channel_id=1, source_target_pairs={{16,0},{32,16},{48,32},{64,48},{80,64},{96,80},{112,96},{17,1},{33... | collective-permute-start | bytes 196616 | tf_op jit(solution)/shard_map/ppermute | solution.py:400
  2.8 4.7 %collective-permute-start = (bf16[64,512]{1,0:T(8,128)(2,1)S(1)}, bf16[64,512]{1,0:T(8,128)(2,1)S(1)}, u32[]{:S(2)}, u32[]{:S(2)}) collective-permute-start(bf16[64,512]{1,0:T(8,128)(2,1)S(1)} %get-tuple-element.43), channel_id=1, source_target_pairs={{0,16},{16,32},{32,48},{48,64},{64,80},{80,96},{96,112},{1,17},{17... | collective-permute-start | bytes 196616 | tf_op jit(solution)/shard_map/ppermute | solution.py:400
  7.5 0.9 fusion.2
  8.4 1.0 fusion.1
  9.4 1.0 fusion
  10.6 0.0 collective-permute-done.before
  10.7 0.1 concatenate.6
  10.8 4.3 %collective-permute-start.2 = (bf16[80,512]{1,0:T(8,128)(2,1)S(1)}, bf16[80,512]{1,0:T(8,128)(2,1)S(1)}, u32[]{:S(2)}, u32[]{:S(2)}) collective-permute-start(bf16[80,512]{1,0:T(8,128)(2,1)S(1)} %concatenate.6), channel_id=1, source_target_pairs={{0,1},{1,2},{2,3},{3,4},{4,5},{5,6},{6,7},{7,8},{8,9},{9,10},{10,1... | collective-permute-start | bytes 245768 | tf_op jit(solution)/shard_map/ppermute | solution.py:400
  15.1 0.1 concatenate.7
  15.2 0.1 collective-permute-start.3
  15.3 1.3 %collective-permute-done.2.left = bf16[80,512]{1,0:T(8,128)(2,1)S(1)} collective-permute-done((bf16[80,512]{1,0:T(8,128)(2,1)S(1)}, bf16[80,512]{1,0:T(8,128)(2,1)S(1)}, u32[]{:S(2)}, u32[]{:S(2)}) %collective-permute-start.2) | collective-permute-done | bytes 81952 | tf_op jit(solution)/shard_map/ppermute | solution.py:400
  16.5 4.1 %collective-permute-done.3.right = bf16[80,512]{1,0:T(8,128)(2,1)S(1)} collective-permute-done((bf16[80,512]{1,0:T(8,128)(2,1)S(1)}, bf16[80,512]{1,0:T(8,128)(2,1)S(1)}, u32[]{:S(2)}, u32[]{:S(2)}) %collective-permute-start.3) | collective-permute-done | bytes 81952 | tf_op jit(solution)/shard_map/ppermute | solution.py:400
  20.6 0.6 copy-done.5
  21.2 33.0 %main.1 = (bf16[2048,1024]{1,0:T(8,128)(2,1)}, bf16[2048,512]{1,0:T(8,128)(2,1)}, bf16[64,512]{1,0:T(8,128)(2,1)}, bf16[160,512]{1,0:T(8,128)(2,1)}, bf16[160,51...) custom-call(s32[1]{0:T(128)} %bitcast.1.core, bf16[8,64,512]{2,1,0:T(8,128)(2,1)} %lat.1, ...), custom_call_target="tpu_custom_call" | custom-call | flops 21474836480 | bytes 37748736 | tf_op jit(solution)/shard_map/main/pallas_call | solution.py:212
  54.2 0.1 collective-permute-start.4
  54.3 3.3 %collective-permute-start.5 = (bf16[160,512]{1,0:T(8,128)(2,1)}, bf16[160,512]{1,0:T(8,128)(2,1)S(1)}, u32[]{:S(2)}, u32[]{:S(2)}) collective-permute-start(bf16[160,512]{1,0:T(8,128)(2,1)} %get-tuple-element.23), channel_id=1, source_target_pairs={{0,16},{16,32},{32,48},{48,64},{64,80},{80,96},{96,112},{1,17},{17... | collective-permute-start | bytes 491528 | tf_op jit(solution)/shard_map/ppermute | solution.py:400
  57.7 1.3 %collective-permute-start.6 = (bf16[160,512]{1,0:T(8,128)(2,1)}, bf16[160,512]{1,0:T(8,128)(2,1)S(1)}, u32[]{:S(2)}, u32[]{:S(2)}) collective-permute-start(bf16[160,512]{1,0:T(8,128)(2,1)} %get-tuple-element.24), channel_id=1, source_target_pairs={{16,0},{32,16},{48,32},{64,48},{80,64},{96,80},{112,96},{17,1},{33... | collective-permute-start | bytes 491528 | tf_op jit(solution)/shard_map/ppermute | solution.py:400
  59.0 3.0 %add_convert_fusion = bf16[4,4,4,96,128]{4,3,2,1,0:T(8,128)(2,1)} fusion(bf16[4,4,4,96,128]{4,3,2,1,0:T(8,128)(2,1)S(1)} %collective-permute-done.4, bf16[4,4,4,96,128]{4,3,2,1,0:T(8,128)(2,1)} %get-tuple-element.21), kind=kLoop, calls=%fused_computation | loop fusion | flops 3145728 | bytes 4718592 | tf_op jit(solution)/shard_map/convert_element_type | solution.py:450
  62.0 3.7 %collective-permute-done.6.after = bf16[160,512]{1,0:T(8,128)(2,1)S(1)} collective-permute-done((bf16[160,512]{1,0:T(8,128)(2,1)}, bf16[160,512]{1,0:T(8,128)(2,1)S(1)}, u32[]{:S(2)}, u32[]{:S(2)}) %collective-permute-start.6) | collective-permute-done | bytes 163872 | tf_op jit(solution)/shard_map/ppermute | solution.py:400
  65.8 13.0 %all-to-all-start = ((bf16[64,96,128]{2,1,0:T(8,128)(2,1)}), bf16[64,96,128]{2,1,0:T(8,128)(2,1)S(1)}, u32[]{:S(2)}, u32[]{:S(2)}) async-start(bf16[64,96,128]{2,1,0:T(8,128)(2,1)} %bitcast.17), calls=%async_computation | async-start | bytes 3145728 | tf_op jit(solution)/shard_map/all_to_all | solution.py:452
  78.8 14.4 %tail.1 = (bf16[2048,512]{1,0:T(8,128)(2,1)}, f32[512,512]{1,0:T(8,128)}) custom-call(bf16[2048,512]{1,0:T(8,128)(2,1)} %bitcast.39, bf16[2048,1024]{1,0:T(8,128)(2,1)} %get-tuple-element.18.act, bf16[1024,512]{1,0:T(8,128)(2,1)} %w_out.1, bf16[16,128,512]{2,1,0:T(8,128)(2,1)} %bitcast.43, bf16[64,512]{1,0:T(8,128)(2,1)} %get-tuple-element.20.edge, ...), custom_call_target="tpu_custom_call" | custom-call | flops 7516192768 | bytes 23068672 | tf_op jit(solution)/shard_map/tail/pallas_call | solution.py:343
  93.1 8.3 %all-to-all-done.parts = bf16[64,96,128]{2,1,0:T(8,128)(2,1)S(1)} async-done(((bf16[64,96,128]{2,1,0:T(8,128)(2,1)}), bf16[64,96,128]{2,1,0:T(8,128)(2,1)S(1)}, u32[]{:S(2)}, u32[]{:S(2)}) %all-to-all-start) | async-done | bytes 1572896 | tf_op jit(solution)/shard_map/all_to_all | solution.py:452
  101.4 0.9 sum_blocks.1
  (31 shorter events, 0.1 us)
Async XLA Ops:
  1.5 9.1 %collective-permute-start.1 = (bf16[64,512]{1,0:T(8,128)(2,1)S(1)}, bf16[64,512]{1,0:T(8,128)(2,1)S(1)}, u32[]{:S(2)}, u32[]{:S(2)}) collective-permute-start(bf16[64,512]{1,0:T(8,128)(2,1)S(1)} %get-tuple-element.42), channel_id=1, source_target_pairs={{16,0},{32,16},{48,32},{64,48},{80,64},{96,80},{112,96},{17,1},{33... | collective-permute-start | bytes 196616 | tf_op jit(solution)/shard_map/ppermute | solution.py:400
  2.8 7.8 %collective-permute-start = (bf16[64,512]{1,0:T(8,128)(2,1)S(1)}, bf16[64,512]{1,0:T(8,128)(2,1)S(1)}, u32[]{:S(2)}, u32[]{:S(2)}) collective-permute-start(bf16[64,512]{1,0:T(8,128)(2,1)S(1)} %get-tuple-element.43), channel_id=1, source_target_pairs={{0,16},{16,32},{32,48},{48,64},{64,80},{80,96},{96,112},{1,17},{17... | collective-permute-start | bytes 196616 | tf_op jit(solution)/shard_map/ppermute | solution.py:400
  10.6 10.0 %copy-start = (bf16[64,512]{1,0:T(8,128)(2,1)}, bf16[64,512]{1,0:T(8,128)(2,1)S(1)}, u32[]{:S(2)}) copy-start(bf16[64,512]{1,0:T(8,128)(2,1)S(1)} %collective-permute-done.1.after) | copy-start | bytes 196612
  10.6 10.0 %copy-start.1 = (bf16[64,512]{1,0:T(8,128)(2,1)}, bf16[64,512]{1,0:T(8,128)(2,1)S(1)}, u32[]{:S(2)}) copy-start(bf16[64,512]{1,0:T(8,128)(2,1)S(1)} %collective-permute-done.before) | copy-start | bytes 196612
  10.8 5.7 %collective-permute-start.2 = (bf16[80,512]{1,0:T(8,128)(2,1)S(1)}, bf16[80,512]{1,0:T(8,128)(2,1)S(1)}, u32[]{:S(2)}, u32[]{:S(2)}) collective-permute-start(bf16[80,512]{1,0:T(8,128)(2,1)S(1)} %concatenate.6), channel_id=1, source_target_pairs={{0,1},{1,2},{2,3},{3,4},{4,5},{5,6},{6,7},{7,8},{8,9},{9,10},{10,1... | collective-permute-start | bytes 245768 | tf_op jit(solution)/shard_map/ppermute | solution.py:400
  15.2 5.4 %collective-permute-start.3 = (bf16[80,512]{1,0:T(8,128)(2,1)S(1)}, bf16[80,512]{1,0:T(8,128)(2,1)S(1)}, u32[]{:S(2)}, u32[]{:S(2)}) collective-permute-start(bf16[80,512]{1,0:T(8,128)(2,1)S(1)} %concatenate.7), channel_id=1, source_target_pairs={{1,0},{2,1},{3,2},{4,3},{5,4},{6,5},{7,6},{8,7},{9,8},{10,9},{11,1... | collective-permute-start | bytes 245768 | tf_op jit(solution)/shard_map/ppermute | solution.py:400
  16.5 4.1 %copy-start.4 = (bf16[80,512]{1,0:T(8,128)(2,1)}, bf16[80,512]{1,0:T(8,128)(2,1)S(1)}, u32[]{:S(2)}) copy-start(bf16[80,512]{1,0:T(8,128)(2,1)S(1)} %collective-permute-done.2.left) | copy-start | bytes 245764
  20.6 0.6 copy-start.5
  54.2 4.7 %collective-permute-start.4 = (bf16[4,4,4,96,128]{4,3,2,1,0:T(8,128)(2,1)}, bf16[4,4,4,96,128]{4,3,2,1,0:T(8,128)(2,1)S(1)}, u32[]{:S(2)}, u32[]{:S(2)}) collective-permute-start(bf16[4,4,4,96,128]{4,3,2,1,0:T(8,128)(2,1)} %get-tuple-element.22), channel_id=1, source_target_pairs={{0,1},{1,0},{2,3},{3,2},{4,5},{5,4},{6,7},{7,6},{8,9},{9,8},{10,11... | collective-permute-start | bytes 4718600 | tf_op jit(solution)/shard_map/ppermute | solution.py:433
  54.3 7.7 %collective-permute-start.5 = (bf16[160,512]{1,0:T(8,128)(2,1)}, bf16[160,512]{1,0:T(8,128)(2,1)S(1)}, u32[]{:S(2)}, u32[]{:S(2)}) collective-permute-start(bf16[160,512]{1,0:T(8,128)(2,1)} %get-tuple-element.23), channel_id=1, source_target_pairs={{0,16},{16,32},{32,48},{48,64},{64,80},{80,96},{96,112},{1,17},{17... | collective-permute-start | bytes 491528 | tf_op jit(solution)/shard_map/ppermute | solution.py:400
  57.7 8.1 %collective-permute-start.6 = (bf16[160,512]{1,0:T(8,128)(2,1)}, bf16[160,512]{1,0:T(8,128)(2,1)S(1)}, u32[]{:S(2)}, u32[]{:S(2)}) collective-permute-start(bf16[160,512]{1,0:T(8,128)(2,1)} %get-tuple-element.24), channel_id=1, source_target_pairs={{16,0},{32,16},{48,32},{64,48},{80,64},{96,80},{112,96},{17,1},{33... | collective-permute-start | bytes 491528 | tf_op jit(solution)/shard_map/ppermute | solution.py:400
  62.0 16.8 %copy-start.2 = (bf16[160,512]{1,0:T(8,128)(2,1)}, bf16[160,512]{1,0:T(8,128)(2,1)S(1)}, u32[]{:S(2)}) copy-start(bf16[160,512]{1,0:T(8,128)(2,1)S(1)} %collective-permute-done.5.before) | copy-start | bytes 491524
  65.8 13.0 %copy-start.3 = (bf16[160,512]{1,0:T(8,128)(2,1)}, bf16[160,512]{1,0:T(8,128)(2,1)S(1)}, u32[]{:S(2)}) copy-start(bf16[160,512]{1,0:T(8,128)(2,1)S(1)} %collective-permute-done.6.after) | copy-start | bytes 491524
  65.8 35.7 %all-to-all-start = ((bf16[64,96,128]{2,1,0:T(8,128)(2,1)}), bf16[64,96,128]{2,1,0:T(8,128)(2,1)S(1)}, u32[]{:S(2)}, u32[]{:S(2)}) async-start(bf16[64,96,128]{2,1,0:T(8,128)(2,1)} %bitcast.17), calls=%async_computation | async-start | bytes 3145728 | tf_op jit(solution)/shard_map/all_to_all | solution.py:452

commit v6 on v5

--- a/solution.py
+++ b/solution.py
@@ -8,6 +8,7 @@
 BF16 = jnp.bfloat16
 F32 = jnp.float32
 BOTH = ("lat", "lon")
+GRANT = 46
 
 
 def dot_nn(a, b):
@@ -22,18 +23,14 @@
     return pl.CostEstimate(flops=flops, bytes_accessed=nbytes, transcendentals=0)
 
 
-def params():
-    return pltpu.CompilerParams(vmem_limit_bytes=60 << 20)
-
-
 def iota(shape, dim):
     return lax.broadcasted_iota(jnp.int32, shape, dim)
 
 
 def main_body(
-    core, lat, before, after, left, right, w_a, w_b, tokens_hbm, cot_hbm, w_in_hbm, w_out_hbm,
+    core, lat, before, after, left, right, w_a, w_b, tokens, cot, w_in_hbm, w_out_hbm,
     act_out, up_cot, up_cot_edge, first_row, last_row, keep, send,
-    sources, edges, tokens, cot, tokens_edge, cot_edge, w_in, w_out, up, act, pre, pre_edge,
+    sources, edges, tokens_edge, cot_edge, w_in, w_out, up, act, pre, pre_edge,
     turned, sems,
 ):
     step = pl.program_id(0)
@@ -41,19 +38,22 @@
     hidden, model = w_out.shape
     half_model = model // 2
     block = act_out.shape[0]
-    count = tokens.shape[0]
+    count = act.shape[0]
     fine_cols = 2 * cols
     copies = [
         pltpu.make_async_copy(source, target, sems.at[i])
         for i, (source, target) in enumerate(
-            ((w_in_hbm, w_in), (w_out_hbm, w_out), (tokens_hbm, tokens), (cot_hbm, cot))
+            ((w_in_hbm, w_in), (w_out_hbm, w_out))
         )
     ]
 
-    @pl.when(step == 0)
+    @pl.when(step == 1)
     def _():
         for copy in copies:
             copy.start()
+
+    @pl.when(step == 0)
+    def _():
         lefts, rights = left[0:16].astype(F32), right[0:16].astype(F32)
         edges[...] = jnp.zeros_like(edges)
         place = iota((cols, width), 0)
@@ -139,26 +139,24 @@
         for n in range(0, hidden, 256):
             span = slice(n, n + 256)
             wide, grad = network(
-                lambda: tokens[at, :], lambda i: up[i, at], lambda: cot[at, :], span
+                lambda: tokens[...], lambda i: up[i, at], lambda: cot[...], span
             )
             act[at, span] = wide
             act_out[:, span] = wide
             pre[at, span] = grad
-        value = dot_nt(pre[at, :], w_in[model:, :]).astype(BF16)
-        up_cot[...] = value
-
-        @pl.when(step == 5)
-        def _():
-            first_row[0:fine_cols] = value[:fine_cols]
-
-        @pl.when(step == 8)
-        def _():
-            last_row[0:fine_cols] = value[block - fine_cols :]
-
-        turned[0:model, at] = tokens[at, :].T
+        turned[0:model, at] = tokens[...].T
         turned[model : model + half_model, at] = up[0, at].T
         turned[model + half_model : 2 * model, at] = up[1, at].T
-        turned[2 * model :, at] = cot[at, :].T
+        turned[2 * model :, at] = cot[...].T
+        up_cot[...] = dot_nt(pre[at, :], w_in[model:, :]).astype(BF16)
+
+    @pl.when(step == 5)
+    def _():
+        first_row[0:fine_cols] = up_cot[0:fine_cols]
+
+    @pl.when(step == 8)
+    def _():
+        last_row[0:fine_cols] = up_cot[block - fine_cols :]
 
     for j in range(4):
 
@@ -222,8 +220,8 @@
                 whole(*right.shape),
                 pl.BlockSpec((1, 4, half, width), lambda i, c: kernel_row(i, 1)),
                 pl.BlockSpec((1, 4, half, width), lambda i, c: kernel_row(i, 3)),
-                pl.BlockSpec(memory_space=pl.ANY),
-                pl.BlockSpec(memory_space=pl.ANY),
+                tokens_of(model),
+                tokens_of(model),
                 pl.BlockSpec(memory_space=pl.ANY),
                 pl.BlockSpec(memory_space=pl.ANY),
             ],
@@ -239,8 +237,6 @@
             scratch_shapes=[
                 pltpu.VMEM((4, (rows + 2) * cols + 32, width), BF16),
                 pltpu.VMEM((2, 16, width), F32),
-                pltpu.VMEM((count, model), BF16),
-                pltpu.VMEM((count, model), BF16),
                 pltpu.VMEM((edge, model), BF16),
                 pltpu.VMEM((edge, model), BF16),
                 pltpu.VMEM((2 * model, hidden), BF16),
@@ -250,7 +246,7 @@
                 pltpu.VMEM((count, hidden), BF16),
                 pltpu.VMEM((edge, hidden), BF16),
                 pltpu.VMEM((3 * model, count), BF16),
-                pltpu.SemaphoreType.DMA((4,)),
+                pltpu.SemaphoreType.DMA((2,)),
             ],
         ),
         out_shape=[
@@ -262,7 +258,7 @@
             jax.ShapeDtypeStruct(blocks, BF16),
             jax.ShapeDtypeStruct(blocks, BF16),
         ],
-        compiler_params=params(),
+        compiler_params=pltpu.CompilerParams(vmem_limit_bytes=GRANT << 20),
         cost_estimate=cost(20 << 30, 36 << 20),
         name="main",
     )(
@@ -448,7 +444,6 @@
     other = other_core(send)
     above, below = swap(last_row, first_row, "lat", False)
     halves = (keep.astype(F32) + other.astype(F32)).astype(BF16).reshape(64, 96, 128)
-    halves, above, below = lax.optimization_barrier((halves, above, below))
     parts = lax.all_to_all(
         halves, BOTH, 0, 0, axis_index_groups=chip_groups(), tiled=True
     )

time: 104 us -> 110 us (1.058)
  waiting for transfers between devices: 17.4 us -> 25.6 us
  Pallas kernels: 48.2 us -> 45 us
  local copies, waits for them, and re-layouts: 4.78 us -> 7.17 us
  other arithmetic: 3.02 us -> 1.6 us
    ppermute x6, waiting for transfers between devices: 9.1 us -> 22.6 us  [swap(): return (lax.ppermute(last, axis, up), lax.ppermute(first, axis, down))]
    all_to_all x1, waiting for transfers between devices: 8.29 us -> 0.01 us  [shards(): lax.all_to_all(halves, BOTH, 0, 0, axis_index_groups=chip_groups(), tiled...]
    all_to_all x1, starting transfers between devices: 13 us -> 6.04 us  [shards(): lax.all_to_all(halves, BOTH, 0, 0, axis_index_groups=chip_groups(), tiled...]
    ppermute x1, starting transfers between devices: 0.08 us -> 6.79 us  [other_core(): return lax.ppermute(array, 'lon', [(i, i ^ 1) for i in range(16)])]
    pallas_call x1, Pallas kernels: 33 us -> 29.8 us  [main_kernel(): pl.pallas_call(main_body, grid_spec=pltpu.PrefetchScalarGridSpec(num_scal...]
    ppermute x1, waiting for transfers between devices: 0.01 us -> 3.04 us  [other_core(): return lax.ppermute(array, 'lon', [(i, i ^ 1) for i in range(16)])]
    unnamed x14, local copies, waits for them, and re-layouts: 0.64 us -> 3.04 us
    convert_element_type x1, other arithmetic: 3.02 us -> 1.6 us  [shards(): (keep.astype(F32) + other.astype(F32)).astype(BF16).reshape(64, 96, 128)]
  transfers between devices with their start and end apart: 8 -> 8, of which waited for: 4 -> 4; matrix products, arithmetic and copies ran while one was open for 6% -> 3% of each run, Pallas kernels for 14% -> 13%
where the time goes in v6:
time: 110 us; the launch traced here: 108 us
  Pallas kernels  45 us (41%)
  starting transfers between devices  27.3 us (25%)
  waiting for transfers between devices  25.6 us (23%)
  local copies, waits for them, and re-layouts  7.17 us (7%)
  other arithmetic  1.6 us (1%)
    pallas_call x1, Pallas kernels, main_kernel(): pl.pallas_call(main_body, grid_spec=pltpu.PrefetchScalarGridSpec(num_scal...  29.8 us
    ppermute x6, waiting for transfers between devices, swap(): return (lax.ppermute(last, axis, up), lax.ppermute(first, axis, down))  22.6 us
    ppermute x6, starting transfers between devices, swap(): return (lax.ppermute(last, axis, up), lax.ppermute(first, axis, down))  14.5 us
    pallas_call x1, Pallas kernels, tail_kernel(): pl.pallas_call(tail_body, grid=(8,), in_specs=[tokens_of(model), tokens_o...  14.3 us
    ppermute x1, starting transfers between devices, other_core(): return lax.ppermute(array, 'lon', [(i, i ^ 1) for i in range(16)])  6.79 us
    all_to_all x1, starting transfers between devices, shards(): lax.all_to_all(halves, BOTH, 0, 0, axis_index_groups=chip_groups(), tiled...  6.04 us
    unnamed x14, local copies, waits for them, and re-layouts  3.04 us
    ppermute x1, waiting for transfers between devices, other_core(): return lax.ppermute(array, 'lon', [(i, i ^ 1) for i in range(16)])  3.04 us
  transfers between devices with their start and end apart: 8, of which 4 were waited for; matrix products, arithmetic and copies ran while one was open for 3% of the time, Pallas kernels for 13%

profile of v6, /device:TPU:1, one launch (start us, length us, event | category | flops | bytes accessed | tf_op | source)
XLA Modules:
  0.0 107.6 jit_solution(1421874427467925813)
XLA Ops:
  0.6 0.9 slice_bitcast_fusion
  1.5 1.3 %collective-permute-start.1 = (bf16[64,512]{1,0:T(8,128)(2,1)S(1)}, bf16[64,512]{1,0:T(8,128)(2,1)S(1)}, u32[]{:S(2)}, u32[]{:S(2)}) collective-permute-start(bf16[64,512]{1,0:T(8,128)(2,1)S(1)} %get-tuple-element.36), channel_id=1, source_target_pairs={{16,0},{32,16},{48,32},{64,48},{80,64},{96,80},{112,96},{17,1},{33... | collective-permute-start | bytes 196616 | tf_op jit(solution)/shard_map/ppermute | solution.py:396
  2.8 4.7 %collective-permute-start = (bf16[64,512]{1,0:T(8,128)(2,1)S(1)}, bf16[64,512]{1,0:T(8,128)(2,1)S(1)}, u32[]{:S(2)}, u32[]{:S(2)}) collective-permute-start(bf16[64,512]{1,0:T(8,128)(2,1)S(1)} %get-tuple-element.37), channel_id=1, source_target_pairs={{0,16},{16,32},{32,48},{48,64},{64,80},{80,96},{96,112},{1,17},{17... | collective-permute-start | bytes 196616 | tf_op jit(solution)/shard_map/ppermute | solution.py:396
  7.5 0.9 fusion.2
  8.4 1.0 fusion.1
  9.4 1.0 fusion
  10.6 0.1 concatenate.7
  10.8 1.3 %collective-permute-start.3 = (bf16[80,512]{1,0:T(8,128)(2,1)S(1)}, bf16[80,512]{1,0:T(8,128)(2,1)S(1)}, u32[]{:S(2)}, u32[]{:S(2)}) collective-permute-start(bf16[80,512]{1,0:T(8,128)(2,1)S(1)} %concatenate.7), channel_id=1, source_target_pairs={{1,0},{2,1},{3,2},{4,3},{5,4},{6,5},{7,6},{8,7},{9,8},{10,9},{11,1... | collective-permute-start | bytes 245768 | tf_op jit(solution)/shard_map/ppermute | solution.py:396
  12.2 3.0 %collective-permute-start.2 = (bf16[80,512]{1,0:T(8,128)(2,1)S(1)}, bf16[80,512]{1,0:T(8,128)(2,1)S(1)}, u32[]{:S(2)}, u32[]{:S(2)}) collective-permute-start(bf16[80,512]{1,0:T(8,128)(2,1)S(1)} %concatenate.6), channel_id=1, source_target_pairs={{0,1},{1,2},{2,3},{3,4},{4,5},{5,6},{6,7},{7,8},{8,9},{9,10},{10,1... | collective-permute-start | bytes 245768 | tf_op jit(solution)/shard_map/ppermute | solution.py:396
  15.3 1.9 %collective-permute-done.3.right = bf16[80,512]{1,0:T(8,128)(2,1)S(1)} collective-permute-done((bf16[80,512]{1,0:T(8,128)(2,1)S(1)}, bf16[80,512]{1,0:T(8,128)(2,1)S(1)}, u32[]{:S(2)}, u32[]{:S(2)}) %collective-permute-start.3) | collective-permute-done | bytes 81952 | tf_op jit(solution)/shard_map/ppermute | solution.py:396
  17.2 1.6 %collective-permute-done.2.left = bf16[80,512]{1,0:T(8,128)(2,1)S(1)} collective-permute-done((bf16[80,512]{1,0:T(8,128)(2,1)S(1)}, bf16[80,512]{1,0:T(8,128)(2,1)S(1)}, u32[]{:S(2)}, u32[]{:S(2)}) %collective-permute-start.2) | collective-permute-done | bytes 81952 | tf_op jit(solution)/shard_map/ppermute | solution.py:396
  18.7 1.0 copy-done
  19.8 1.2 %copy-done.1 = bf16[1024,512]{1,0:T(8,128)(2,1)S(1)} copy-done((bf16[1024,512]{1,0:T(8,128)(2,1)S(1)}, bf16[1024,512]{1,0:T(8,128)(2,1)}, u32[]{:S(2)}) %copy-start.1) | copy-done | bytes 1048600
  21.0 29.8 %main.1 = (bf16[2048,1024]{1,0:T(8,128)(2,1)}, bf16[2048,512]{1,0:T(8,128)(2,1)S(1)}, bf16[64,512]{1,0:T(8,128)(2,1)S(1)}, bf16[160,512]{1,0:T(8,128)(2,1)S(1)},...) custom-call(s32[1]{0:T(128)} %bitcast.1.core, ...), custom_call_target="tpu_custom_call" | custom-call | flops 21474836480 | bytes 37748736 | tf_op jit(solution)/shard_map/main/pallas_call | solution.py:210
  50.9 6.8 %collective-permute-start.6 = (bf16[4,4,4,96,128]{4,3,2,1,0:T(8,128)(2,1)S(1)}, bf16[4,4,4,96,128]{4,3,2,1,0:T(8,128)(2,1)S(1)}, u32[]{:S(2)}, u32[]{:S(2)}) collective-permute-start(bf16[4,4,4,96,128]{4,3,2,1,0:T(8,128)(2,1)S(1)} %get-tuple-element.23), channel_id=1, source_target_pairs={{0,1},{1,0},{2,3},{3,2},{4,5},{5,4},{6,7},{7,6},{8,9},{9,8},{10,11... | collective-permute-start | bytes 4718600 | tf_op jit(solution)/shard_map/ppermute | solution.py:429
  57.7 3.0 %collective-permute-done.6 = bf16[4,4,4,96,128]{4,3,2,1,0:T(8,128)(2,1)S(1)} collective-permute-done((bf16[4,4,4,96,128]{4,3,2,1,0:T(8,128)(2,1)S(1)}, bf16[4,4,4,96,128]{4,3,2,1,0:T(8,128)(2,1)S(1)}, u32[]{:S(2)}, u32[]{:S(2)}) %collective-permute-start.6) | collective-permute-done | bytes 1572896 | tf_op jit(solution)/shard_map/ppermute | solution.py:429
  60.7 1.6 %add_convert_fusion = bf16[4,4,4,96,128]{4,3,2,1,0:T(8,128)(2,1)} fusion(bf16[4,4,4,96,128]{4,3,2,1,0:T(8,128)(2,1)S(1)} %collective-permute-done.6, bf16[4,4,4,96,128]{4,3,2,1,0:T(8,128)(2,1)S(1)} %get-tuple-element.22), kind=kLoop, calls=%fused_computation | loop fusion | flops 3145728 | bytes 4718592 | tf_op jit(solution)/shard_map/convert_element_type | solution.py:446
  62.3 6.0 %all-to-all-start = ((bf16[64,96,128]{2,1,0:T(8,128)(2,1)}), bf16[64,96,128]{2,1,0:T(8,128)(2,1)S(1)}, u32[]{:S(2)}, u32[]{:S(2)}) async-start(bf16[64,96,128]{2,1,0:T(8,128)(2,1)} %bitcast.20), calls=%async_computation | async-start | bytes 3145728 | tf_op jit(solution)/shard_map/all_to_all | solution.py:447
  68.3 2.9 %collective-permute-start.4 = (bf16[160,512]{1,0:T(8,128)(2,1)S(1)}, bf16[160,512]{1,0:T(8,128)(2,1)S(1)}, u32[]{:S(2)}, u32[]{:S(2)}) collective-permute-start(bf16[160,512]{1,0:T(8,128)(2,1)S(1)} %get-tuple-element.18), channel_id=1, source_target_pairs={{0,16},{16,32},{32,48},{48,64},{64,80},{80,96},{96,112},{1,17},{17... | collective-permute-start | bytes 491528 | tf_op jit(solution)/shard_map/ppermute | solution.py:396
  71.3 1.3 %collective-permute-start.5 = (bf16[160,512]{1,0:T(8,128)(2,1)S(1)}, bf16[160,512]{1,0:T(8,128)(2,1)S(1)}, u32[]{:S(2)}, u32[]{:S(2)}) collective-permute-start(bf16[160,512]{1,0:T(8,128)(2,1)S(1)} %get-tuple-element.19), channel_id=1, source_target_pairs={{16,0},{32,16},{48,32},{64,48},{80,64},{96,80},{112,96},{17,1},{33... | collective-permute-start | bytes 491528 | tf_op jit(solution)/shard_map/ppermute | solution.py:396
  72.6 19.1 %collective-permute-done.4.before = bf16[160,512]{1,0:T(8,128)(2,1)S(1)} collective-permute-done((bf16[160,512]{1,0:T(8,128)(2,1)S(1)}, bf16[160,512]{1,0:T(8,128)(2,1)S(1)}, u32[]{:S(2)}, u32[]{:S(2)}) %collective-permute-start.4) | collective-permute-done | bytes 163872 | tf_op jit(solution)/shard_map/ppermute | solution.py:396
  91.7 0.7 copy-done.4
  92.4 14.3 %tail.1 = (bf16[2048,512]{1,0:T(8,128)(2,1)}, f32[512,512]{1,0:T(8,128)}) custom-call(bf16[2048,512]{1,0:T(8,128)(2,1)} %bitcast.40, bf16[2048,1024]{1,0:T(8,128)(2,1)} %get-tuple-element.15.act, bf16[1024,512]{1,0:T(8,128)(2,1)} %w_out.1, bf16[16,128,512]{2,1,0:T(8,128)(2,1)} %bitcast.35, bf16[64,512]{1,0:T(8,128)(2,1)} %copy-done.3, ...), custom_call_target="tpu_custom_call" | custom-call | flops 7516192768 | bytes 23068672 | tf_op jit(solution)/shard_map/tail/pallas_call | solution.py:339
  106.8 0.9 sum_blocks.1
  (31 shorter events, 0.3 us)
Async XLA Ops:
  1.5 9.1 %collective-permute-start.1 = (bf16[64,512]{1,0:T(8,128)(2,1)S(1)}, bf16[64,512]{1,0:T(8,128)(2,1)S(1)}, u32[]{:S(2)}, u32[]{:S(2)}) collective-permute-start(bf16[64,512]{1,0:T(8,128)(2,1)S(1)} %get-tuple-element.36), channel_id=1, source_target_pairs={{16,0},{32,16},{48,32},{64,48},{80,64},{96,80},{112,96},{17,1},{33... | collective-permute-start | bytes 196616 | tf_op jit(solution)/shard_map/ppermute | solution.py:396
  2.8 7.8 %collective-permute-start = (bf16[64,512]{1,0:T(8,128)(2,1)S(1)}, bf16[64,512]{1,0:T(8,128)(2,1)S(1)}, u32[]{:S(2)}, u32[]{:S(2)}) collective-permute-start(bf16[64,512]{1,0:T(8,128)(2,1)S(1)} %get-tuple-element.37), channel_id=1, source_target_pairs={{0,16},{16,32},{32,48},{48,64},{64,80},{80,96},{96,112},{1,17},{17... | collective-permute-start | bytes 196616 | tf_op jit(solution)/shard_map/ppermute | solution.py:396
  10.8 6.4 %collective-permute-start.3 = (bf16[80,512]{1,0:T(8,128)(2,1)S(1)}, bf16[80,512]{1,0:T(8,128)(2,1)S(1)}, u32[]{:S(2)}, u32[]{:S(2)}) collective-permute-start(bf16[80,512]{1,0:T(8,128)(2,1)S(1)} %concatenate.7), channel_id=1, source_target_pairs={{1,0},{2,1},{3,2},{4,3},{5,4},{6,5},{7,6},{8,7},{9,8},{10,9},{11,1... | collective-permute-start | bytes 245768 | tf_op jit(solution)/shard_map/ppermute | solution.py:396
  12.2 6.5 %collective-permute-start.2 = (bf16[80,512]{1,0:T(8,128)(2,1)S(1)}, bf16[80,512]{1,0:T(8,128)(2,1)S(1)}, u32[]{:S(2)}, u32[]{:S(2)}) collective-permute-start(bf16[80,512]{1,0:T(8,128)(2,1)S(1)} %concatenate.6), channel_id=1, source_target_pairs={{0,1},{1,2},{2,3},{3,4},{4,5},{5,6},{6,7},{7,8},{8,9},{9,10},{10,1... | collective-permute-start | bytes 245768 | tf_op jit(solution)/shard_map/ppermute | solution.py:396
  18.7 1.0 copy-start
  19.8 1.2 %copy-start.1 = (bf16[1024,512]{1,0:T(8,128)(2,1)S(1)}, bf16[1024,512]{1,0:T(8,128)(2,1)}, u32[]{:S(2)}) copy-start(bf16[1024,512]{1,0:T(8,128)(2,1)} %w_out.1) | copy-start | bytes 3145732
  50.8 11.5 %copy-start.2 = (bf16[2048,512]{1,0:T(8,128)(2,1)}, bf16[2048,512]{1,0:T(8,128)(2,1)S(1)}, u32[]{:S(2)}) copy-start(bf16[2048,512]{1,0:T(8,128)(2,1)S(1)} %get-tuple-element.16) | copy-start | bytes 6291460
  50.8 11.4 %copy-start.3 = (bf16[64,512]{1,0:T(8,128)(2,1)}, bf16[64,512]{1,0:T(8,128)(2,1)S(1)}, u32[]{:S(2)}) copy-start(bf16[64,512]{1,0:T(8,128)(2,1)S(1)} %get-tuple-element.17.edge) | copy-start | bytes 196612
  50.9 9.8 %collective-permute-start.6 = (bf16[4,4,4,96,128]{4,3,2,1,0:T(8,128)(2,1)S(1)}, bf16[4,4,4,96,128]{4,3,2,1,0:T(8,128)(2,1)S(1)}, u32[]{:S(2)}, u32[]{:S(2)}) collective-permute-start(bf16[4,4,4,96,128]{4,3,2,1,0:T(8,128)(2,1)S(1)} %get-tuple-element.23), channel_id=1, source_target_pairs={{0,1},{1,0},{2,3},{3,2},{4,5},{5,4},{6,7},{7,6},{8,9},{9,8},{10,11... | collective-permute-start | bytes 4718600 | tf_op jit(solution)/shard_map/ppermute | solution.py:429
  62.3 44.5 %all-to-all-start = ((bf16[64,96,128]{2,1,0:T(8,128)(2,1)}), bf16[64,96,128]{2,1,0:T(8,128)(2,1)S(1)}, u32[]{:S(2)}, u32[]{:S(2)}) async-start(bf16[64,96,128]{2,1,0:T(8,128)(2,1)} %bitcast.20), calls=%async_computation | async-start | bytes 3145728 | tf_op jit(solution)/shard_map/all_to_all | solution.py:447
  68.3 23.3 %collective-permute-start.4 = (bf16[160,512]{1,0:T(8,128)(2,1)S(1)}, bf16[160,512]{1,0:T(8,128)(2,1)S(1)}, u32[]{:S(2)}, u32[]{:S(2)}) collective-permute-start(bf16[160,512]{1,0:T(8,128)(2,1)S(1)} %get-tuple-element.18), channel_id=1, source_target_pairs={{0,16},{16,32},{32,48},{48,64},{64,80},{80,96},{96,112},{1,17},{17... | collective-permute-start | bytes 491528 | tf_op jit(solution)/shard_map/ppermute | solution.py:396
  71.3 20.4 %collective-permute-start.5 = (bf16[160,512]{1,0:T(8,128)(2,1)S(1)}, bf16[160,512]{1,0:T(8,128)(2,1)S(1)}, u32[]{:S(2)}, u32[]{:S(2)}) collective-permute-start(bf16[160,512]{1,0:T(8,128)(2,1)S(1)} %get-tuple-element.19), channel_id=1, source_target_pairs={{16,0},{32,16},{48,32},{64,48},{80,64},{96,80},{112,96},{17,1},{33... | collective-permute-start | bytes 491528 | tf_op jit(solution)/shard_map/ppermute | solution.py:396
  91.6 0.7 copy-start.4
  91.6 0.8 copy-start.5

commit v7 on v6

--- a/solution.py
+++ b/solution.py
@@ -222,8 +222,8 @@
                 pl.BlockSpec((1, 4, half, width), lambda i, c: kernel_row(i, 3)),
                 tokens_of(model),
                 tokens_of(model),
-                pl.BlockSpec(memory_space=pl.ANY),
-                pl.BlockSpec(memory_space=pl.ANY),
+                pl.BlockSpec(memory_space=pltpu.HBM),
+                pl.BlockSpec(memory_space=pltpu.HBM),
             ],
             out_specs=[
                 tokens_of(hidden),
@@ -393,7 +393,9 @@
     devices = lax.axis_size(axis)
     up = [(i, (i + 1) % devices) for i in range(devices if wrap else devices - 1)]
     down = [(j, i) for i, j in up]
-    return lax.ppermute(last, axis, up), lax.ppermute(first, axis, down)
+    one = lax.ppermute(last, axis, up)
+    other = lax.ppermute(first, axis, down)
+    return one, other
 
 
 def halos(latents, tokens, cot):

time: 110 us -> 110 us (level)
  no operation moved by 1% of the time
where the time goes in v7:
time: 110 us; the launch traced here: 108 us
  Pallas kernels  45 us (41%)
  starting transfers between devices  27.3 us (25%)
  waiting for transfers between devices  25.6 us (23%)
  local copies, waits for them, and re-layouts  7.17 us (7%)
  other arithmetic  1.6 us (1%)
    pallas_call x1, Pallas kernels, main_kernel(): pl.pallas_call(main_body, grid_spec=pltpu.PrefetchScalarGridSpec(num_scal...  29.8 us
    ppermute x3, waiting for transfers between devices, swap(): one = lax.ppermute(last, axis, up)  20.7 us
    pallas_call x1, Pallas kernels, tail_kernel(): pl.pallas_call(tail_body, grid=(8,), in_specs=[tokens_of(model), tokens_o...  14.3 us
    ppermute x3, starting transfers between devices, swap(): one = lax.ppermute(last, axis, up)  10.6 us
    ppermute x1, starting transfers between devices, other_core(): return lax.ppermute(array, 'lon', [(i, i ^ 1) for i in range(16)])  6.79 us
    all_to_all x1, starting transfers between devices, shards(): lax.all_to_all(halves, BOTH, 0, 0, axis_index_groups=chip_groups(), tiled...  6.04 us
    ppermute x3, starting transfers between devices, swap(): other = lax.ppermute(first, axis, down)  3.93 us
    unnamed x14, local copies, waits for them, and re-layouts  3.04 us
  transfers between devices with their start and end apart: 8, of which 4 were waited for; matrix products, arithmetic and copies ran while one was open for 3% of the time, Pallas kernels for 13%

profile of v7, /device:TPU:1, one launch (start us, length us, event | category | flops | bytes accessed | tf_op | source)
XLA Modules:
  0.0 107.6 jit_solution(1421874427467925813)
XLA Ops:
  0.6 0.9 slice_bitcast_fusion
  1.5 1.3 %collective-permute-start.1 = (bf16[64,512]{1,0:T(8,128)(2,1)S(1)}, bf16[64,512]{1,0:T(8,128)(2,1)S(1)}, u32[]{:S(2)}, u32[]{:S(2)}) collective-permute-start(bf16[64,512]{1,0:T(8,128)(2,1)S(1)} %get-tuple-element.36), channel_id=1, source_target_pairs={{16,0},{32,16},{48,32},{64,48},{80,64},{96,80},{112,96},{17,1},{33... | collective-permute-start | bytes 196616 | tf_op jit(solution)/shard_map/ppermute | solution.py:397
  2.8 4.7 %collective-permute-start = (bf16[64,512]{1,0:T(8,128)(2,1)S(1)}, bf16[64,512]{1,0:T(8,128)(2,1)S(1)}, u32[]{:S(2)}, u32[]{:S(2)}) collective-permute-start(bf16[64,512]{1,0:T(8,128)(2,1)S(1)} %get-tuple-element.37), channel_id=1, source_target_pairs={{0,16},{16,32},{32,48},{48,64},{64,80},{80,96},{96,112},{1,17},{17... | collective-permute-start | bytes 196616 | tf_op jit(solution)/shard_map/ppermute | solution.py:396
  7.5 0.9 fusion.2
  8.4 1.0 fusion.1
  9.4 1.0 fusion
  10.6 0.1 concatenate.7
  10.8 1.3 %collective-permute-start.3 = (bf16[80,512]{1,0:T(8,128)(2,1)S(1)}, bf16[80,512]{1,0:T(8,128)(2,1)S(1)}, u32[]{:S(2)}, u32[]{:S(2)}) collective-permute-start(bf16[80,512]{1,0:T(8,128)(2,1)S(1)} %concatenate.7), channel_id=1, source_target_pairs={{1,0},{2,1},{3,2},{4,3},{5,4},{6,5},{7,6},{8,7},{9,8},{10,9},{11,1... | collective-permute-start | bytes 245768 | tf_op jit(solution)/shard_map/ppermute | solution.py:397
  12.2 3.0 %collective-permute-start.2 = (bf16[80,512]{1,0:T(8,128)(2,1)S(1)}, bf16[80,512]{1,0:T(8,128)(2,1)S(1)}, u32[]{:S(2)}, u32[]{:S(2)}) collective-permute-start(bf16[80,512]{1,0:T(8,128)(2,1)S(1)} %concatenate.6), channel_id=1, source_target_pairs={{0,1},{1,2},{2,3},{3,4},{4,5},{5,6},{6,7},{7,8},{8,9},{9,10},{10,1... | collective-permute-start | bytes 245768 | tf_op jit(solution)/shard_map/ppermute | solution.py:396
  15.3 1.9 %collective-permute-done.3.right = bf16[80,512]{1,0:T(8,128)(2,1)S(1)} collective-permute-done((bf16[80,512]{1,0:T(8,128)(2,1)S(1)}, bf16[80,512]{1,0:T(8,128)(2,1)S(1)}, u32[]{:S(2)}, u32[]{:S(2)}) %collective-permute-start.3) | collective-permute-done | bytes 81952 | tf_op jit(solution)/shard_map/ppermute | solution.py:397
  17.2 1.6 %collective-permute-done.2.left = bf16[80,512]{1,0:T(8,128)(2,1)S(1)} collective-permute-done((bf16[80,512]{1,0:T(8,128)(2,1)S(1)}, bf16[80,512]{1,0:T(8,128)(2,1)S(1)}, u32[]{:S(2)}, u32[]{:S(2)}) %collective-permute-start.2) | collective-permute-done | bytes 81952 | tf_op jit(solution)/shard_map/ppermute | solution.py:396
  18.7 1.0 copy-done
  19.8 1.2 %copy-done.1 = bf16[1024,512]{1,0:T(8,128)(2,1)S(1)} copy-done((bf16[1024,512]{1,0:T(8,128)(2,1)S(1)}, bf16[1024,512]{1,0:T(8,128)(2,1)}, u32[]{:S(2)}) %copy-start.1) | copy-done | bytes 1048600
  21.0 29.8 %main.1 = (bf16[2048,1024]{1,0:T(8,128)(2,1)}, bf16[2048,512]{1,0:T(8,128)(2,1)S(1)}, bf16[64,512]{1,0:T(8,128)(2,1)S(1)}, bf16[160,512]{1,0:T(8,128)(2,1)S(1)},...) custom-call(s32[1]{0:T(128)} %bitcast.1.core, ...), custom_call_target="tpu_custom_call" | custom-call | flops 21474836480 | bytes 37748736 | tf_op jit(solution)/shard_map/main/pallas_call | solution.py:210
  50.9 6.8 %collective-permute-start.6 = (bf16[4,4,4,96,128]{4,3,2,1,0:T(8,128)(2,1)S(1)}, bf16[4,4,4,96,128]{4,3,2,1,0:T(8,128)(2,1)S(1)}, u32[]{:S(2)}, u32[]{:S(2)}) collective-permute-start(bf16[4,4,4,96,128]{4,3,2,1,0:T(8,128)(2,1)S(1)} %get-tuple-element.23), channel_id=1, source_target_pairs={{0,1},{1,0},{2,3},{3,2},{4,5},{5,4},{6,7},{7,6},{8,9},{9,8},{10,11... | collective-permute-start | bytes 4718600 | tf_op jit(solution)/shard_map/ppermute | solution.py:431
  57.7 3.0 %collective-permute-done.6 = bf16[4,4,4,96,128]{4,3,2,1,0:T(8,128)(2,1)S(1)} collective-permute-done((bf16[4,4,4,96,128]{4,3,2,1,0:T(8,128)(2,1)S(1)}, bf16[4,4,4,96,128]{4,3,2,1,0:T(8,128)(2,1)S(1)}, u32[]{:S(2)}, u32[]{:S(2)}) %collective-permute-start.6) | collective-permute-done | bytes 1572896 | tf_op jit(solution)/shard_map/ppermute | solution.py:431
  60.7 1.6 %add_convert_fusion = bf16[4,4,4,96,128]{4,3,2,1,0:T(8,128)(2,1)} fusion(bf16[4,4,4,96,128]{4,3,2,1,0:T(8,128)(2,1)S(1)} %collective-permute-done.6, bf16[4,4,4,96,128]{4,3,2,1,0:T(8,128)(2,1)S(1)} %get-tuple-element.22), kind=kLoop, calls=%fused_computation | loop fusion | flops 3145728 | bytes 4718592 | tf_op jit(solution)/shard_map/convert_element_type | solution.py:448
  62.3 6.0 %all-to-all-start = ((bf16[64,96,128]{2,1,0:T(8,128)(2,1)}), bf16[64,96,128]{2,1,0:T(8,128)(2,1)S(1)}, u32[]{:S(2)}, u32[]{:S(2)}) async-start(bf16[64,96,128]{2,1,0:T(8,128)(2,1)} %bitcast.20), calls=%async_computation | async-start | bytes 3145728 | tf_op jit(solution)/shard_map/all_to_all | solution.py:449
  68.3 2.9 %collective-permute-start.4 = (bf16[160,512]{1,0:T(8,128)(2,1)S(1)}, bf16[160,512]{1,0:T(8,128)(2,1)S(1)}, u32[]{:S(2)}, u32[]{:S(2)}) collective-permute-start(bf16[160,512]{1,0:T(8,128)(2,1)S(1)} %get-tuple-element.18), channel_id=1, source_target_pairs={{0,16},{16,32},{32,48},{48,64},{64,80},{80,96},{96,112},{1,17},{17... | collective-permute-start | bytes 491528 | tf_op jit(solution)/shard_map/ppermute | solution.py:396
  71.3 1.3 %collective-permute-start.5 = (bf16[160,512]{1,0:T(8,128)(2,1)S(1)}, bf16[160,512]{1,0:T(8,128)(2,1)S(1)}, u32[]{:S(2)}, u32[]{:S(2)}) collective-permute-start(bf16[160,512]{1,0:T(8,128)(2,1)S(1)} %get-tuple-element.19), channel_id=1, source_target_pairs={{16,0},{32,16},{48,32},{64,48},{80,64},{96,80},{112,96},{17,1},{33... | collective-permute-start | bytes 491528 | tf_op jit(solution)/shard_map/ppermute | solution.py:397
  72.6 19.1 %collective-permute-done.4.before = bf16[160,512]{1,0:T(8,128)(2,1)S(1)} collective-permute-done((bf16[160,512]{1,0:T(8,128)(2,1)S(1)}, bf16[160,512]{1,0:T(8,128)(2,1)S(1)}, u32[]{:S(2)}, u32[]{:S(2)}) %collective-permute-start.4) | collective-permute-done | bytes 163872 | tf_op jit(solution)/shard_map/ppermute | solution.py:396
  91.7 0.7 copy-done.4
  92.4 14.3 %tail.1 = (bf16[2048,512]{1,0:T(8,128)(2,1)}, f32[512,512]{1,0:T(8,128)}) custom-call(bf16[2048,512]{1,0:T(8,128)(2,1)} %bitcast.40, bf16[2048,1024]{1,0:T(8,128)(2,1)} %get-tuple-element.15.act, bf16[1024,512]{1,0:T(8,128)(2,1)} %w_out.1, bf16[16,128,512]{2,1,0:T(8,128)(2,1)} %bitcast.35, bf16[64,512]{1,0:T(8,128)(2,1)} %copy-done.3, ...), custom_call_target="tpu_custom_call" | custom-call | flops 7516192768 | bytes 23068672 | tf_op jit(solution)/shard_map/tail/pallas_call | solution.py:339
  106.8 0.9 sum_blocks.1
  (31 shorter events, 0.3 us)
Async XLA Ops:
  1.5 9.1 %collective-permute-start.1 = (bf16[64,512]{1,0:T(8,128)(2,1)S(1)}, bf16[64,512]{1,0:T(8,128)(2,1)S(1)}, u32[]{:S(2)}, u32[]{:S(2)}) collective-permute-start(bf16[64,512]{1,0:T(8,128)(2,1)S(1)} %get-tuple-element.36), channel_id=1, source_target_pairs={{16,0},{32,16},{48,32},{64,48},{80,64},{96,80},{112,96},{17,1},{33... | collective-permute-start | bytes 196616 | tf_op jit(solution)/shard_map/ppermute | solution.py:397
  2.8 7.8 %collective-permute-start = (bf16[64,512]{1,0:T(8,128)(2,1)S(1)}, bf16[64,512]{1,0:T(8,128)(2,1)S(1)}, u32[]{:S(2)}, u32[]{:S(2)}) collective-permute-start(bf16[64,512]{1,0:T(8,128)(2,1)S(1)} %get-tuple-element.37), channel_id=1, source_target_pairs={{0,16},{16,32},{32,48},{48,64},{64,80},{80,96},{96,112},{1,17},{17... | collective-permute-start | bytes 196616 | tf_op jit(solution)/shard_map/ppermute | solution.py:396
  10.8 6.4 %collective-permute-start.3 = (bf16[80,512]{1,0:T(8,128)(2,1)S(1)}, bf16[80,512]{1,0:T(8,128)(2,1)S(1)}, u32[]{:S(2)}, u32[]{:S(2)}) collective-permute-start(bf16[80,512]{1,0:T(8,128)(2,1)S(1)} %concatenate.7), channel_id=1, source_target_pairs={{1,0},{2,1},{3,2},{4,3},{5,4},{6,5},{7,6},{8,7},{9,8},{10,9},{11,1... | collective-permute-start | bytes 245768 | tf_op jit(solution)/shard_map/ppermute | solution.py:397
  12.2 6.5 %collective-permute-start.2 = (bf16[80,512]{1,0:T(8,128)(2,1)S(1)}, bf16[80,512]{1,0:T(8,128)(2,1)S(1)}, u32[]{:S(2)}, u32[]{:S(2)}) collective-permute-start(bf16[80,512]{1,0:T(8,128)(2,1)S(1)} %concatenate.6), channel_id=1, source_target_pairs={{0,1},{1,2},{2,3},{3,4},{4,5},{5,6},{6,7},{7,8},{8,9},{9,10},{10,1... | collective-permute-start | bytes 245768 | tf_op jit(solution)/shard_map/ppermute | solution.py:396
  18.7 1.0 copy-start
  19.8 1.2 %copy-start.1 = (bf16[1024,512]{1,0:T(8,128)(2,1)S(1)}, bf16[1024,512]{1,0:T(8,128)(2,1)}, u32[]{:S(2)}) copy-start(bf16[1024,512]{1,0:T(8,128)(2,1)} %w_out.1) | copy-start | bytes 3145732
  50.8 11.5 %copy-start.2 = (bf16[2048,512]{1,0:T(8,128)(2,1)}, bf16[2048,512]{1,0:T(8,128)(2,1)S(1)}, u32[]{:S(2)}) copy-start(bf16[2048,512]{1,0:T(8,128)(2,1)S(1)} %get-tuple-element.16) | copy-start | bytes 6291460
  50.8 11.4 %copy-start.3 = (bf16[64,512]{1,0:T(8,128)(2,1)}, bf16[64,512]{1,0:T(8,128)(2,1)S(1)}, u32[]{:S(2)}) copy-start(bf16[64,512]{1,0:T(8,128)(2,1)S(1)} %get-tuple-element.17.edge) | copy-start | bytes 196612
  50.9 9.8 %collective-permute-start.6 = (bf16[4,4,4,96,128]{4,3,2,1,0:T(8,128)(2,1)S(1)}, bf16[4,4,4,96,128]{4,3,2,1,0:T(8,128)(2,1)S(1)}, u32[]{:S(2)}, u32[]{:S(2)}) collective-permute-start(bf16[4,4,4,96,128]{4,3,2,1,0:T(8,128)(2,1)S(1)} %get-tuple-element.23), channel_id=1, source_target_pairs={{0,1},{1,0},{2,3},{3,2},{4,5},{5,4},{6,7},{7,6},{8,9},{9,8},{10,11... | collective-permute-start | bytes 4718600 | tf_op jit(solution)/shard_map/ppermute | solution.py:431
  62.3 44.5 %all-to-all-start = ((bf16[64,96,128]{2,1,0:T(8,128)(2,1)}), bf16[64,96,128]{2,1,0:T(8,128)(2,1)S(1)}, u32[]{:S(2)}, u32[]{:S(2)}) async-start(bf16[64,96,128]{2,1,0:T(8,128)(2,1)} %bitcast.20), calls=%async_computation | async-start | bytes 3145728 | tf_op jit(solution)/shard_map/all_to_all | solution.py:449
  68.3 23.3 %collective-permute-start.4 = (bf16[160,512]{1,0:T(8,128)(2,1)S(1)}, bf16[160,512]{1,0:T(8,128)(2,1)S(1)}, u32[]{:S(2)}, u32[]{:S(2)}) collective-permute-start(bf16[160,512]{1,0:T(8,128)(2,1)S(1)} %get-tuple-element.18), channel_id=1, source_target_pairs={{0,16},{16,32},{32,48},{48,64},{64,80},{80,96},{96,112},{1,17},{17... | collective-permute-start | bytes 491528 | tf_op jit(solution)/shard_map/ppermute | solution.py:396
  71.3 20.4 %collective-permute-start.5 = (bf16[160,512]{1,0:T(8,128)(2,1)S(1)}, bf16[160,512]{1,0:T(8,128)(2,1)S(1)}, u32[]{:S(2)}, u32[]{:S(2)}) collective-permute-start(bf16[160,512]{1,0:T(8,128)(2,1)S(1)} %get-tuple-element.19), channel_id=1, source_target_pairs={{16,0},{32,16},{48,32},{64,48},{80,64},{96,80},{112,96},{17,1},{33... | collective-permute-start | bytes 491528 | tf_op jit(solution)/shard_map/ppermute | solution.py:397
  91.6 0.7 copy-start.4
  91.6 0.8 copy-start.5

commit v8 on v7

--- a/solution.py
+++ b/solution.py
@@ -28,7 +28,7 @@
 
 
 def main_body(
-    core, lat, before, after, left, right, w_a, w_b, tokens, cot, w_in_hbm, w_out_hbm,
+    core, lat, before, after, left, right, w_a, w_b, tokens, cot, a_own, w_in_hbm, w_out_hbm,
     act_out, up_cot, up_cot_edge, first_row, last_row, keep, send,
     sources, edges, tokens_edge, cot_edge, w_in, w_out, up, act, pre, pre_edge,
     turned, sems,
@@ -37,7 +37,7 @@
     rows, cols, width = lat.shape
     hidden, model = w_out.shape
     half_model = model // 2
-    block = act_out.shape[0]
+    block = up_cot.shape[0]
     count = act.shape[0]
     fine_cols = 2 * cols
     copies = [
@@ -47,10 +47,16 @@
         )
     ]
 
+    act_copy = pltpu.make_async_copy(act, act_out, sems.at[2])
+
     @pl.when(step == 1)
     def _():
         for copy in copies:
             copy.start()
+
+    @pl.when(step == 9)
+    def _():
+        act_copy.start()
 
     @pl.when(step == 0)
     def _():
@@ -110,13 +116,13 @@
         for copy in copies:
             copy.wait()
 
-    def network(tokens_of, up_of, cot_of, span):
+    def network(tokens_of, up_of, a_of, span):
         h = dot_nn(tokens_of(), w_in[:model, span])
         h += dot_nn(up_of(0), w_in[model : model + half_model, span])
         h += dot_nn(up_of(1), w_in[model + half_model :, span])
         g = 0.5 * jnp.tanh(0.5 * h) + 0.5
         y = h * g
-        a = dot_nt(cot_of(), w_out[span, :])
+        a = a_of()
         return y.astype(BF16), (a * (g + y * (1.0 - g))).astype(BF16)
 
     @pl.when(step == 4)
@@ -124,7 +130,10 @@
         for n in range(0, hidden, 256):
             span = slice(n, n + 256)
             _, pre_edge[:, span] = network(
-                lambda: tokens_edge[...], lambda i: up[i, count + fine_cols :], lambda: cot_edge[...], span
+                lambda: tokens_edge[...],
+                lambda i: up[i, count + fine_cols :],
+                lambda: dot_nt(cot_edge[...], w_out[span, :]),
+                span,
             )
         value = dot_nt(pre_edge[...], w_in[model:, :]).astype(BF16)
         up_cot_edge[...] = value
@@ -139,10 +148,12 @@
         for n in range(0, hidden, 256):
             span = slice(n, n + 256)
             wide, grad = network(
-                lambda: tokens[...], lambda i: up[i, at], lambda: cot[...], span
+                lambda: tokens[...],
+                lambda i: up[i, at],
+                lambda: a_own[:, span].astype(F32),
+                span,
             )
             act[at, span] = wide
-            act_out[:, span] = wide
             pre[at, span] = grad
         turned[0:model, at] = tokens[...].T
         turned[model : model + half_model, at] = up[0, at].T
@@ -192,8 +203,12 @@
                         mine == 0, second, first
                     ).astype(BF16)
 
-
-def main_kernel(core, lat, before, after, left, right, weight, tokens, cot, w_in, w_out):
+    @pl.when(step == 12)
+    def _():
+        act_copy.wait()
+
+
+def main_kernel(core, lat, before, after, left, right, weight, tokens, cot, a_own, w_in, w_out):
     rows, cols, width = lat.shape
     model = weight.shape[0] // 16
     half = model // 2
@@ -222,11 +237,12 @@
                 pl.BlockSpec((1, 4, half, width), lambda i, c: kernel_row(i, 3)),
                 tokens_of(model),
                 tokens_of(model),
+                tokens_of(hidden),
                 pl.BlockSpec(memory_space=pltpu.HBM),
                 pl.BlockSpec(memory_space=pltpu.HBM),
             ],
             out_specs=[
-                tokens_of(hidden),
+                pl.BlockSpec(memory_space=pl.ANY),
                 tokens_of(model),
                 whole(edge, model),
                 whole(pack, model),
@@ -246,7 +262,7 @@
                 pltpu.VMEM((count, hidden), BF16),
                 pltpu.VMEM((edge, hidden), BF16),
                 pltpu.VMEM((3 * model, count), BF16),
-                pltpu.SemaphoreType.DMA((2,)),
+                pltpu.SemaphoreType.DMA((3,)),
             ],
         ),
         out_shape=[
@@ -263,7 +279,7 @@
         name="main",
     )(
         core, lat, before, after, left, right, *[weight.reshape(4, 4, model, width)] * 2,
-        tokens, cot, w_in, w_out,
+        tokens, cot, a_own, w_in, w_out,
     )
 
 
@@ -439,9 +455,10 @@
     cot = cotangent.reshape(count, model)
 
     before, after, left, right = halos(latents, fine_tokens, cotangent)
+    a_own = dot_nt(cot, uniting_out).astype(BF16)
     act, up_cot, up_cot_edge, first_row, last_row, keep, send = main_kernel(
         core, latents, before, after, left, right, upsample_weight,
-        tokens, cot, uniting_in, uniting_out,
+        tokens, cot, a_own, uniting_in, uniting_out,
     )
     other = other_core(send)
     above, below = swap(last_row, first_row, "lat", False)

time: 110 us -> 109 us (level)
  matrix products: 0 us -> 6.37 us
  waiting for transfers between devices: 25.6 us -> 22.1 us
  local copies, waits for them, and re-layouts: 7.17 us -> 4.92 us
    dot_general x0 -> x1, matrix products: none -> 6.37 us  [dot_nt(): lax.dot_general(a, b, (((1,), (1,)), ((), ())), preferred_element_type=F32)]
    all_to_all x1, starting transfers between devices: 6.04 us -> 10.1 us  [shards(): lax.all_to_all(halves, BOTH, 0, 0, axis_index_groups=chip_groups(), tiled...]
    ppermute x1, starting transfers between devices: 6.79 us -> 2.83 us  [other_core(): return lax.ppermute(array, 'lon', [(i, i ^ 1) for i in range(16)])]
    unnamed x14, local copies, waits for them, and re-layouts: 3.04 us -> 0.79 us
    ppermute x3, waiting for transfers between devices: 1.91 us -> 0.01 us  [swap(): other = lax.ppermute(first, axis, down)]
    ppermute x3, waiting for transfers between devices: 20.7 us -> 19.1 us  [swap(): one = lax.ppermute(last, axis, up)]
    ppermute x3, starting transfers between devices: 3.93 us -> 2.66 us  [swap(): other = lax.ppermute(first, axis, down)]
    ppermute x3, starting transfers between devices: 10.6 us -> 11.8 us  [swap(): one = lax.ppermute(last, axis, up)]
  transfers between devices with their start and end apart: 8 -> 8, of which waited for: 4 -> 2; matrix products, arithmetic and copies ran while one was open for 3% -> 9% of each run, Pallas kernels for 13% -> 13%
where the time goes in v8:
time: 109 us; the launch traced here: 107 us
  Pallas kernels  44.2 us (41%)
  starting transfers between devices  27.4 us (25%)
  waiting for transfers between devices  22.1 us (20%)
  matrix products  6.37 us (6%)
  local copies, waits for them, and re-layouts  4.92 us (5%)
  other arithmetic  1.6 us (1%)
    pallas_call x1, Pallas kernels, main_kernel(): pl.pallas_call(main_body, grid_spec=pltpu.PrefetchScalarGridSpec(num_scal...  29 us
    ppermute x3, waiting for transfers between devices, swap(): one = lax.ppermute(last, axis, up)  19.1 us
    pallas_call x1, Pallas kernels, tail_kernel(): pl.pallas_call(tail_body, grid=(8,), in_specs=[tokens_of(model), tokens_o...  14.3 us
    ppermute x3, starting transfers between devices, swap(): one = lax.ppermute(last, axis, up)  11.8 us
    all_to_all x1, starting transfers between devices, shards(): lax.all_to_all(halves, BOTH, 0, 0, axis_index_groups=chip_groups(), tiled...  10.1 us
    dot_general x1, matrix products, dot_nt(): lax.dot_general(a, b, (((1,), (1,)), ((), ())), preferred_element_type=F32)  6.37 us
    ppermute x1, waiting for transfers between devices, other_core(): return lax.ppermute(array, 'lon', [(i, i ^ 1) for i in range(16)])  3.04 us
    ppermute x1, starting transfers between devices, other_core(): return lax.ppermute(array, 'lon', [(i, i ^ 1) for i in range(16)])  2.83 us
  transfers between devices with their start and end apart: 8, of which 2 were waited for; matrix products, arithmetic and copies ran while one was open for 9% of the time, Pallas kernels for 13%

profile of v8, /device:TPU:1, one launch (start us, length us, event | category | flops | bytes accessed | tf_op | source)
XLA Modules:
  0.0 107.5 jit_solution(18281010209643551401)
XLA Ops:
  0.6 0.9 slice_bitcast_fusion
  1.5 1.3 %collective-permute-start.1 = (bf16[64,512]{1,0:T(8,128)(2,1)S(1)}, bf16[64,512]{1,0:T(8,128)(2,1)S(1)}, u32[]{:S(2)}, u32[]{:S(2)}) collective-permute-start(bf16[64,512]{1,0:T(8,128)(2,1)S(1)} %get-tuple-element.36), channel_id=1, source_target_pairs={{16,0},{32,16},{48,32},{64,48},{80,64},{96,80},{112,96},{17,1},{33... | collective-permute-start | bytes 196616 | tf_op jit(solution)/shard_map/ppermute | solution.py:413
  2.8 4.7 %collective-permute-start = (bf16[64,512]{1,0:T(8,128)(2,1)S(1)}, bf16[64,512]{1,0:T(8,128)(2,1)S(1)}, u32[]{:S(2)}, u32[]{:S(2)}) collective-permute-start(bf16[64,512]{1,0:T(8,128)(2,1)S(1)} %get-tuple-element.37), channel_id=1, source_target_pairs={{0,16},{16,32},{32,48},{48,64},{64,80},{80,96},{96,112},{1,17},{17... | collective-permute-start | bytes 196616 | tf_op jit(solution)/shard_map/ppermute | solution.py:412
  7.5 0.9 fusion.2
  8.4 1.0 fusion.1
  9.4 1.0 fusion
  10.6 0.1 concatenate.6
  10.8 4.3 %collective-permute-start.2 = (bf16[80,512]{1,0:T(8,128)(2,1)S(1)}, bf16[80,512]{1,0:T(8,128)(2,1)S(1)}, u32[]{:S(2)}, u32[]{:S(2)}) collective-permute-start(bf16[80,512]{1,0:T(8,128)(2,1)S(1)} %concatenate.6), channel_id=1, source_target_pairs={{0,1},{1,2},{2,3},{3,4},{4,5},{5,6},{6,7},{7,8},{8,9},{9,10},{10,1... | collective-permute-start | bytes 245768 | tf_op jit(solution)/shard_map/ppermute | solution.py:412
  15.0 0.1 concatenate.7
  15.2 0.1 collective-permute-start.3
  15.2 0.0 copy-start
  15.3 6.4 %convolution_convert_fusion.a_own = bf16[2048,1024]{1,0:T(8,128)(2,1)} fusion(bf16[2048,512]{1,0:T(8,128)(2,1)} %bitcast.41, bf16[1024,512]{1,0:T(8,128)(2,1)} %w_out.1), kind=kOutput, calls=%fused_computation | convolution fusion | flops 2149580800 | bytes 7340032 | tf_op jit(solution)/shard_map/dot_general | solution.py:19
  21.6 29.0 %main.1 = (bf16[2048,1024]{1,0:T(8,128)(2,1)}, bf16[2048,512]{1,0:T(8,128)(2,1)S(1)}, bf16[64,512]{1,0:T(8,128)(2,1)S(1)}, bf16[160,512]{1,0:T(8,128)(2,1)S(1)},...) custom-call(s32[1]{0:T(128)} %bitcast.1.core, ...), custom_call_target="tpu_custom_call" | custom-call | flops 21474836480 | bytes 37748736 | tf_op jit(solution)/shard_map/main/pallas_call | solution.py:225
  50.7 2.8 %collective-permute-start.6 = (bf16[4,4,4,96,128]{4,3,2,1,0:T(8,128)(2,1)S(1)}, bf16[4,4,4,96,128]{4,3,2,1,0:T(8,128)(2,1)S(1)}, u32[]{:S(2)}, u32[]{:S(2)}) collective-permute-start(bf16[4,4,4,96,128]{4,3,2,1,0:T(8,128)(2,1)S(1)} %get-tuple-element.23), channel_id=1, source_target_pairs={{0,1},{1,0},{2,3},{3,2},{4,5},{5,4},{6,7},{7,6},{8,9},{9,8},{10,11... | collective-permute-start | bytes 4718600 | tf_op jit(solution)/shard_map/ppermute | solution.py:447
  53.5 3.0 %collective-permute-done.6 = bf16[4,4,4,96,128]{4,3,2,1,0:T(8,128)(2,1)S(1)} collective-permute-done((bf16[4,4,4,96,128]{4,3,2,1,0:T(8,128)(2,1)S(1)}, bf16[4,4,4,96,128]{4,3,2,1,0:T(8,128)(2,1)S(1)}, u32[]{:S(2)}, u32[]{:S(2)}) %collective-permute-start.6) | collective-permute-done | bytes 1572896 | tf_op jit(solution)/shard_map/ppermute | solution.py:447
  56.5 1.6 %add_convert_fusion = bf16[4,4,4,96,128]{4,3,2,1,0:T(8,128)(2,1)} fusion(bf16[4,4,4,96,128]{4,3,2,1,0:T(8,128)(2,1)S(1)} %collective-permute-done.6, bf16[4,4,4,96,128]{4,3,2,1,0:T(8,128)(2,1)S(1)} %get-tuple-element.22), kind=kLoop, calls=%fused_computation.1 | loop fusion | flops 3145728 | bytes 4718592 | tf_op jit(solution)/shard_map/convert_element_type | solution.py:465
  58.1 10.1 %all-to-all-start = ((bf16[64,96,128]{2,1,0:T(8,128)(2,1)}), bf16[64,96,128]{2,1,0:T(8,128)(2,1)S(1)}, u32[]{:S(2)}, u32[]{:S(2)}) async-start(bf16[64,96,128]{2,1,0:T(8,128)(2,1)} %bitcast.38), calls=%async_computation | async-start | bytes 3145728 | tf_op jit(solution)/shard_map/all_to_all | solution.py:466
  68.2 2.9 %collective-permute-start.4 = (bf16[160,512]{1,0:T(8,128)(2,1)S(1)}, bf16[160,512]{1,0:T(8,128)(2,1)S(1)}, u32[]{:S(2)}, u32[]{:S(2)}) collective-permute-start(bf16[160,512]{1,0:T(8,128)(2,1)S(1)} %get-tuple-element.18), channel_id=1, source_target_pairs={{0,16},{16,32},{32,48},{48,64},{64,80},{80,96},{96,112},{1,17},{17... | collective-permute-start | bytes 491528 | tf_op jit(solution)/shard_map/ppermute | solution.py:412
  71.1 1.3 %collective-permute-start.5 = (bf16[160,512]{1,0:T(8,128)(2,1)S(1)}, bf16[160,512]{1,0:T(8,128)(2,1)S(1)}, u32[]{:S(2)}, u32[]{:S(2)}) collective-permute-start(bf16[160,512]{1,0:T(8,128)(2,1)S(1)} %get-tuple-element.19), channel_id=1, source_target_pairs={{16,0},{32,16},{48,32},{64,48},{80,64},{96,80},{112,96},{17,1},{33... | collective-permute-start | bytes 491528 | tf_op jit(solution)/shard_map/ppermute | solution.py:413
  72.4 19.1 %collective-permute-done.4.before = bf16[160,512]{1,0:T(8,128)(2,1)S(1)} collective-permute-done((bf16[160,512]{1,0:T(8,128)(2,1)S(1)}, bf16[160,512]{1,0:T(8,128)(2,1)S(1)}, u32[]{:S(2)}, u32[]{:S(2)}) %collective-permute-start.4) | collective-permute-done | bytes 163872 | tf_op jit(solution)/shard_map/ppermute | solution.py:412
  91.5 0.7 copy-done.4
  92.2 0.1 copy-done.5
  92.3 14.3 %tail.1 = (bf16[2048,512]{1,0:T(8,128)(2,1)}, f32[512,512]{1,0:T(8,128)}) custom-call(bf16[2048,512]{1,0:T(8,128)(2,1)} %bitcast.44, bf16[2048,1024]{1,0:T(8,128)(2,1)} %get-tuple-element.15.act, bf16[1024,512]{1,0:T(8,128)(2,1)} %w_out.1, bf16[16,128,512]{2,1,0:T(8,128)(2,1)} %bitcast.37, bf16[64,512]{1,0:T(8,128)(2,1)} %copy-done.3, ...), custom_call_target="tpu_custom_call" | custom-call | flops 7516192768 | bytes 23068672 | tf_op jit(solution)/shard_map/tail/pallas_call | solution.py:355
  106.6 0.9 sum_blocks.1
  (32 shorter events, 0.1 us)
Async XLA Ops:
  1.5 9.1 %collective-permute-start.1 = (bf16[64,512]{1,0:T(8,128)(2,1)S(1)}, bf16[64,512]{1,0:T(8,128)(2,1)S(1)}, u32[]{:S(2)}, u32[]{:S(2)}) collective-permute-start(bf16[64,512]{1,0:T(8,128)(2,1)S(1)} %get-tuple-element.36), channel_id=1, source_target_pairs={{16,0},{32,16},{48,32},{64,48},{80,64},{96,80},{112,96},{17,1},{33... | collective-permute-start | bytes 196616 | tf_op jit(solution)/shard_map/ppermute | solution.py:413
  2.8 7.8 %collective-permute-start = (bf16[64,512]{1,0:T(8,128)(2,1)S(1)}, bf16[64,512]{1,0:T(8,128)(2,1)S(1)}, u32[]{:S(2)}, u32[]{:S(2)}) collective-permute-start(bf16[64,512]{1,0:T(8,128)(2,1)S(1)} %get-tuple-element.37), channel_id=1, source_target_pairs={{0,16},{16,32},{32,48},{48,64},{64,80},{80,96},{96,112},{1,17},{17... | collective-permute-start | bytes 196616 | tf_op jit(solution)/shard_map/ppermute | solution.py:412
  10.8 10.9 %collective-permute-start.2 = (bf16[80,512]{1,0:T(8,128)(2,1)S(1)}, bf16[80,512]{1,0:T(8,128)(2,1)S(1)}, u32[]{:S(2)}, u32[]{:S(2)}) collective-permute-start(bf16[80,512]{1,0:T(8,128)(2,1)S(1)} %concatenate.6), channel_id=1, source_target_pairs={{0,1},{1,2},{2,3},{3,4},{4,5},{5,6},{6,7},{7,8},{8,9},{9,10},{10,1... | collective-permute-start | bytes 245768 | tf_op jit(solution)/shard_map/ppermute | solution.py:412
  15.2 6.5 %collective-permute-start.3 = (bf16[80,512]{1,0:T(8,128)(2,1)S(1)}, bf16[80,512]{1,0:T(8,128)(2,1)S(1)}, u32[]{:S(2)}, u32[]{:S(2)}) collective-permute-start(bf16[80,512]{1,0:T(8,128)(2,1)S(1)} %concatenate.7), channel_id=1, source_target_pairs={{1,0},{2,1},{3,2},{4,3},{5,4},{6,5},{7,6},{8,7},{9,8},{10,9},{11,1... | collective-permute-start | bytes 245768 | tf_op jit(solution)/shard_map/ppermute | solution.py:413
  15.2 6.4 %copy-start = (bf16[8,64,512]{2,1,0:T(8,128)(2,1)S(1)}, bf16[8,64,512]{2,1,0:T(8,128)(2,1)}, u32[]{:S(2)}) copy-start(bf16[8,64,512]{2,1,0:T(8,128)(2,1)} %lat.1) | copy-start | bytes 1572868
  15.2 6.4 %copy-start.1 = (bf16[1024,512]{1,0:T(8,128)(2,1)S(1)}, bf16[1024,512]{1,0:T(8,128)(2,1)}, u32[]{:S(2)}) copy-start(bf16[1024,512]{1,0:T(8,128)(2,1)} %w_out.1) | copy-start | bytes 3145732
  50.6 7.5 %copy-start.2 = (bf16[2048,512]{1,0:T(8,128)(2,1)}, bf16[2048,512]{1,0:T(8,128)(2,1)S(1)}, u32[]{:S(2)}) copy-start(bf16[2048,512]{1,0:T(8,128)(2,1)S(1)} %get-tuple-element.16) | copy-start | bytes 6291460
  50.7 7.5 %copy-start.3 = (bf16[64,512]{1,0:T(8,128)(2,1)}, bf16[64,512]{1,0:T(8,128)(2,1)S(1)}, u32[]{:S(2)}) copy-start(bf16[64,512]{1,0:T(8,128)(2,1)S(1)} %get-tuple-element.17.edge) | copy-start | bytes 196612
  50.7 5.9 %collective-permute-start.6 = (bf16[4,4,4,96,128]{4,3,2,1,0:T(8,128)(2,1)S(1)}, bf16[4,4,4,96,128]{4,3,2,1,0:T(8,128)(2,1)S(1)}, u32[]{:S(2)}, u32[]{:S(2)}) collective-permute-start(bf16[4,4,4,96,128]{4,3,2,1,0:T(8,128)(2,1)S(1)} %get-tuple-element.23), channel_id=1, source_target_pairs={{0,1},{1,0},{2,3},{3,2},{4,5},{5,4},{6,7},{7,6},{8,9},{9,8},{10,11... | collective-permute-start | bytes 4718600 | tf_op jit(solution)/shard_map/ppermute | solution.py:447
  58.1 48.5 %all-to-all-start = ((bf16[64,96,128]{2,1,0:T(8,128)(2,1)}), bf16[64,96,128]{2,1,0:T(8,128)(2,1)S(1)}, u32[]{:S(2)}, u32[]{:S(2)}) async-start(bf16[64,96,128]{2,1,0:T(8,128)(2,1)} %bitcast.38), calls=%async_computation | async-start | bytes 3145728 | tf_op jit(solution)/shard_map/all_to_all | solution.py:466
  68.2 23.3 %collective-permute-start.4 = (bf16[160,512]{1,0:T(8,128)(2,1)S(1)}, bf16[160,512]{1,0:T(8,128)(2,1)S(1)}, u32[]{:S(2)}, u32[]{:S(2)}) collective-permute-start(bf16[160,512]{1,0:T(8,128)(2,1)S(1)} %get-tuple-element.18), channel_id=1, source_target_pairs={{0,16},{16,32},{32,48},{48,64},{64,80},{80,96},{96,112},{1,17},{17... | collective-permute-start | bytes 491528 | tf_op jit(solution)/shard_map/ppermute | solution.py:412
  71.1 20.4 %collective-permute-start.5 = (bf16[160,512]{1,0:T(8,128)(2,1)S(1)}, bf16[160,512]{1,0:T(8,128)(2,1)S(1)}, u32[]{:S(2)}, u32[]{:S(2)}) collective-permute-start(bf16[160,512]{1,0:T(8,128)(2,1)S(1)} %get-tuple-element.19), channel_id=1, source_target_pairs={{16,0},{32,16},{48,32},{64,48},{80,64},{96,80},{112,96},{17,1},{33... | collective-permute-start | bytes 491528 | tf_op jit(solution)/shard_map/ppermute | solution.py:413
  91.5 0.7 copy-start.4
  91.5 0.8 copy-start.5

commit v9 on v8

--- a/solution.py
+++ b/solution.py
@@ -8,7 +8,9 @@
 BF16 = jnp.bfloat16
 F32 = jnp.float32
 BOTH = ("lat", "lon")
-GRANT = 46
+GRANT = 44
+WINDOW = 57
+FLOPS = 4
 
 
 def dot_nn(a, b):
@@ -208,6 +210,29 @@
         act_copy.wait()
 
 
+def project_body(cot, w_out, out):
+    out[...] = dot_nt(cot[...], w_out[...]).astype(BF16)
+
+
+def project(cot, w_out):
+    count, model = cot.shape
+    hidden = w_out.shape[0]
+    block = count // 4
+    return pl.pallas_call(
+        project_body,
+        grid=(4,),
+        in_specs=[
+            pl.BlockSpec((block, model), lambda i: (i, 0)),
+            pl.BlockSpec((hidden, model), lambda i: (0, 0), pipeline_mode=pl.Buffered(1)),
+        ],
+        out_specs=pl.BlockSpec((block, hidden), lambda i: (i, 0)),
+        out_shape=jax.ShapeDtypeStruct((count, hidden), BF16),
+        compiler_params=pltpu.CompilerParams(vmem_limit_bytes=WINDOW << 20),
+        cost_estimate=cost(FLOPS << 30, 7 << 20),
+        name="project",
+    )(cot, w_out)
+
+
 def main_kernel(core, lat, before, after, left, right, weight, tokens, cot, a_own, w_in, w_out):
     rows, cols, width = lat.shape
     model = weight.shape[0] // 16
@@ -218,7 +243,9 @@
     edge = 64
     pack = 2 * cols + 32
     clamp = lambda i, low: jnp.clip(i - low, 0, 3)
-    whole = lambda *shape: pl.BlockSpec(shape, lambda i, c: (0,) * len(shape))
+    whole = lambda *shape: pl.BlockSpec(
+        shape, lambda i, c: (0,) * len(shape), pipeline_mode=pl.Buffered(1)
+    )
     kernel_row = lambda i, top: (top - clamp(i, 0) // 2, 0, clamp(i, 0) % 2, 0)
     tokens_of = lambda w: pl.BlockSpec((block, w), lambda i, c: (clamp(i, 5), 0))
     blocks = (4, 4, 4, 96, 128)
@@ -455,7 +482,7 @@
     cot = cotangent.reshape(count, model)
 
     before, after, left, right = halos(latents, fine_tokens, cotangent)
-    a_own = dot_nt(cot, uniting_out).astype(BF16)
+    a_own = project(cot, uniting_out)
     act, up_cot, up_cot_edge, first_row, last_row, keep, send = main_kernel(
         core, latents, before, after, left, right, upsample_weight,
         tokens, cot, a_own, uniting_in, uniting_out,

time: 109 us -> 111 us (1.018)
  matrix products: 6.37 us -> 0 us
  Pallas kernels: 44.2 us -> 50.1 us
  local copies, waits for them, and re-layouts: 4.92 us -> 6.14 us
    dot_general x1 -> x0, matrix products: 6.37 us -> none  [dot_nt(): lax.dot_general(a, b, (((1,), (1,)), ((), ())), preferred_element_type=F32)]
    pallas_call x0 -> x1, Pallas kernels: none -> 6.33 us  [project(): pl.pallas_call(project_body, grid=(4,), in_specs=[pl.BlockSpec((block, mo...]
    unnamed x14 -> x16, local copies, waits for them, and re-layouts: 0.79 us -> 2 us
  transfers between devices with their start and end apart: 8 -> 8, of which waited for: 2 -> 2; matrix products, arithmetic and copies ran while one was open for 9% -> 3% of each run, Pallas kernels for 13% -> 19%
where the time goes in v9:
time: 111 us; the launch traced here: 108 us
  Pallas kernels  50.1 us (45%)
  starting transfers between devices  27.5 us (25%)
  waiting for transfers between devices  22.1 us (20%)
  local copies, waits for them, and re-layouts  6.14 us (6%)
  other arithmetic  1.62 us (1%)
    pallas_call x1, Pallas kernels, main_kernel(): pl.pallas_call(main_body, grid_spec=pltpu.PrefetchScalarGridSpec(num_scal...  28.5 us
    ppermute x3, waiting for transfers between devices, swap(): one = lax.ppermute(last, axis, up)  19.1 us
    pallas_call x1, Pallas kernels, tail_kernel(): pl.pallas_call(tail_body, grid=(8,), in_specs=[tokens_of(model), tokens_o...  14.3 us
    ppermute x3, starting transfers between devices, swap(): one = lax.ppermute(last, axis, up)  11.8 us
    all_to_all x1, starting transfers between devices, shards(): lax.all_to_all(halves, BOTH, 0, 0, axis_index_groups=chip_groups(), tiled...  10.2 us
    pallas_call x1, Pallas kernels, project(): pl.pallas_call(project_body, grid=(4,), in_specs=[pl.BlockSpec((block, mo...  6.33 us
    ppermute x1, waiting for transfers between devices, other_core(): return lax.ppermute(array, 'lon', [(i, i ^ 1) for i in range(16)])  3.04 us
    ppermute x1, starting transfers between devices, other_core(): return lax.ppermute(array, 'lon', [(i, i ^ 1) for i in range(16)])  2.81 us
  transfers between devices with their start and end apart: 8, of which 2 were waited for; matrix products, arithmetic and copies ran while one was open for 3% of the time, Pallas kernels for 19%

profile of v9, /device:TPU:1, one launch (start us, length us, event | category | flops | bytes accessed | tf_op | source)
XLA Modules:
  0.0 108.4 jit_solution(5410439054786037616)
XLA Ops:
  0.6 0.9 slice_bitcast_fusion
  1.5 1.3 %collective-permute-start.1 = (bf16[64,512]{1,0:T(8,128)(2,1)S(1)}, bf16[64,512]{1,0:T(8,128)(2,1)S(1)}, u32[]{:S(2)}, u32[]{:S(2)}) collective-permute-start(bf16[64,512]{1,0:T(8,128)(2,1)S(1)} %get-tuple-element.36), channel_id=1, source_target_pairs={{16,0},{32,16},{48,32},{64,48},{80,64},{96,80},{112,96},{17,1},{33... | collective-permute-start | bytes 196616 | tf_op jit(solution)/shard_map/ppermute | solution.py:440
  2.8 4.7 %collective-permute-start = (bf16[64,512]{1,0:T(8,128)(2,1)S(1)}, bf16[64,512]{1,0:T(8,128)(2,1)S(1)}, u32[]{:S(2)}, u32[]{:S(2)}) collective-permute-start(bf16[64,512]{1,0:T(8,128)(2,1)S(1)} %get-tuple-element.37), channel_id=1, source_target_pairs={{0,16},{16,32},{32,48},{48,64},{64,80},{80,96},{96,112},{1,17},{17... | collective-permute-start | bytes 196616 | tf_op jit(solution)/shard_map/ppermute | solution.py:439
  7.5 0.9 fusion.2
  8.4 1.0 fusion.1
  9.4 1.0 fusion
  10.6 0.1 concatenate.6
  10.8 4.3 %collective-permute-start.2 = (bf16[80,512]{1,0:T(8,128)(2,1)S(1)}, bf16[80,512]{1,0:T(8,128)(2,1)S(1)}, u32[]{:S(2)}, u32[]{:S(2)}) collective-permute-start(bf16[80,512]{1,0:T(8,128)(2,1)S(1)} %concatenate.6), channel_id=1, source_target_pairs={{0,1},{1,2},{2,3},{3,4},{4,5},{5,6},{6,7},{7,8},{8,9},{9,10},{10,1... | collective-permute-start | bytes 245768 | tf_op jit(solution)/shard_map/ppermute | solution.py:439
  15.0 0.1 concatenate.7
  15.2 0.1 collective-permute-start.3
  15.3 6.3 %project.1.a_own = bf16[2048,1024]{1,0:T(8,128)(2,1)} custom-call(bf16[2048,512]{1,0:T(8,128)(2,1)} %bitcast.41, bf16[1024,512]{1,0:T(8,128)(2,1)} %w_out.3), custom_call_target="tpu_custom_call" | custom-call | flops 4294967296 | bytes 7340032 | tf_op jit(solution)/shard_map/project/pallas_call | solution.py:221
  21.6 1.2 %copy-done.2 = bf16[1024,512]{1,0:T(8,128)(2,1)S(1)} copy-done((bf16[1024,512]{1,0:T(8,128)(2,1)S(1)}, bf16[1024,512]{1,0:T(8,128)(2,1)}, u32[]{:S(2)}) %copy-start.2) | copy-done | bytes 1048600
  22.8 28.5 %main.1 = (bf16[2048,1024]{1,0:T(8,128)(2,1)}, bf16[2048,512]{1,0:T(8,128)(2,1)S(1)}, bf16[64,512]{1,0:T(8,128)(2,1)S(1)}, bf16[160,512]{1,0:T(8,128)(2,1)S(1)},...) custom-call(s32[1]{0:T(128)} %bitcast.1.core, ...), custom_call_target="tpu_custom_call" | custom-call | flops 21474836480 | bytes 37748736 | tf_op jit(solution)/shard_map/main/pallas_call | solution.py:252
  51.4 2.8 %collective-permute-start.6 = (bf16[4,4,4,96,128]{4,3,2,1,0:T(8,128)(2,1)S(1)}, bf16[4,4,4,96,128]{4,3,2,1,0:T(8,128)(2,1)S(1)}, u32[]{:S(2)}, u32[]{:S(2)}) collective-permute-start(bf16[4,4,4,96,128]{4,3,2,1,0:T(8,128)(2,1)S(1)} %get-tuple-element.23), channel_id=1, source_target_pairs={{0,1},{1,0},{2,3},{3,2},{4,5},{5,4},{6,7},{7,6},{8,9},{9,8},{10,11... | collective-permute-start | bytes 4718600 | tf_op jit(solution)/shard_map/ppermute | solution.py:474
  54.2 3.0 %collective-permute-done.6 = bf16[4,4,4,96,128]{4,3,2,1,0:T(8,128)(2,1)S(1)} collective-permute-done((bf16[4,4,4,96,128]{4,3,2,1,0:T(8,128)(2,1)S(1)}, bf16[4,4,4,96,128]{4,3,2,1,0:T(8,128)(2,1)S(1)}, u32[]{:S(2)}, u32[]{:S(2)}) %collective-permute-start.6) | collective-permute-done | bytes 1572896 | tf_op jit(solution)/shard_map/ppermute | solution.py:474
  57.3 1.6 %add_convert_fusion = bf16[4,4,4,96,128]{4,3,2,1,0:T(8,128)(2,1)} fusion(bf16[4,4,4,96,128]{4,3,2,1,0:T(8,128)(2,1)S(1)} %collective-permute-done.6, bf16[4,4,4,96,128]{4,3,2,1,0:T(8,128)(2,1)S(1)} %get-tuple-element.22), kind=kLoop, calls=%fused_computation | loop fusion | flops 3145728 | bytes 4718592 | tf_op jit(solution)/shard_map/convert_element_type | solution.py:492
  58.9 10.2 %all-to-all-start = ((bf16[64,96,128]{2,1,0:T(8,128)(2,1)}), bf16[64,96,128]{2,1,0:T(8,128)(2,1)S(1)}, u32[]{:S(2)}, u32[]{:S(2)}) async-start(bf16[64,96,128]{2,1,0:T(8,128)(2,1)} %bitcast.38), calls=%async_computation | async-start | bytes 3145728 | tf_op jit(solution)/shard_map/all_to_all | solution.py:493
  69.1 2.9 %collective-permute-start.4 = (bf16[160,512]{1,0:T(8,128)(2,1)S(1)}, bf16[160,512]{1,0:T(8,128)(2,1)S(1)}, u32[]{:S(2)}, u32[]{:S(2)}) collective-permute-start(bf16[160,512]{1,0:T(8,128)(2,1)S(1)} %get-tuple-element.18), channel_id=1, source_target_pairs={{0,16},{16,32},{32,48},{48,64},{64,80},{80,96},{96,112},{1,17},{17... | collective-permute-start | bytes 491528 | tf_op jit(solution)/shard_map/ppermute | solution.py:439
  72.1 1.3 %collective-permute-start.5 = (bf16[160,512]{1,0:T(8,128)(2,1)S(1)}, bf16[160,512]{1,0:T(8,128)(2,1)S(1)}, u32[]{:S(2)}, u32[]{:S(2)}) collective-permute-start(bf16[160,512]{1,0:T(8,128)(2,1)S(1)} %get-tuple-element.19), channel_id=1, source_target_pairs={{16,0},{32,16},{48,32},{64,48},{80,64},{96,80},{112,96},{17,1},{33... | collective-permute-start | bytes 491528 | tf_op jit(solution)/shard_map/ppermute | solution.py:440
  73.4 19.1 %collective-permute-done.4.before = bf16[160,512]{1,0:T(8,128)(2,1)S(1)} collective-permute-done((bf16[160,512]{1,0:T(8,128)(2,1)S(1)}, bf16[160,512]{1,0:T(8,128)(2,1)S(1)}, u32[]{:S(2)}, u32[]{:S(2)}) %collective-permute-start.4) | collective-permute-done | bytes 163872 | tf_op jit(solution)/shard_map/ppermute | solution.py:439
  92.4 0.7 copy-done.5
  93.1 0.1 copy-done.6
  93.2 14.3 %tail.1 = (bf16[2048,512]{1,0:T(8,128)(2,1)}, f32[512,512]{1,0:T(8,128)}) custom-call(bf16[2048,512]{1,0:T(8,128)(2,1)} %bitcast.35, bf16[2048,1024]{1,0:T(8,128)(2,1)} %get-tuple-element.15.act, bf16[1024,512]{1,0:T(8,128)(2,1)} %w_out.3, bf16[16,128,512]{2,1,0:T(8,128)(2,1)} %bitcast.37, bf16[64,512]{1,0:T(8,128)(2,1)} %copy-done.4, ...), custom_call_target="tpu_custom_call" | custom-call | flops 7516192768 | bytes 23068672 | tf_op jit(solution)/shard_map/tail/pallas_call | solution.py:382
  107.5 0.9 sum_blocks.1
  (34 shorter events, 0.2 us)
Async XLA Ops:
  1.5 9.1 %collective-permute-start.1 = (bf16[64,512]{1,0:T(8,128)(2,1)S(1)}, bf16[64,512]{1,0:T(8,128)(2,1)S(1)}, u32[]{:S(2)}, u32[]{:S(2)}) collective-permute-start(bf16[64,512]{1,0:T(8,128)(2,1)S(1)} %get-tuple-element.36), channel_id=1, source_target_pairs={{16,0},{32,16},{48,32},{64,48},{80,64},{96,80},{112,96},{17,1},{33... | collective-permute-start | bytes 196616 | tf_op jit(solution)/shard_map/ppermute | solution.py:440
  2.8 7.8 %collective-permute-start = (bf16[64,512]{1,0:T(8,128)(2,1)S(1)}, bf16[64,512]{1,0:T(8,128)(2,1)S(1)}, u32[]{:S(2)}, u32[]{:S(2)}) collective-permute-start(bf16[64,512]{1,0:T(8,128)(2,1)S(1)} %get-tuple-element.37), channel_id=1, source_target_pairs={{0,16},{16,32},{32,48},{48,64},{64,80},{80,96},{96,112},{1,17},{17... | collective-permute-start | bytes 196616 | tf_op jit(solution)/shard_map/ppermute | solution.py:439
  10.8 10.8 %collective-permute-start.2 = (bf16[80,512]{1,0:T(8,128)(2,1)S(1)}, bf16[80,512]{1,0:T(8,128)(2,1)S(1)}, u32[]{:S(2)}, u32[]{:S(2)}) collective-permute-start(bf16[80,512]{1,0:T(8,128)(2,1)S(1)} %concatenate.6), channel_id=1, source_target_pairs={{0,1},{1,2},{2,3},{3,4},{4,5},{5,6},{6,7},{7,8},{8,9},{9,10},{10,1... | collective-permute-start | bytes 245768 | tf_op jit(solution)/shard_map/ppermute | solution.py:439
  15.2 6.4 %collective-permute-start.3 = (bf16[80,512]{1,0:T(8,128)(2,1)S(1)}, bf16[80,512]{1,0:T(8,128)(2,1)S(1)}, u32[]{:S(2)}, u32[]{:S(2)}) collective-permute-start(bf16[80,512]{1,0:T(8,128)(2,1)S(1)} %concatenate.7), channel_id=1, source_target_pairs={{1,0},{2,1},{3,2},{4,3},{5,4},{6,5},{7,6},{8,7},{9,8},{10,9},{11,1... | collective-permute-start | bytes 245768 | tf_op jit(solution)/shard_map/ppermute | solution.py:440
  15.2 6.4 %copy-start = (bf16[8,64,512]{2,1,0:T(8,128)(2,1)S(1)}, bf16[8,64,512]{2,1,0:T(8,128)(2,1)}, u32[]{:S(2)}) copy-start(bf16[8,64,512]{2,1,0:T(8,128)(2,1)} %lat.1) | copy-start | bytes 1572868
  15.2 6.4 %copy-start.1 = (bf16[16,128,512]{2,1,0:T(8,128)(2,1)S(1)}, bf16[16,128,512]{2,1,0:T(8,128)(2,1)}, u32[]{:S(2)}) copy-start(bf16[16,128,512]{2,1,0:T(8,128)(2,1)} %param.6) | copy-start | bytes 6291460
  21.6 1.2 %copy-start.2 = (bf16[1024,512]{1,0:T(8,128)(2,1)S(1)}, bf16[1024,512]{1,0:T(8,128)(2,1)}, u32[]{:S(2)}) copy-start(bf16[1024,512]{1,0:T(8,128)(2,1)} %w_out.3) | copy-start | bytes 3145732
  51.4 7.5 %copy-start.3 = (bf16[2048,512]{1,0:T(8,128)(2,1)}, bf16[2048,512]{1,0:T(8,128)(2,1)S(1)}, u32[]{:S(2)}) copy-start(bf16[2048,512]{1,0:T(8,128)(2,1)S(1)} %get-tuple-element.16) | copy-start | bytes 6291460
  51.4 7.5 %copy-start.4 = (bf16[64,512]{1,0:T(8,128)(2,1)}, bf16[64,512]{1,0:T(8,128)(2,1)S(1)}, u32[]{:S(2)}) copy-start(bf16[64,512]{1,0:T(8,128)(2,1)S(1)} %get-tuple-element.17.edge) | copy-start | bytes 196612
  51.4 5.8 %collective-permute-start.6 = (bf16[4,4,4,96,128]{4,3,2,1,0:T(8,128)(2,1)S(1)}, bf16[4,4,4,96,128]{4,3,2,1,0:T(8,128)(2,1)S(1)}, u32[]{:S(2)}, u32[]{:S(2)}) collective-permute-start(bf16[4,4,4,96,128]{4,3,2,1,0:T(8,128)(2,1)S(1)} %get-tuple-element.23), channel_id=1, source_target_pairs={{0,1},{1,0},{2,3},{3,2},{4,5},{5,4},{6,7},{7,6},{8,9},{9,8},{10,11... | collective-permute-start | bytes 4718600 | tf_op jit(solution)/shard_map/ppermute | solution.py:474
  58.9 48.7 %all-to-all-start = ((bf16[64,96,128]{2,1,0:T(8,128)(2,1)}), bf16[64,96,128]{2,1,0:T(8,128)(2,1)S(1)}, u32[]{:S(2)}, u32[]{:S(2)}) async-start(bf16[64,96,128]{2,1,0:T(8,128)(2,1)} %bitcast.38), calls=%async_computation | async-start | bytes 3145728 | tf_op jit(solution)/shard_map/all_to_all | solution.py:493
  69.1 23.3 %collective-permute-start.4 = (bf16[160,512]{1,0:T(8,128)(2,1)S(1)}, bf16[160,512]{1,0:T(8,128)(2,1)S(1)}, u32[]{:S(2)}, u32[]{:S(2)}) collective-permute-start(bf16[160,512]{1,0:T(8,128)(2,1)S(1)} %get-tuple-element.18), channel_id=1, source_target_pairs={{0,16},{16,32},{32,48},{48,64},{64,80},{80,96},{96,112},{1,17},{17... | collective-permute-start | bytes 491528 | tf_op jit(solution)/shard_map/ppermute | solution.py:439
  72.1 20.4 %collective-permute-start.5 = (bf16[160,512]{1,0:T(8,128)(2,1)S(1)}, bf16[160,512]{1,0:T(8,128)(2,1)S(1)}, u32[]{:S(2)}, u32[]{:S(2)}) collective-permute-start(bf16[160,512]{1,0:T(8,128)(2,1)S(1)} %get-tuple-element.19), channel_id=1, source_target_pairs={{16,0},{32,16},{48,32},{64,48},{80,64},{96,80},{112,96},{17,1},{33... | collective-permute-start | bytes 491528 | tf_op jit(solution)/shard_map/ppermute | solution.py:440
  92.4 0.7 copy-start.5
  92.4 0.8 copy-start.6

commit v10 on v8

--- a/solution.py
+++ b/solution.py
@@ -142,15 +142,14 @@
             last_row[at] = value[32 * i : 32 * i + 16]
             first_row[at] = value[32 * i + 16 : 32 * i + 32]
 
-    @pl.when((step > 4) & (step < 9))
-    def _():
+    def own_tokens(a_of):
         at = pl.ds(pl.multiple_of((step - 5) * block, block), block)
         for n in range(0, hidden, 256):
             span = slice(n, n + 256)
             wide, grad = network(
                 lambda: tokens[...],
                 lambda i: up[i, at],
-                lambda: a_own[:, span].astype(F32),
+                lambda: a_of(span),
                 span,
             )
             act[at, span] = wide
@@ -160,6 +159,14 @@
         turned[model + half_model : 2 * model, at] = up[1, at].T
         turned[2 * model :, at] = cot[...].T
         up_cot[...] = dot_nt(pre[at, :], w_in[model:, :]).astype(BF16)
+
+    @pl.when((step > 4) & (step < 7))
+    def _():
+        own_tokens(lambda span: a_own[:, span].astype(F32))
+
+    @pl.when((step > 6) & (step < 9))
+    def _():
+        own_tokens(lambda span: dot_nt(cot[...], w_out[span, :]))
 
     @pl.when(step == 5)
     def _():
@@ -237,7 +244,7 @@
                 pl.BlockSpec((1, 4, half, width), lambda i, c: kernel_row(i, 3)),
                 tokens_of(model),
                 tokens_of(model),
-                tokens_of(hidden),
+                pl.BlockSpec((block, hidden), lambda i, c: (jnp.clip(i - 5, 0, 1), 0)),
                 pl.BlockSpec(memory_space=pltpu.HBM),
                 pl.BlockSpec(memory_space=pltpu.HBM),
             ],
@@ -455,7 +462,7 @@
     cot = cotangent.reshape(count, model)
 
     before, after, left, right = halos(latents, fine_tokens, cotangent)
-    a_own = dot_nt(cot, uniting_out).astype(BF16)
+    a_own = dot_nt(cot[: count // 2], uniting_out).astype(BF16)
     act, up_cot, up_cot_edge, first_row, last_row, keep, send = main_kernel(
         core, latents, before, after, left, right, upsample_weight,
         tokens, cot, a_own, uniting_in, uniting_out,

time: 109 us -> 111 us (1.018)
  matrix products: 6.37 us -> 3.89 us
  local copies, waits for them, and re-layouts: 4.92 us -> 7.27 us
    ppermute x1, starting transfers between devices: 2.83 us -> 6.13 us  [other_core(): return lax.ppermute(array, 'lon', [(i, i ^ 1) for i in range(16)])]
    all_to_all x1, starting transfers between devices: 10.1 us -> 7.48 us  [shards(): lax.all_to_all(halves, BOTH, 0, 0, axis_index_groups=chip_groups(), tiled...]
    dot_general x1, matrix products: 6.37 us -> 3.89 us  [dot_nt(): lax.dot_general(a, b, (((1,), (1,)), ((), ())), preferred_element_type=F32)]
    slice x0 -> x1, local copies, waits for them, and re-layouts: none -> 2.26 us  [shards(): a_own = dot_nt(cot[:count // 2], uniting_out).astype(BF16)]
    ppermute x3, starting transfers between devices: 2.66 us -> 3.93 us  [swap(): other = lax.ppermute(first, axis, down)]
    ppermute x3, starting transfers between devices: 11.8 us -> 10.6 us  [swap(): one = lax.ppermute(last, axis, up)]
where the time goes in v10:
time: 111 us; the launch traced here: 109 us
  Pallas kernels  44.8 us (40%)
  starting transfers between devices  28.1 us (25%)
  waiting for transfers between devices  22.4 us (20%)
  local copies, waits for them, and re-layouts  7.27 us (7%)
  matrix products  3.89 us (4%)
  other arithmetic  1.61 us (1%)
    pallas_call x1, Pallas kernels, main_kernel(): pl.pallas_call(main_body, grid_spec=pltpu.PrefetchScalarGridSpec(num_scal...  29.6 us
    ppermute x3, waiting for transfers between devices, swap(): one = lax.ppermute(last, axis, up)  19.3 us
    pallas_call x1, Pallas kernels, tail_kernel(): pl.pallas_call(tail_body, grid=(8,), in_specs=[tokens_of(model), tokens_o...  14.3 us
    ppermute x3, starting transfers between devices, swap(): one = lax.ppermute(last, axis, up)  10.6 us
    all_to_all x1, starting transfers between devices, shards(): lax.all_to_all(halves, BOTH, 0, 0, axis_index_groups=chip_groups(), tiled...  7.48 us
    ppermute x1, starting transfers between devices, other_core(): return lax.ppermute(array, 'lon', [(i, i ^ 1) for i in range(16)])  6.13 us
    ppermute x3, starting transfers between devices, swap(): other = lax.ppermute(first, axis, down)  3.93 us
    dot_general x1, matrix products, dot_nt(): lax.dot_general(a, b, (((1,), (1,)), ((), ())), preferred_element_type=F32)  3.89 us
  transfers between devices with their start and end apart: 8, of which 2 were waited for; matrix products, arithmetic and copies ran while one was open for 9% of the time, Pallas kernels for 13%

profile of v10, /device:TPU:1, one launch (start us, length us, event | category | flops | bytes accessed | tf_op | source)
XLA Modules:
  0.0 108.9 jit_solution(13626391626922944657)
XLA Ops:
  0.6 1.0 slice_bitcast_fusion
  1.6 1.3 %collective-permute-start.1 = (bf16[64,512]{1,0:T(8,128)(2,1)S(1)}, bf16[64,512]{1,0:T(8,128)(2,1)S(1)}, u32[]{:S(2)}, u32[]{:S(2)}) collective-permute-start(bf16[64,512]{1,0:T(8,128)(2,1)S(1)} %get-tuple-element.36), channel_id=1, source_target_pairs={{16,0},{32,16},{48,32},{64,48},{80,64},{96,80},{112,96},{17,1},{33... | collective-permute-start | bytes 196616 | tf_op jit(solution)/shard_map/ppermute | solution.py:420
  2.9 4.7 %collective-permute-start = (bf16[64,512]{1,0:T(8,128)(2,1)S(1)}, bf16[64,512]{1,0:T(8,128)(2,1)S(1)}, u32[]{:S(2)}, u32[]{:S(2)}) collective-permute-start(bf16[64,512]{1,0:T(8,128)(2,1)S(1)} %get-tuple-element.37), channel_id=1, source_target_pairs={{0,16},{16,32},{32,48},{48,64},{64,80},{80,96},{96,112},{1,17},{17... | collective-permute-start | bytes 196616 | tf_op jit(solution)/shard_map/ppermute | solution.py:419
  7.6 0.9 fusion.2
  8.5 1.0 fusion.1
  9.5 1.0 fusion
  10.5 2.3 %slice.70 = bf16[8,128,512]{2,1,0:T(8,128)(2,1)} slice(bf16[16,128,512]{2,1,0:T(8,128)(2,1)} %param.11), slice={[0:8], [0:128], [0:512]} | slice | bytes 2097152 | tf_op jit(solution)/shard_map/slice | solution.py:465
  13.0 0.1 concatenate.7
  13.1 1.3 %collective-permute-start.3 = (bf16[80,512]{1,0:T(8,128)(2,1)S(1)}, bf16[80,512]{1,0:T(8,128)(2,1)S(1)}, u32[]{:S(2)}, u32[]{:S(2)}) collective-permute-start(bf16[80,512]{1,0:T(8,128)(2,1)S(1)} %concatenate.7), channel_id=1, source_target_pairs={{1,0},{2,1},{3,2},{4,3},{5,4},{6,5},{7,6},{8,7},{9,8},{10,9},{11,1... | collective-permute-start | bytes 245768 | tf_op jit(solution)/shard_map/ppermute | solution.py:420
  14.5 0.1 concatenate.6
  14.6 3.0 %collective-permute-start.2 = (bf16[80,512]{1,0:T(8,128)(2,1)S(1)}, bf16[80,512]{1,0:T(8,128)(2,1)S(1)}, u32[]{:S(2)}, u32[]{:S(2)}) collective-permute-start(bf16[80,512]{1,0:T(8,128)(2,1)S(1)} %concatenate.6), channel_id=1, source_target_pairs={{0,1},{1,2},{2,3},{3,4},{4,5},{5,6},{6,7},{7,8},{8,9},{9,10},{10,1... | collective-permute-start | bytes 245768 | tf_op jit(solution)/shard_map/ppermute | solution.py:419
  17.6 3.9 %convolution_convert_fusion.a_own = bf16[1024,1024]{1,0:T(8,128)(2,1)} fusion(bf16[1024,512]{1,0:T(8,128)(2,1)} %bitcast.40, bf16[1024,512]{1,0:T(8,128)(2,1)S(1)} %copy-done.1), kind=kOutput, calls=%fused_computation.1 | convolution fusion | flops 1074790400 | bytes 4194304 | tf_op jit(solution)/shard_map/dot_general | solution.py:19
  21.5 29.6 %main.1 = (bf16[2048,1024]{1,0:T(8,128)(2,1)}, bf16[2048,512]{1,0:T(8,128)(2,1)S(1)}, bf16[64,512]{1,0:T(8,128)(2,1)S(1)}, bf16[160,512]{1,0:T(8,128)(2,1)S(1)},...) custom-call(s32[1]{0:T(128)} %bitcast.1.core, ...), custom_call_target="tpu_custom_call" | custom-call | flops 21474836480 | bytes 37748736 | tf_op jit(solution)/shard_map/main/pallas_call | solution.py:232
  51.2 6.1 %collective-permute-start.6 = (bf16[4,4,4,96,128]{4,3,2,1,0:T(8,128)(2,1)S(1)}, bf16[4,4,4,96,128]{4,3,2,1,0:T(8,128)(2,1)S(1)}, u32[]{:S(2)}, u32[]{:S(2)}) collective-permute-start(bf16[4,4,4,96,128]{4,3,2,1,0:T(8,128)(2,1)S(1)} %get-tuple-element.23), channel_id=1, source_target_pairs={{0,1},{1,0},{2,3},{3,2},{4,5},{5,4},{6,7},{7,6},{8,9},{9,8},{10,11... | collective-permute-start | bytes 4718600 | tf_op jit(solution)/shard_map/ppermute | solution.py:454
  57.3 3.0 %collective-permute-done.6 = bf16[4,4,4,96,128]{4,3,2,1,0:T(8,128)(2,1)S(1)} collective-permute-done((bf16[4,4,4,96,128]{4,3,2,1,0:T(8,128)(2,1)S(1)}, bf16[4,4,4,96,128]{4,3,2,1,0:T(8,128)(2,1)S(1)}, u32[]{:S(2)}, u32[]{:S(2)}) %collective-permute-start.6) | collective-permute-done | bytes 1572896 | tf_op jit(solution)/shard_map/ppermute | solution.py:454
  60.3 1.6 %add_convert_fusion = bf16[4,4,4,96,128]{4,3,2,1,0:T(8,128)(2,1)} fusion(bf16[4,4,4,96,128]{4,3,2,1,0:T(8,128)(2,1)S(1)} %collective-permute-done.6, bf16[4,4,4,96,128]{4,3,2,1,0:T(8,128)(2,1)S(1)} %get-tuple-element.22), kind=kLoop, calls=%fused_computation | loop fusion | flops 3145728 | bytes 4718592 | tf_op jit(solution)/shard_map/convert_element_type | solution.py:472
  61.9 7.5 %all-to-all-start = ((bf16[64,96,128]{2,1,0:T(8,128)(2,1)}), bf16[64,96,128]{2,1,0:T(8,128)(2,1)S(1)}, u32[]{:S(2)}, u32[]{:S(2)}) async-start(bf16[64,96,128]{2,1,0:T(8,128)(2,1)} %bitcast.39), calls=%async_computation | async-start | bytes 3145728 | tf_op jit(solution)/shard_map/all_to_all | solution.py:473
  69.4 2.9 %collective-permute-start.4 = (bf16[160,512]{1,0:T(8,128)(2,1)S(1)}, bf16[160,512]{1,0:T(8,128)(2,1)S(1)}, u32[]{:S(2)}, u32[]{:S(2)}) collective-permute-start(bf16[160,512]{1,0:T(8,128)(2,1)S(1)} %get-tuple-element.18), channel_id=1, source_target_pairs={{0,16},{16,32},{32,48},{48,64},{64,80},{80,96},{96,112},{1,17},{17... | collective-permute-start | bytes 491528 | tf_op jit(solution)/shard_map/ppermute | solution.py:419
  72.3 1.3 %collective-permute-start.5 = (bf16[160,512]{1,0:T(8,128)(2,1)S(1)}, bf16[160,512]{1,0:T(8,128)(2,1)S(1)}, u32[]{:S(2)}, u32[]{:S(2)}) collective-permute-start(bf16[160,512]{1,0:T(8,128)(2,1)S(1)} %get-tuple-element.19), channel_id=1, source_target_pairs={{16,0},{32,16},{48,32},{64,48},{80,64},{96,80},{112,96},{17,1},{33... | collective-permute-start | bytes 491528 | tf_op jit(solution)/shard_map/ppermute | solution.py:420
  73.6 19.3 %collective-permute-done.4.before = bf16[160,512]{1,0:T(8,128)(2,1)S(1)} collective-permute-done((bf16[160,512]{1,0:T(8,128)(2,1)S(1)}, bf16[160,512]{1,0:T(8,128)(2,1)S(1)}, u32[]{:S(2)}, u32[]{:S(2)}) %collective-permute-start.4) | collective-permute-done | bytes 163872 | tf_op jit(solution)/shard_map/ppermute | solution.py:419
  92.9 0.7 copy-done.4
  93.6 0.1 copy-done.5
  93.7 14.3 %tail.1 = (bf16[2048,512]{1,0:T(8,128)(2,1)}, f32[512,512]{1,0:T(8,128)}) custom-call(bf16[2048,512]{1,0:T(8,128)(2,1)} %bitcast.45, bf16[2048,1024]{1,0:T(8,128)(2,1)} %get-tuple-element.15.act, bf16[1024,512]{1,0:T(8,128)(2,1)} %w_out.1, bf16[16,128,512]{2,1,0:T(8,128)(2,1)} %bitcast.38, bf16[64,512]{1,0:T(8,128)(2,1)} %copy-done.3, ...), custom_call_target="tpu_custom_call" | custom-call | flops 7516192768 | bytes 23068672 | tf_op jit(solution)/shard_map/tail/pallas_call | solution.py:362
  108.1 0.9 sum_blocks.1
  (33 shorter events, 0.1 us)
Async XLA Ops:
  0.6 17.0 %copy-start.1 = (bf16[1024,512]{1,0:T(8,128)(2,1)S(1)}, bf16[1024,512]{1,0:T(8,128)(2,1)}, u32[]{:S(2)}) copy-start(bf16[1024,512]{1,0:T(8,128)(2,1)} %w_out.1) | copy-start | bytes 3145732
  1.6 11.3 %collective-permute-start.1 = (bf16[64,512]{1,0:T(8,128)(2,1)S(1)}, bf16[64,512]{1,0:T(8,128)(2,1)S(1)}, u32[]{:S(2)}, u32[]{:S(2)}) collective-permute-start(bf16[64,512]{1,0:T(8,128)(2,1)S(1)} %get-tuple-element.36), channel_id=1, source_target_pairs={{16,0},{32,16},{48,32},{64,48},{80,64},{96,80},{112,96},{17,1},{33... | collective-permute-start | bytes 196616 | tf_op jit(solution)/shard_map/ppermute | solution.py:420
  2.9 10.0 %collective-permute-start = (bf16[64,512]{1,0:T(8,128)(2,1)S(1)}, bf16[64,512]{1,0:T(8,128)(2,1)S(1)}, u32[]{:S(2)}, u32[]{:S(2)}) collective-permute-start(bf16[64,512]{1,0:T(8,128)(2,1)S(1)} %get-tuple-element.37), channel_id=1, source_target_pairs={{0,16},{16,32},{32,48},{48,64},{64,80},{80,96},{96,112},{1,17},{17... | collective-permute-start | bytes 196616 | tf_op jit(solution)/shard_map/ppermute | solution.py:419
  13.1 8.4 %collective-permute-start.3 = (bf16[80,512]{1,0:T(8,128)(2,1)S(1)}, bf16[80,512]{1,0:T(8,128)(2,1)S(1)}, u32[]{:S(2)}, u32[]{:S(2)}) collective-permute-start(bf16[80,512]{1,0:T(8,128)(2,1)S(1)} %concatenate.7), channel_id=1, source_target_pairs={{1,0},{2,1},{3,2},{4,3},{5,4},{6,5},{7,6},{8,7},{9,8},{10,9},{11,1... | collective-permute-start | bytes 245768 | tf_op jit(solution)/shard_map/ppermute | solution.py:420
  14.6 6.9 %collective-permute-start.2 = (bf16[80,512]{1,0:T(8,128)(2,1)S(1)}, bf16[80,512]{1,0:T(8,128)(2,1)S(1)}, u32[]{:S(2)}, u32[]{:S(2)}) collective-permute-start(bf16[80,512]{1,0:T(8,128)(2,1)S(1)} %concatenate.6), channel_id=1, source_target_pairs={{0,1},{1,2},{2,3},{3,4},{4,5},{5,6},{6,7},{7,8},{8,9},{9,10},{10,1... | collective-permute-start | bytes 245768 | tf_op jit(solution)/shard_map/ppermute | solution.py:419
  17.6 3.9 %copy-start = (bf16[8,64,512]{2,1,0:T(8,128)(2,1)S(1)}, bf16[8,64,512]{2,1,0:T(8,128)(2,1)}, u32[]{:S(2)}) copy-start(bf16[8,64,512]{2,1,0:T(8,128)(2,1)} %lat.1) | copy-start | bytes 1572868
  51.1 10.8 %copy-start.2 = (bf16[2048,512]{1,0:T(8,128)(2,1)}, bf16[2048,512]{1,0:T(8,128)(2,1)S(1)}, u32[]{:S(2)}) copy-start(bf16[2048,512]{1,0:T(8,128)(2,1)S(1)} %get-tuple-element.16) | copy-start | bytes 6291460
  51.1 10.8 %copy-start.3 = (bf16[64,512]{1,0:T(8,128)(2,1)}, bf16[64,512]{1,0:T(8,128)(2,1)S(1)}, u32[]{:S(2)}) copy-start(bf16[64,512]{1,0:T(8,128)(2,1)S(1)} %get-tuple-element.17.edge) | copy-start | bytes 196612
  51.2 9.2 %collective-permute-start.6 = (bf16[4,4,4,96,128]{4,3,2,1,0:T(8,128)(2,1)S(1)}, bf16[4,4,4,96,128]{4,3,2,1,0:T(8,128)(2,1)S(1)}, u32[]{:S(2)}, u32[]{:S(2)}) collective-permute-start(bf16[4,4,4,96,128]{4,3,2,1,0:T(8,128)(2,1)S(1)} %get-tuple-element.23), channel_id=1, source_target_pairs={{0,1},{1,0},{2,3},{3,2},{4,5},{5,4},{6,7},{7,6},{8,9},{9,8},{10,11... | collective-permute-start | bytes 4718600 | tf_op jit(solution)/shard_map/ppermute | solution.py:454
  61.9 46.1 %all-to-all-start = ((bf16[64,96,128]{2,1,0:T(8,128)(2,1)}), bf16[64,96,128]{2,1,0:T(8,128)(2,1)S(1)}, u32[]{:S(2)}, u32[]{:S(2)}) async-start(bf16[64,96,128]{2,1,0:T(8,128)(2,1)} %bitcast.39), calls=%async_computation | async-start | bytes 3145728 | tf_op jit(solution)/shard_map/all_to_all | solution.py:473
  69.4 23.5 %collective-permute-start.4 = (bf16[160,512]{1,0:T(8,128)(2,1)S(1)}, bf16[160,512]{1,0:T(8,128)(2,1)S(1)}, u32[]{:S(2)}, u32[]{:S(2)}) collective-permute-start(bf16[160,512]{1,0:T(8,128)(2,1)S(1)} %get-tuple-element.18), channel_id=1, source_target_pairs={{0,16},{16,32},{32,48},{48,64},{64,80},{80,96},{96,112},{1,17},{17... | collective-permute-start | bytes 491528 | tf_op jit(solution)/shard_map/ppermute | solution.py:419
  72.3 20.6 %collective-permute-start.5 = (bf16[160,512]{1,0:T(8,128)(2,1)S(1)}, bf16[160,512]{1,0:T(8,128)(2,1)S(1)}, u32[]{:S(2)}, u32[]{:S(2)}) collective-permute-start(bf16[160,512]{1,0:T(8,128)(2,1)S(1)} %get-tuple-element.19), channel_id=1, source_target_pairs={{16,0},{32,16},{48,32},{64,48},{80,64},{96,80},{112,96},{17,1},{33... | collective-permute-start | bytes 491528 | tf_op jit(solution)/shard_map/ppermute | solution.py:420
  92.9 0.7 copy-start.4
  92.9 0.8 copy-start.5
